TPU v7x, 512 devices: a whole 4x8x8 slice. The times are simulated.
512 devices in a mesh: row: 32 (over z, x), col: 16 (over y, core).
Axes of the slice: x: 4, y: 8, z: 8, core: 2. Of those that a mesh axis runs over, the one named last changes fastest.
Arguments:
- tiles: bfloat16 [32, 16, 32, 128, 128], P('row', 'col'), may hold values from -0.375 to 0.375
- coords: int32 [32, 16, 32, 2], P('row', 'col'), may hold values from 0 to 2047, as said below
- counts: int32 [32, 16], P('row', 'col'), may hold values from 16 to 32, as said below
- rhs: float32 [2, 4194304], P(None, ('row', 'col')), may hold values from -50 to 50
Outputs:
- solution: float32 [2, 4194304], P(None, ('col', 'row'))
- phi_bar: float32 [2], replicated
Inputs may be any that keep to these rules, and one draw needn't show every extreme that they name: coords[p, q, k, 0] is a local block row below 1024 and coords[p, q, k, 1] a local block column below 2048; within one tile no two slots share a block row and no two share a block column; counting all 32 slots of a tile, exactly 2 of its block rows fall in each of the 16 ranges of 64 consecutive block rows, and exactly 1 of its block columns in each of the 32 ranges of 64 consecutive block columns. The first counts[p, q] slots of tile (p, q) are used; some tile uses all 32.
All inputs are finite; a program needn't handle non-finite values.
Results may differ from a plain program's by a relative error of at most 0.015.
Values may be sent and summed in bfloat16 or wider, within the bound.
No kernel may reach another device: no remote copies, remote signals or barrier semaphores. Data moves between devices by JAX's collectives and lax.ppermute only.
A program may use at most 192 MiB of HBM per device.

v0:
```python
import jax
import jax.numpy as jnp
from jax import lax
from jax.sharding import PartitionSpec as P

ITERS = 2


EPS = 1e-06


def rounded(values):
    return lax.optimization_barrier(values.astype(jnp.bfloat16))


def select_blocks(piece, block_ids, block):
    width = piece.shape[1]
    offsets = block_ids[:, None] * block + jnp.arange(block, dtype=jnp.int32)[None, :]
    inside = (offsets >= 0) & (offsets < width)
    clipped = jnp.clip(offsets, 0, width - 1)
    taken = jnp.take(piece, clipped.reshape(-1), axis=1).reshape(
        piece.shape[0], block_ids.shape[0], block
    )
    taken = jnp.where(inside[None, :, :], taken, jnp.zeros_like(taken))
    values = piece.astype(jnp.float32)
    return (taken, jnp.sum(values * values, axis=1))


def forward_products(picked, tile_data):
    return jnp.einsum("rkc,kdc->krd", picked, tile_data, preferred_element_type=jnp.float32)


def adjoint_products(picked, tile_data):
    return jnp.einsum("rkd,kdc->krc", picked, tile_data, preferred_element_type=jnp.float32)


def bucket_blocks(products, block_ids, valid, range_len, owners):
    slot_count = block_ids.shape[0]
    capacity = slot_count // owners
    values = rounded(products * valid[:, None, None])
    owner_ids = block_ids // range_len
    local_ids = block_ids % range_len
    slot_index = jnp.arange(slot_count, dtype=jnp.int32)
    live = valid > 0.5
    earlier = (
        (owner_ids[:, None] == owner_ids[None, :])
        & live[None, :]
        & (slot_index[None, :] < slot_index[:, None])
    )
    position = jnp.sum(earlier.astype(jnp.int32), axis=1)
    target = owner_ids * capacity + position
    onehot = (target[None, :] == jnp.arange(owners * capacity, dtype=jnp.int32)[:, None]) & live[
        None, :
    ]
    sent = jnp.einsum(
        "ek,krd->erd", onehot.astype(jnp.bfloat16), values, preferred_element_type=jnp.float32
    ).astype(jnp.bfloat16)
    sent = sent.reshape(owners, capacity, values.shape[1], values.shape[2])
    labels = jnp.sum(jnp.where(onehot, local_ids[None, :] + 1, 0), axis=1).reshape(owners, capacity)
    return (sent, labels)


def place_blocks(received, labels, range_len):
    flat = received.reshape(-1, received.shape[2], received.shape[3])
    flat_labels = labels.reshape(-1)
    placing = (
        flat_labels[None, :] == jnp.arange(1, range_len + 1, dtype=jnp.int32)[:, None]
    ).astype(jnp.bfloat16)
    summed = jnp.einsum("bk,krd->rbd", placing, flat, preferred_element_type=jnp.float32)
    return summed.reshape(flat.shape[1], range_len * flat.shape[2])


def on_device(tiles, coords, counts, rhs):
    tile_data = tiles[0, 0]
    row_ids = coords[0, 0, :, 0]
    col_ids = coords[0, 0, :, 1]
    slot_count = tile_data.shape[0]
    block = tile_data.shape[1]
    valid = (jnp.arange(slot_count, dtype=jnp.int32) < counts[0, 0]).astype(jnp.float32)
    realizations = rhs.shape[0]
    piece_len = rhs.shape[1]
    range_len = piece_len // block

    def fold_rows(piece):
        return select_blocks(piece, row_ids, block)

    def fold_cols(piece):
        return select_blocks(piece, col_ids, block)

    def gather_u(u_rounded):
        return fold_rows(lax.all_gather(u_rounded, "col", axis=1, tiled=True))

    def gather_v(v_rounded):
        return fold_cols(lax.all_gather(v_rounded, "row", axis=1, tiled=True))

    def own_norm(vector_bf):
        values = vector_bf.astype(jnp.float32)
        return jnp.sqrt(lax.psum(jnp.sum(values * values, axis=1), ("row", "col")) + EPS)

    def u_norm(u_rounded):
        return own_norm(u_rounded)

    def v_norm(v_piece):
        return own_norm(v_piece)

    def forward_sum(picked_v):
        products = forward_products(picked_v, tile_data)
        sent, labels = bucket_blocks(products, row_ids, valid, range_len, lax.axis_size("col"))
        received, got_labels = (
            lax.all_to_all(sent, "col", split_axis=0, concat_axis=0, tiled=True),
            lax.all_to_all(labels, "col", split_axis=0, concat_axis=0, tiled=True),
        )
        return place_blocks(received, got_labels, range_len)

    def adjoint(picked_u, beta_now, v_former):
        products = adjoint_products(picked_u, tile_data)
        sent, labels = bucket_blocks(products, col_ids, valid, range_len, lax.axis_size("row"))
        received, got_labels = (
            lax.all_to_all(sent, "row", split_axis=0, concat_axis=0, tiled=True),
            lax.all_to_all(labels, "row", split_axis=0, concat_axis=0, tiled=True),
        )
        summed = place_blocks(received, got_labels, range_len)
        v_rounded = rounded(summed / beta_now[:, None] - beta_now[:, None] * v_former)
        picked_v, squares = gather_v(v_rounded)
        return (v_rounded, v_rounded, picked_v, squares)

    u_rounded = rounded(rhs)
    picked_u, u_squares = gather_u(u_rounded)
    beta_now = u_norm(u_rounded)
    u_unit = u_rounded.astype(jnp.float32) / beta_now[:, None]
    v_store, v_piece, picked_v, v_squares = adjoint(picked_u, beta_now, jnp.zeros((), jnp.float32))
    alpha_now = v_norm(v_piece)
    v_unit = v_store.astype(jnp.float32) / alpha_now[:, None]
    direction = v_piece.astype(jnp.float32) / alpha_now[:, None]
    solution = jnp.zeros((realizations, piece_len), jnp.float32)
    phi_bar = beta_now
    rho_bar = alpha_now
    for step in range(ITERS):
        final_turn = step + 1 == ITERS
        summed = forward_sum(picked_v)
        u_rounded = rounded(summed / alpha_now[:, None] - alpha_now[:, None] * u_unit)
        if final_turn:
            beta_now = u_norm(u_rounded)
        else:
            picked_u, u_squares = gather_u(u_rounded)
            beta_now = u_norm(u_rounded)
        rho_value = jnp.sqrt(rho_bar * rho_bar + beta_now * beta_now)
        cosine = rho_bar / rho_value
        sine = beta_now / rho_value
        phi_value = cosine * phi_bar
        phi_bar = sine * phi_bar
        solution = solution + (phi_value / rho_value)[:, None] * direction
        u_unit = u_rounded.astype(jnp.float32) / beta_now[:, None]
        if not final_turn:
            v_store, v_piece, picked_v, v_squares = adjoint(picked_u, beta_now, v_unit)
            alpha_now = v_norm(v_piece)
            theta_value = sine * alpha_now
            rho_bar = -cosine * alpha_now
            v_unit = v_store.astype(jnp.float32) / alpha_now[:, None]
            piece_unit = v_piece.astype(jnp.float32) / alpha_now[:, None]
            direction = piece_unit - (theta_value / rho_value)[:, None] * direction
    return (solution, phi_bar)


def solution(mesh):
    return jax.shard_map(
        on_device,
        mesh=mesh,
        in_specs=(
            P("row", "col", None, None, None),
            P("row", "col", None, None),
            P("row", "col"),
            P(None, ("row", "col")),
        ),
        out_specs=(P(None, ("col", "row")), P()),
        check_vma=False,
    )
```

profile of v0, /device:TPU:1, one launch (start us, length us, event | category | flops | bytes accessed | tf_op | source)
XLA Modules:
  0.0 923.0 jit_solution(12879823360342886995)
XLA Ops:
  7.9 0.7 fusion.82
  8.6 0.8 bitcast_multiply_fusion.1
  9.4 0.7 and_select_fusion.1
  10.4 0.7 copy.71
  11.1 13.7 %all-to-all-start.1 = ((s32[32,1,1]{2,1,0:T(1,128)}), s32[32,1,1]{2,1,0:T(1,128)S(1)}, u32[]{:S(2)}, u32[]{:S(2)}) async-start(s32[32,1,1]{2,1,0:T(1,128)} %copy.71), calls=%async_computation.1 | async-start | bytes 32768 | tf_op jit(solution)/shard_map/all_to_all | solution.py:120
  25.0 0.9 convert_element_type.88
  25.9 19.8 %all_gather.12 = bf16[2,131072]{1,0:T(2,128)(2,1)S(1)} all-gather(bf16[2,8192]{1,0:T(2,128)(2,1)S(1)} %convert_element_type.88), channel_id=1, replica_groups=mesh['row'=32,'col'=16] {'col'}, dimensions={1}, use_global_device_ids=true | all-gather | bytes 557056 | tf_op jit(solution)/shard_map/all_gather | solution.py:91
  45.8 20.3 %copy.66 = bf16[2,131072]{0,1:T(8,128)(2,1)} copy(bf16[2,131072]{1,0:T(2,128)(2,1)S(1)} %all_gather.12) | data formatting | bytes 1048576 | tf_op jit(solution)/shard_map/all_gather | solution.py:91
  66.2 43.5 %gather_fusion = bf16[4096,2]{1,0:T(8,128)(2,1)S(1)} fusion(bf16[2,131072]{0,1:T(8,128)(2,1)} %copy.66, s32[4096]{0:T(1024)S(1)} %fusion.37), kind=kCustom, calls=%fused_computation.clone | custom fusion | bytes 49152 | tf_op jit(solution)/shard_map/jit(_take)/gather | solution.py:21
  109.7 2.1 broadcast_select_fusion.3
  112.7 97.4 %psum.35 = f32[2]{0:T(128)S(1)} all-reduce(f32[2]{0:T(128)S(1)} %fusion.13), channel_id=1, replica_groups=mesh['row'=32,'col'=16] {'row','col'}, use_global_device_ids=true, to_apply=%region_3.5 | all-reduce | flops 2 | bytes 16 | tf_op jit(solution)/shard_map/psum | solution.py:98
  210.2 0.6 copy.69
  210.9 5.5 all-to-all-start
  216.4 0.7 reduce
  217.1 7.8 all-to-all-done
  225.1 0.7 fusion.18
  225.9 0.7 all_to_all.30
  226.6 6.3 all-to-all-start.3
  233.0 6.9 all-to-all-done.3
  240.4 0.7 reduce.4
  241.1 0.9 fusion.14
  242.1 94.6 %psum.36 = f32[2]{0:T(128)S(1)} all-reduce(f32[2]{0:T(128)S(1)} %fusion.14), channel_id=1, replica_groups=mesh['row'=32,'col'=16] {'row','col'}, use_global_device_ids=true, to_apply=%region_5.7 | all-reduce | flops 2 | bytes 16 | tf_op jit(solution)/shard_map/psum | solution.py:98
  336.7 40.2 %copy.72 = bf16[2,262144]{0,1:T(8,128)(2,1)} copy(bf16[2,262144]{1,0:T(2,128)(2,1)} %all-gather.3.cloned.1.call-done) | data formatting | bytes 2097152 | tf_op jit(solution)/shard_map/all_gather | solution.py:94
  376.9 43.7 %gather_fusion.1 = bf16[4096,2]{1,0:T(8,128)(2,1)S(1)} fusion(bf16[2,262144]{0,1:T(8,128)(2,1)} %copy.72, s32[4096]{0:T(1024)S(1)} %fusion.32), kind=kCustom, calls=%fused_computation.1.clone | custom fusion | bytes 49152 | tf_op jit(solution)/shard_map/jit(_take)/gather | solution.py:21
  420.6 2.1 broadcast_select_fusion.1
  423.1 0.7 fusion.1
  423.9 0.6 copy.75
  424.5 4.1 all-to-all-start.2
  428.6 7.3 all-to-all-done.2
  436.3 16.5 %all_gather.14 = bf16[2,131072]{1,0:T(2,128)(2,1)S(1)} all-gather(bf16[2,8192]{1,0:T(2,128)(2,1)S(1)} %fusion.19), channel_id=1, replica_groups=mesh['row'=32,'col'=16] {'col'}, dimensions={1}, use_global_device_ids=true | all-gather | bytes 557056 | tf_op jit(solution)/shard_map/all_gather | solution.py:91
  453.0 20.3 %copy.78 = bf16[2,131072]{0,1:T(8,128)(2,1)} copy(bf16[2,131072]{1,0:T(2,128)(2,1)S(1)} %all_gather.14) | data formatting | bytes 1048576 | tf_op jit(solution)/shard_map/all_gather | solution.py:91
  473.3 43.5 %gather_fusion.2 = bf16[4096,2]{1,0:T(8,128)(2,1)S(1)} fusion(bf16[2,131072]{0,1:T(8,128)(2,1)} %copy.78, s32[4096]{0:T(1024)S(1)} %fusion.37), kind=kCustom, calls=%fused_computation.2.clone | custom fusion | bytes 49152 | tf_op jit(solution)/shard_map/jit(_take)/gather | solution.py:21
  516.9 2.1 broadcast_select_fusion.2
  519.9 0.6 copy.81
  520.5 5.2 all-to-all-start.4
  525.8 97.0 %psum.37 = f32[2]{0:T(128)S(1)} all-reduce(f32[2]{0:T(128)S(1)} %fusion.15), channel_id=1, replica_groups=mesh['row'=32,'col'=16] {'row','col'}, use_global_device_ids=true, to_apply=%region_9.12 | all-reduce | flops 2 | bytes 16 | tf_op jit(solution)/shard_map/psum | solution.py:98
  623.1 0.7 fusion.21
  623.9 1.0 fusion.16
  624.8 94.5 %psum.38 = f32[2]{0:T(128)S(1)} all-reduce(f32[2]{0:T(128)S(1)} %fusion.16), channel_id=1, replica_groups=mesh['row'=32,'col'=16] {'row','col'}, use_global_device_ids=true, to_apply=%region_11.14 | all-reduce | flops 2 | bytes 16 | tf_op jit(solution)/shard_map/psum | solution.py:98
  719.3 40.2 %copy.83 = bf16[2,262144]{0,1:T(8,128)(2,1)} copy(bf16[2,262144]{1,0:T(2,128)(2,1)} %all-gather.5.cloned.1.call-done) | data formatting | bytes 2097152 | tf_op jit(solution)/shard_map/all_gather | solution.py:94
  759.5 43.7 %gather_fusion.3 = bf16[4096,2]{1,0:T(8,128)(2,1)S(1)} fusion(bf16[2,262144]{0,1:T(8,128)(2,1)} %copy.83, s32[4096]{0:T(1024)S(1)} %fusion.32), kind=kCustom, calls=%fused_computation.3.clone | custom fusion | bytes 49152 | tf_op jit(solution)/shard_map/jit(_take)/gather | solution.py:21
  803.2 2.1 broadcast_select_fusion
  805.7 0.7 fusion.3
  806.5 0.6 copy.86
  807.1 4.8 all-to-all-start.5
  811.9 7.3 all-to-all-done.5
  819.9 94.9 %psum.39 = f32[2]{0:T(128)S(1)} all-reduce(f32[2]{0:T(128)S(1)} %multiply_reduce_fusion), channel_id=1, replica_groups=mesh['row'=32,'col'=16] {'row','col'}, use_global_device_ids=true, to_apply=%region_13.16 | all-reduce | flops 2 | bytes 16 | tf_op jit(solution)/shard_map/psum | solution.py:98
  915.4 0.8 multiply_add_fusion
  (54 shorter events, 6.8 us)
Async XLA Ops:
  7.2 105.2 %copy-start = (bf16[1,1,32,128,128]{4,3,2,1,0:T(8,128)(2,1)S(1)}, bf16[1,1,32,128,128]{4,3,2,1,0:T(8,128)(2,1)}, u32[]{:S(2)}) copy-start(bf16[1,1,32,128,128]{4,3,2,1,0:T(8,128)(2,1)} %param.8) | copy-start | bytes 3145732
  11.1 199.8 %all-to-all-start.1 = ((s32[32,1,1]{2,1,0:T(1,128)}), s32[32,1,1]{2,1,0:T(1,128)S(1)}, u32[]{:S(2)}, u32[]{:S(2)}) async-start(s32[32,1,1]{2,1,0:T(1,128)} %copy.71), calls=%async_computation.1 | async-start | bytes 32768 | tf_op jit(solution)/shard_map/all_to_all | solution.py:120
  210.9 14.0 %all-to-all-start = ((bf16[32,1,2,128]{3,2,1,0:T(2,128)(2,1)}), bf16[32,1,2,128]{3,2,1,0:T(2,128)(2,1)S(1)}, u32[]{:S(2)}, u32[]{:S(2)}) async-start(bf16[32,1,2,128]{3,2,1,0:T(2,128)(2,1)} %copy.69), calls=%async_computation | async-start | bytes 32768 | tf_op jit(solution)/shard_map/all_to_all | solution.py:119
  216.4 120.4 %all-gather.3.cloned.1.call-start = ((), (), s32[]{:S(2)}) async-start(), calls=%async_computation.6 | async-start | bytes 1081344 | tf_op jit(solution)/shard_map/all_gather | solution.py:94
  225.9 397.2 %copy-start.1 = (bf16[2,8192]{1,0:T(2,128)(2,1)S(1)}, bf16[2,8192]{1,0:T(2,128)(2,1)}, u32[]{:S(2)}) copy-start(bf16[2,8192]{1,0:T(2,128)(2,1)} %fusion.18) | copy-start | bytes 98308
  226.6 13.3 %all-to-all-start.3 = ((s32[16,1,2]{2,1,0:T(1,128)}), s32[16,1,2]{2,1,0:T(1,128)S(1)}, u32[]{:S(2)}, u32[]{:S(2)}) async-start(s32[16,1,2]{2,1,0:T(1,128)} %bitcast.19), calls=%async_computation.3 | async-start | bytes 16384 | tf_op jit(solution)/shard_map/all_to_all | solution.py:111
  424.5 11.4 %all-to-all-start.2 = ((bf16[16,2,2,128]{3,1,2,0:T(2,128)(2,1)}), bf16[16,2,2,128]{3,1,2,0:T(2,128)(2,1)S(1)}, u32[]{:S(2)}, u32[]{:S(2)}) async-start(bf16[16,2,2,128]{3,1,2,0:T(2,128)(2,1)} %copy.75), calls=%async_computation.2 | async-start | bytes 32768 | tf_op jit(solution)/shard_map/all_to_all | solution.py:110
  520.5 102.3 %all-to-all-start.4 = ((bf16[32,1,2,128]{3,2,1,0:T(2,128)(2,1)}), bf16[32,1,2,128]{3,2,1,0:T(2,128)(2,1)S(1)}, u32[]{:S(2)}, u32[]{:S(2)}) async-start(bf16[32,1,2,128]{3,2,1,0:T(2,128)(2,1)} %copy.81), calls=%async_computation.4 | async-start | bytes 32768 | tf_op jit(solution)/shard_map/all_to_all | solution.py:119
  525.7 193.6 %all-gather.5.cloned.1.call-start = ((), (), s32[]{:S(2)}) async-start(), calls=%async_computation.7 | async-start | bytes 1081344 | tf_op jit(solution)/shard_map/all_gather | solution.py:94
  623.8 291.6 %copy-start.2 = (bf16[2,8192]{1,0:T(2,128)(2,1)S(1)}, bf16[2,8192]{1,0:T(2,128)(2,1)}, u32[]{:S(2)}) copy-start(bf16[2,8192]{1,0:T(2,128)(2,1)} %get-tuple-element.20) | copy-start | bytes 98308
  807.1 12.1 %all-to-all-start.5 = ((bf16[16,2,2,128]{3,1,2,0:T(2,128)(2,1)}), bf16[16,2,2,128]{3,1,2,0:T(2,128)(2,1)S(1)}, u32[]{:S(2)}, u32[]{:S(2)}) async-start(bf16[16,2,2,128]{3,1,2,0:T(2,128)(2,1)} %copy.86), calls=%async_computation.5 | async-start | bytes 32768 | tf_op jit(solution)/shard_map/all_to_all | solution.py:110
Sparse Core Ops, SparseCore 0:
  226.0 71.3 all-gather.2
  624.0 71.4 all-gather.4
where the time goes:
time: 929 us; the launch traced here: 923 us
  blocking collectives  515 us (55%)
  local copies, waits for them, and re-layouts  301 us (32%)
  starting transfers between devices  39.6 us (4%)
  waiting for transfers between devices  29.3 us (3%)
  other arithmetic  19.2 us (2%)
  between operations  15 us (2%)
    psum x5, blocking collectives, own_norm(): lax.psum(jnp.sum(values * values, axis=1), ('row', 'col')) + EPS  478 us
    gather x4, local copies, waits for them, and re-layouts, select_blocks(): jnp.take(piece, clipped.reshape(-1), axis=1)  174 us
    all_gather x2, local copies, waits for them, and re-layouts, gather_v(): return fold_cols(lax.all_gather(v_rounded, 'row', axis=1, tiled=True))  80.3 us
    all_gather x2, local copies, waits for them, and re-layouts, gather_u(): return fold_rows(lax.all_gather(u_rounded, 'col', axis=1, tiled=True))  40.6 us
    all_gather x2, blocking collectives, gather_u(): return fold_rows(lax.all_gather(u_rounded, 'col', axis=1, tiled=True))  36.3 us
  transfers between devices with their start and end apart: 8, of which 4 were waited for; matrix products, arithmetic and copies ran while one was open for 8% of the time, Pallas kernels for 0%

commit v1 on v0

v1 whole, which is shorter than its diff:
```python
import functools

import jax
import jax.numpy as jnp
from jax import lax
from jax.experimental import pallas as pl
from jax.experimental.pallas import tpu as pltpu
from jax.sharding import PartitionSpec as P

EPS = 1e-06
F32 = jnp.float32
BF16 = jnp.bfloat16
VMEM = pl.BlockSpec(memory_space=pltpu.VMEM)
SMEM = pl.BlockSpec(memory_space=pltpu.SMEM)


def iota(shape, dim):
    return lax.broadcasted_iota(jnp.int32, shape, dim)


def fill_row_keys(keys_ref, coords_ref, count, axis):
    parity = iota((2, 128), 0)
    for k in range(coords_ref.shape[0]):
        base = jnp.where(k < count, coords_ref[k, axis] * 2, -8)
        keys_ref[2 * k : 2 * k + 2, :] = (base + parity).astype(F32)


def lane_keys(coords_ref, count, axis):
    lane = iota((8, 128), 1)
    slot = (lane % 64) // 2
    keys = jnp.full((8, 128), -2, jnp.int32)
    for k in range(coords_ref.shape[0]):
        base = jnp.where(k < count, coords_ref[k, axis] * 2, -2)
        keys = jnp.where(slot == k, base, keys)
    keys = (keys + lane % 2).astype(F32)
    high = jnp.floor(keys * (1.0 / 64.0))
    low = keys - 64.0 * high
    sub = iota((8, 128), 0)
    return jnp.where(sub == 0, high, jnp.where(sub == 1, low, 0.0)).astype(BF16)


def read_lane_keys(received_ref, map_ref, rows):
    first = iota((8, 128), 1) < 64
    for g in range(received_ref.shape[0] // 2):
        even = received_ref[2 * g, rows : rows + 8, :].astype(F32)
        odd = received_ref[2 * g + 1, rows : rows + 8, :].astype(F32)
        both = jnp.where(first, even, odd)
        map_ref[g : g + 1, :] = both[0:1, :] * 64.0 + both[1:2, :]


def own_sum(received_ref, map_ref, keys_ref, rows):
    keys = keys_ref[...]
    total = jnp.zeros(keys.shape, F32)
    for g in range(received_ref.shape[0] // 2):
        match = (keys == map_ref[g : g + 1, :]).astype(F32).astype(BF16)
        both = jnp.concatenate([received_ref[2 * g, 0:rows, :], received_ref[2 * g + 1, 0:rows, :]], axis=0)
        total = total + jnp.dot(match, both, preferred_element_type=F32)
    return total


def leaders(map_ref, keys_ref, me, groups):
    keys = keys_ref[...]
    half = iota(keys.shape, 1) // 64
    earlier = jnp.zeros(keys.shape, F32)
    for g in range(groups):
        hit = (keys == map_ref[g : g + 1, :]) & (2 * g + half < me)
        earlier = earlier + hit.astype(F32)
    count = jnp.sum(earlier, axis=1, keepdims=True)
    return ((count == 0.0) & (keys >= 0.0)).astype(F32)


def products(held_ref, tile_ref, out_ref, adjoint):
    for k in range(tile_ref.shape[0]):
        rows = held_ref[2 * k : 2 * k + 2, :].astype(BF16)
        dims = (((1,), (0 if adjoint else 1,)), ((), ()))
        out_ref[2 * k : 2 * k + 2, :] = lax.dot_general(rows, tile_ref[k], dims, preferred_element_type=F32)


def send_all(sent_ref, values, extra):
    rows = values.shape[0]
    for peer in range(sent_ref.shape[0]):
        sent_ref[peer, 0:rows, :] = values
        if extra is not None:
            sent_ref[peer, rows : rows + 8, :] = extra


def first_adjoint(coords_ref, counts_ref, u_ref, tile_ref, sent_ref, own_u_ref, wide, held, out):
    wide[...] = u_ref[...].astype(F32)
    count = counts_ref[0, 0]
    for k in range(coords_ref.shape[0]):
        used = (k < count).astype(F32)
        row = pl.multiple_of(coords_ref[k, 0] * 2, 2)
        held[2 * k : 2 * k + 2, :] = wide[pl.ds(row, 2), :] * used
    own_u_ref[...] = held[...].astype(BF16)
    products(held, tile_ref, out, True)
    send_all(sent_ref, out[...].astype(BF16), lane_keys(coords_ref, count, 1))


def first_forward(coords_ref, counts_ref, got_ref, tile_ref, sent_ref, w_ref, map_ref, keys, held, out):
    count = counts_ref[0, 0]
    rows = keys.shape[0]
    fill_row_keys(keys, coords_ref, count, 1)
    read_lane_keys(got_ref, map_ref, rows)
    w = own_sum(got_ref, map_ref, keys, rows).astype(BF16)
    w_ref[...] = w
    held[...] = w.astype(F32)
    products(held, tile_ref, out, False)
    send_all(sent_ref, out[...].astype(BF16), lane_keys(coords_ref, count, 0))


def second_adjoint(coords_ref, counts_ref, got_ref, tile_ref, sent_ref, w_ref, map_ref, keys, held, out):
    rows = keys.shape[0]
    fill_row_keys(keys, coords_ref, counts_ref[0, 0], 0)
    read_lane_keys(got_ref, map_ref, rows)
    w = own_sum(got_ref, map_ref, keys, rows).astype(BF16)
    w_ref[...] = w
    held[...] = w.astype(F32)
    products(held, tile_ref, out, True)
    send_all(sent_ref, out[...].astype(BF16), None)


def by_parity(values):
    folded = jnp.sum(values.reshape(values.shape[0] // 8, 8, 128), axis=0)
    return jnp.sum(folded, axis=1, keepdims=True)


def digits(sums):
    lane = iota((8, 128), 1)
    block = jnp.zeros((8, 128), F32)
    for j, value in enumerate(sums):
        value = jnp.broadcast_to(value, (8, 128))
        high = value.astype(BF16).astype(F32)
        middle = (value - high).astype(BF16).astype(F32)
        low = (value - high - middle).astype(BF16).astype(F32)
        block = jnp.where(lane == j, high, block)
        block = jnp.where(lane == 16 + j, middle, block)
        block = jnp.where(lane == 32 + j, low, block)
    return block


def undigits(block):
    return block + pltpu.roll(block, 112, 1) + pltpu.roll(block, 96, 1)


def second_forward(
    coords_ref, counts_ref, got_ref, tile_ref, v_map_ref, u_map_ref, w1_ref, w2_ref, own_u_ref, piece_ref,
    sent_ref, w3_ref, lead_ref, keys, held, out,
):
    count = counts_ref[0, 0]
    rows = keys.shape[0]
    fill_row_keys(keys, coords_ref, count, 1)
    w3 = own_sum(got_ref, v_map_ref, keys, rows).astype(BF16)
    w3_ref[...] = w3
    held[...] = w3.astype(F32)
    products(held, tile_ref, out, False)
    sent = out[...].astype(BF16)
    lead_v = leaders(v_map_ref, keys, lax.axis_index("row"), got_ref.shape[0] // 2)
    lead_ref[...] = jnp.broadcast_to(lead_v, lead_ref.shape)
    fill_row_keys(keys, coords_ref, count, 0)
    lead_u = leaders(u_map_ref, keys, lax.axis_index("col"), sent_ref.shape[0] // 2)
    w3 = w3.astype(F32)
    w1 = w1_ref[...].astype(F32)
    w2 = w2_ref[...].astype(F32)
    u0 = own_u_ref[...].astype(F32)
    piece = piece_ref[...].astype(F32)
    c4 = sent.astype(F32)
    sums = [
        by_parity(w1 * w1 * lead_v),
        by_parity(w1 * w3 * lead_v),
        by_parity(w3 * w3 * lead_v),
        by_parity(piece * piece),
        by_parity(u0 * w2 * lead_u),
        by_parity(w2 * w2 * lead_u),
        by_parity(c4 * w2),
        by_parity(c4 * u0),
    ]
    send_all(sent_ref, sent, digits(sums).astype(BF16))


def gather_sums(coords_ref, got_ref, u_map_ref, w1_ref, w3_ref, lead_ref, sent_ref, values, square, held1, held3):
    peers = got_ref.shape[0]
    rows = got_ref.shape[1] - 8
    partial = jnp.zeros((8, 128), F32)
    for peer in range(peers):
        partial = partial + got_ref[peer, rows : rows + 8, :].astype(F32)
        values[peer * rows : (peer + 1) * rows, :] = got_ref[peer, 0:rows, :]
    for g in range(peers // 2):
        column = jnp.transpose(jnp.broadcast_to(u_map_ref[g : g + 1, :], (128, 128)))
        total = jnp.zeros((128, 128), F32)
        for h in range(peers // 2):
            match = (column == u_map_ref[h : h + 1, :]).astype(F32).astype(BF16)
            total = total + jnp.dot(match, values[128 * h : 128 * h + 128, :], preferred_element_type=F32)
        own = values[128 * g : 128 * g + 128, :].astype(F32) * total
        folded = jnp.sum(own.reshape(16, 8, 128), axis=0)
        square[...] = folded if g == 0 else square[...] + folded
    last = digits([jnp.zeros((8, 1), F32)] * 8 + [jnp.sum(square[...], axis=1, keepdims=True)])
    block = partial + last
    block = block + pltpu.roll(block, 2, 0)
    block = block + pltpu.roll(block, 4, 0)
    block = digits_again(block)
    held1[...] = w1_ref[...].astype(F32) * lead_ref[...]
    held3[...] = w3_ref[...].astype(F32) * lead_ref[...]
    me = lax.axis_index("row")
    sub = iota((8, 128), 0)
    lane = iota((8, 128), 1)
    label_here = (lane // 8 + 16 * (sub - 6) == me) & (sub >= 6)
    sums = jnp.where((sub == 4) | (sub == 5), block, 0.0)
    for k in range(coords_ref.shape[0]):
        column = coords_ref[k, 1]
        owner = column // 64
        first = held1[2 * k : 2 * k + 2, :]
        second = held3[2 * k : 2 * k + 2, :]
        lead = lead_ref[2 * k : 2 * k + 1, :]
        label = (column % 64 + 1).astype(F32) * jnp.broadcast_to(lead, (8, 128))
        whole = jnp.concatenate([first, second, jnp.zeros((4, 128), F32)], axis=0)
        whole = whole + sums + jnp.where(label_here, label, 0.0)
        sent_ref[owner] = whole.astype(BF16)


def digits_again(block):
    total = undigits(block)
    lane = iota((8, 128), 1)
    total = jnp.where(lane < 16, total, 0.0)
    high = total.astype(BF16).astype(F32)
    middle = (total - high).astype(BF16).astype(F32)
    low = (total - high - middle).astype(BF16).astype(F32)
    return high + pltpu.roll(middle, 16, 1) + pltpu.roll(low, 32, 1)


def finish(got_ref, solution_ref, phi_ref, wide):
    peers = got_ref.shape[0]
    wide[...] = got_ref[...].astype(F32)
    total = jnp.sum(wide[...], axis=0)
    sub = iota((8, 128), 0)
    sums = jnp.where(sub % 2 == 0, jnp.broadcast_to(total[4:5, :], (8, 128)), jnp.broadcast_to(total[5:6, :], (8, 128)))
    sums = undigits(sums)

    def pick(j):
        return jnp.broadcast_to(sums[:, j : j + 1], (8, 128))

    t11, t13, t33, s00, s02, s22, s24, s04, s44 = [pick(j) for j in range(9)]

    def norm(square):
        return jnp.sqrt(jnp.maximum(square, 0.0) + EPS)

    beta0 = norm(s00)
    alpha1 = norm(t11 / (beta0 * beta0))
    x2 = 1.0 / (beta0 * alpha1)
    x0 = -alpha1 / beta0
    beta1 = norm(x2 * x2 * s22 + 2.0 * x2 * x0 * s02 + x0 * x0 * s00)
    y3 = x2 / beta1
    y1 = x0 / beta1 - beta1 * x2
    alpha2 = norm(y3 * y3 * t33 + 2.0 * y3 * y1 * t13 + y1 * y1 * t11)
    ratio = alpha2 / beta1
    z4 = y3 / alpha2
    z2 = y1 / alpha2 - ratio * x2
    z0 = -ratio * x0
    beta2 = norm(
        z4 * z4 * s44 + z2 * z2 * s22 + z0 * z0 * s00 + 2.0 * (z4 * z2 * s24 + z4 * z0 * s04 + z2 * z0 * s02)
    )
    rho1 = jnp.sqrt(alpha1 * alpha1 + beta1 * beta1)
    cosine1 = alpha1 / rho1
    sine1 = beta1 / rho1
    phi1 = cosine1 * beta0
    phi_bar1 = sine1 * beta0
    theta = sine1 * alpha2
    rho_bar2 = -cosine1 * alpha2
    rho2 = jnp.sqrt(rho_bar2 * rho_bar2 + beta2 * beta2)
    cosine2 = rho_bar2 / rho2
    sine2 = beta2 / rho2
    phi2 = cosine2 * phi_bar1
    phi_ref[...] = sine2 * phi_bar1
    share1 = phi1 / rho1
    share2 = phi2 / rho2
    k1 = share1 * x2 + share2 * (y1 / alpha2 - (theta / rho1) * x2)
    k3 = share2 * y3 / alpha2

    out_rows = solution_ref.shape[0]
    place1 = jnp.zeros((out_rows, 128), F32)
    place3 = jnp.zeros((out_rows, 128), F32)
    row = iota((out_rows, 128), 0)
    slot = iota((out_rows, 128), 1) % 8
    for h in range(peers // 16):
        labels = jnp.broadcast_to(total[6 + h : 7 + h, :], (out_rows, 128)).astype(jnp.int32) - 1
        values = wide[16 * h : 16 * h + 16].reshape(128, 128).astype(BF16)
        hit1 = (labels * 2 + slot == row) & (slot < 2) & (labels >= 0)
        hit3 = (labels * 2 + slot - 2 == row) & (slot >= 2) & (slot < 4) & (labels >= 0)
        place1 = place1 + jnp.dot(hit1.astype(F32).astype(BF16), values, preferred_element_type=F32)
        place3 = place3 + jnp.dot(hit3.astype(F32).astype(BF16), values, preferred_element_type=F32)
    shape = (out_rows // 8, 8, 128)
    result = place1.reshape(shape) * k1[None] + place3.reshape(shape) * k3[None]
    solution_ref[...] = result.reshape(out_rows, 128)


def struct(shape, dtype):
    return jax.ShapeDtypeStruct(shape, dtype)


def on_device(tiles, coords, counts, rhs):
    n_row = lax.axis_size("row")
    n_col = lax.axis_size("col")
    tile = tiles[0, 0]
    places = coords[0, 0]
    slots = tile.shape[0]
    rows = 2 * slots
    piece_rows = rhs.shape[1] // 128 * 2

    def call(body, outs, scratch, specs):
        return pl.pallas_call(
            body,
            out_shape=outs,
            in_specs=specs,
            out_specs=[VMEM] * len(outs),
            scratch_shapes=[pltpu.VMEM(shape, dtype) for shape, dtype in scratch],
            compiler_params=pltpu.CompilerParams(vmem_limit_bytes=32 * 1024 * 1024),
        )

    def exchange(sent, axis):
        return lax.all_to_all(sent, axis, split_axis=0, concat_axis=0, tiled=True)

    work = [((rows, 128), F32)] * 3
    two = [SMEM, SMEM]
    piece = rhs.reshape(2, piece_rows // 2, 128).transpose(1, 0, 2).reshape(piece_rows, 128).astype(BF16)
    u_group = lax.all_gather(piece, "col", axis=0, tiled=True)
    sent, own_u = call(
        first_adjoint,
        [struct((n_row, rows + 8, 128), BF16), struct((rows, 128), BF16)],
        [((n_col * piece_rows, 128), F32)] + work[:2],
        two + [VMEM] * 2,
    )(places, counts, u_group, tile)
    got = exchange(sent, "row")
    sent, w1, v_map = call(
        first_forward,
        [struct((n_col, rows + 8, 128), BF16), struct((rows, 128), BF16), struct((n_row // 2, 128), F32)],
        work,
        two + [VMEM] * 2,
    )(places, counts, got, tile)
    got = exchange(sent, "col")
    sent, w2, u_map = call(
        second_adjoint,
        [struct((n_row, rows, 128), BF16), struct((rows, 128), BF16), struct((n_col // 2, 128), F32)],
        work,
        two + [VMEM] * 2,
    )(places, counts, got, tile)
    got = exchange(sent, "row")
    sent, w3, lead = call(
        second_forward,
        [struct((n_col, rows + 8, 128), BF16), struct((rows, 128), BF16), struct((rows, 128), F32)],
        work,
        two + [VMEM] * 8,
    )(places, counts, got, tile, v_map, u_map, w1, w2, own_u, piece)
    got = exchange(sent, "col")
    (sent,) = call(
        gather_sums,
        [struct((n_row, 8, 128), BF16)],
        [((n_col * rows, 128), BF16), ((8, 128), F32)] + work[:2],
        [SMEM] + [VMEM] * 5,
    )(places, got, u_map, w1, w3, lead)
    got = exchange(sent, "row")
    result, phi = call(
        finish,
        [struct((piece_rows, 128), F32), struct((8, 128), F32)],
        [((n_row, 8, 128), F32)],
        [VMEM],
    )(got)
    result = result.reshape(piece_rows // 2, 2, 128).transpose(1, 0, 2).reshape(2, piece_rows * 64)
    return (result, phi[0:2, 0])


def solution(mesh):
    return jax.shard_map(
        on_device,
        mesh=mesh,
        in_specs=(
            P("row", "col", None, None, None),
            P("row", "col", None, None),
            P("row", "col"),
            P(None, ("row", "col")),
        ),
        out_specs=(P(None, ("col", "row")), P()),
        check_vma=False,
    )
```

time: 929 us -> 136 us (0.15)
  blocking collectives: 515 us -> 121 us
  local copies, waits for them, and re-layouts: 301 us -> 2.61 us
  starting transfers between devices: 39.6 us -> 0 us
  waiting for transfers between devices: 29.3 us -> 0 us
  other arithmetic: 19.2 us -> 0.86 us
  between operations: 15 us -> 1.32 us
  Pallas kernels: 0 us -> 9.78 us
    psum x5 -> x0, blocking collectives: 478 us -> none  [own_norm(): lax.psum(jnp.sum(values * values, axis=1), ('row', 'col')) + EPS]
    gather x4 -> x0, local copies, waits for them, and re-layouts: 174 us -> none  [select_blocks(): jnp.take(piece, clipped.reshape(-1), axis=1)]
    all_gather x4 -> x0, local copies, waits for them, and re-layouts: 121 us -> none  [the longest x2 80.3 us: gather_v(): return fold_cols(lax.all_gather(v_rounded, 'row', axis=1, tiled=True))]
    all_to_all x0 -> x5, blocking collectives: none -> 98.4 us  [exchange(): return lax.all_to_all(sent, axis, split_axis=0, concat_axis=0, tiled=True)]
    all_to_all x6 -> x0, starting transfers between devices: 39.5 us -> none  [the longest x1 13.7 us: adjoint(): lax.all_to_all(labels, 'row', split_axis=0, concat_axis=0, tiled=True)]
    all_to_all x6 -> x0, waiting for transfers between devices: 29.3 us -> none  [the longest x2 14.6 us: forward_sum(): lax.all_to_all(sent, 'col', split_axis=0, concat_axis=0, tiled=True)]
    all_gather x2 -> x1, blocking collectives: 36.3 us -> 22.4 us  [on_device(): u_group = lax.all_gather(piece, 'col', axis=0, tiled=True)]
    pallas_call x0 -> x6, Pallas kernels: none -> 9.78 us  [the longest x1 2.09 us: on_device(): call(second_forward, [struct((n_col, rows + 8, 128), BF16), struct((rows,...]
  transfers between devices with their start and end apart: 8 -> 0, of which waited for: 4 -> 0; matrix products, arithmetic and copies ran while one was open for 8% -> 0% of each run, Pallas kernels for 0% -> 0%
where the time goes in v1:
time: 136 us; the launch traced here: 135 us
  blocking collectives  121 us (89%)
  Pallas kernels  9.78 us (7%)
  local copies, waits for them, and re-layouts  2.61 us (2%)
    all_to_all x5, blocking collectives, exchange(): return lax.all_to_all(sent, axis, split_axis=0, concat_axis=0, tiled=True)  98.4 us
    all_gather x1, blocking collectives, on_device(): u_group = lax.all_gather(piece, 'col', axis=0, tiled=True)  22.4 us

profile of v1, /device:TPU:1, one launch (start us, length us, event | category | flops | bytes accessed | tf_op | source)
XLA Modules:
  0.0 135.4 jit_solution(1606887146849657699)
XLA Ops:
  1.3 0.0 copy-start.2
  1.3 0.7 copy-done.2
  2.0 0.1 copy.18.coords_ref
  2.0 0.9 convert_element_type.9
  2.9 22.4 %all_gather.3.u_ref = bf16[2048,128]{1,0:T(8,128)(2,1)S(1)} all-gather(bf16[128,128]{1,0:T(8,128)(2,1)S(1)} %bitcast.16), channel_id=1, replica_groups=mesh['row'=32,'col'=16] {'col'}, dimensions={0}, use_global_device_ids=true | all-gather | bytes 557056 | tf_op jit(solution)/shard_map/all_gather | solution.py:324
  25.4 0.0 copy-start
  25.4 1.2 copy-done
  26.6 0.0 copy-start.1
  26.6 1.3 shard_map.59
  27.9 28.5 %all_to_all.25.got_ref = bf16[32,72,128]{2,1,0:T(8,128)(2,1)S(1)} all-to-all(bf16[32,72,128]{2,1,0:T(8,128)(2,1)S(1)} %get-tuple-element.15), channel_id=1, replica_groups=mesh['row'=32,'col'=16] {'row'}, dimensions={0} | all-to-all | bytes 1179648 | tf_op jit(solution)/shard_map/all_to_all | solution.py:319
  56.3 0.0 copy-done.1
  56.3 2.0 %shard_map.60 = (bf16[16,72,128]{2,1,0:T(8,128)(2,1)S(1)}, bf16[64,128]{1,0:T(8,128)(2,1)S(1)}, f32[16,128]{1,0:T(8,128)S(1)}) custom-call(s32[32,2]{1,0:T(8,128)S(1)} %copy.18.coords_ref, s32[1,1]{1,0:T(1,128)S(6)} %copy.20.counts_ref, bf16[32,72,128]{2,1,0:T(8,128)(2,1)S(1)} %all_to_all.25.got_ref, bf16[32,128,128]{2,1,0:T(8,128)(2,1)S(1)} %bitcast.13), custom_call_target="tpu_custom_call" | custom-call | tf_op jit(solution)/shard_map/pallas_call | solution.py:332
  58.3 18.5 %all_to_all.26.got_ref = bf16[16,72,128]{2,1,0:T(8,128)(2,1)S(1)} all-to-all(bf16[16,72,128]{2,1,0:T(8,128)(2,1)S(1)} %get-tuple-element.16), channel_id=1, replica_groups=mesh['row'=32,'col'=16] {'col'}, dimensions={0} | all-to-all | bytes 589824 | tf_op jit(solution)/shard_map/all_to_all | solution.py:319
  76.8 1.5 %shard_map.61 = (bf16[32,64,128]{2,1,0:T(8,128)(2,1)S(1)}, bf16[64,128]{1,0:T(8,128)(2,1)S(1)}, f32[8,128]{1,0:T(8,128)S(1)}) custom-call(s32[32,2]{1,0:T(8,128)S(1)} %copy.18.coords_ref, s32[1,1]{1,0:T(1,128)S(6)} %copy.20.counts_ref, bf16[16,72,128]{2,1,0:T(8,128)(2,1)S(1)} %all_to_all.26.got_ref, bf16[32,128,128]{2,1,0:T(8,128)(2,1)S(1)} %bitcast.14), custom_call_target="tpu_custom_call" | custom-call | tf_op jit(solution)/shard_map/pallas_call | solution.py:339
  78.4 21.7 %all_to_all.27.got_ref = bf16[32,64,128]{2,1,0:T(8,128)(2,1)S(1)} all-to-all(bf16[32,64,128]{2,1,0:T(8,128)(2,1)S(1)} %get-tuple-element.17), channel_id=1, replica_groups=mesh['row'=32,'col'=16] {'row'}, dimensions={0} | all-to-all | bytes 1048576 | tf_op jit(solution)/shard_map/all_to_all | solution.py:319
  100.1 2.1 %shard_map.62 = (bf16[16,72,128]{2,1,0:T(8,128)(2,1)S(1)}, bf16[64,128]{1,0:T(8,128)(2,1)S(1)}, f32[64,128]{1,0:T(8,128)S(1)}) custom-call(s32[32,2]{1,0:T(8,128)S(1)} %copy.18.coords_ref, s32[1,1]{1,0:T(1,128)S(6)} %copy.20.counts_ref, bf16[32,64,128]{2,1,0:T(8,128)(2,1)S(1)} %all_to_all.27.got_ref, bf16[32,128,128]{2,1,0:T(8,128)(2,1)S(1)} %bitcast.15, ...), custom_call_target="tpu_custom_call" | custom-call | tf_op jit(solution)/shard_map/pallas_call | solution.py:346
  102.2 16.1 %all_to_all.28.got_ref = bf16[16,72,128]{2,1,0:T(8,128)(2,1)S(1)} all-to-all(bf16[16,72,128]{2,1,0:T(8,128)(2,1)S(1)} %get-tuple-element.23), channel_id=1, replica_groups=mesh['row'=32,'col'=16] {'col'}, dimensions={0} | all-to-all | bytes 589824 | tf_op jit(solution)/shard_map/all_to_all | solution.py:319
  118.3 2.0 %shard_map.63 = bf16[32,8,128]{2,1,0:T(8,128)(2,1)S(1)} custom-call(s32[32,2]{1,0:T(8,128)S(1)} %copy.18.coords_ref, bf16[16,72,128]{2,1,0:T(8,128)(2,1)S(1)} %all_to_all.28.got_ref, f32[8,128]{1,0:T(8,128)S(1)} %get-tuple-element.19.u_map_ref, bf16[64,128]{1,0:T(8,128)(2,1)S(1)} %get-tuple-element.20.w1_ref, bf16[64,128]{1,0:T(8,128)(2,1)S(1)} %get-tuple-element.24.w3_ref, ...), custom_call_target="tpu_custom_call" | custom-call | tf_op jit(solution)/shard_map/pallas_call | solution.py:353
  120.3 13.6 %all_to_all.29.got_ref = bf16[32,8,128]{2,1,0:T(8,128)(2,1)S(1)} all-to-all(bf16[32,8,128]{2,1,0:T(8,128)(2,1)S(1)} %shard_map.63), channel_id=1, replica_groups=mesh['row'=32,'col'=16] {'row'}, dimensions={0} | all-to-all | bytes 131072 | tf_op jit(solution)/shard_map/all_to_all | solution.py:319
  133.8 0.9 shard_map.64
  134.8 0.6 slice_reduce_fusion
Async XLA Ops:
  1.3 0.7 copy-start.2
  25.4 1.2 copy-start
  26.6 29.8 %copy-start.1 = (bf16[1,1,32,128,128]{4,3,2,1,0:T(8,128)(2,1)S(1)}, bf16[1,1,32,128,128]{4,3,2,1,0:T(8,128)(2,1)}, u32[]{:S(2)}) copy-start(bf16[1,1,32,128,128]{4,3,2,1,0:T(8,128)(2,1)} %param.4) | copy-start | bytes 3145732

commit v2 on v0

v2 whole, which is shorter than its diff:
```python
import jax
import jax.numpy as jnp
from jax import lax
from jax.experimental import pallas as pl
from jax.experimental.pallas import tpu as pltpu
from jax.sharding import Mesh
from jax.sharding import PartitionSpec as P

EPS = 1e-06
F32 = jnp.float32
BF16 = jnp.bfloat16
ROW = ("z", "x")
COL = ("y", "core")
VMEM = pl.BlockSpec(memory_space=pltpu.VMEM)
SMEM = pl.BlockSpec(memory_space=pltpu.SMEM)


def iota(shape, dim):
    return lax.broadcasted_iota(jnp.int32, shape, dim)


def row_index():
    return lax.axis_index("z") * lax.axis_size("x") + lax.axis_index("x")


def col_index():
    return lax.axis_index("y") * lax.axis_size("core") + lax.axis_index("core")


def fill_keys(keys_ref, places_ref, count, axis, me):
    slots = places_ref.shape[1]
    for k in range(slots):
        block = jnp.where(k < count, places_ref[axis, k], -8)
        keys_ref[k : k + 1, :] = jnp.full((1, 128), block, jnp.int32).astype(F32)
    own = keys_ref.shape[0] - slots
    keys_ref[slots:, :] = (me * own + iota((own, 128), 0)).astype(F32)


def lane_keys(places_ref, count, axis):
    slots = places_ref.shape[1]
    slot = iota((8, 128), 1) % slots
    keys = jnp.full((8, 128), -1, jnp.int32)
    for k in range(slots):
        keys = jnp.where(slot == k, jnp.where(k < count, places_ref[axis, k], -1), keys)
    keys = keys.astype(F32)
    high = jnp.floor(keys * (1.0 / 64.0))
    sub = iota((8, 128), 0)
    return jnp.where(sub == 0, high, jnp.where(sub == 1, keys - 64.0 * high, 0.0)).astype(BF16)


def read_keys(got_ref, map_ref):
    rows = got_ref.shape[1] - 8
    quarter = iota((8, 128), 1) // 32
    for g in range(got_ref.shape[0] // 4):
        both = got_ref[4 * g, rows:, :].astype(F32)
        for i in range(1, 4):
            both = jnp.where(quarter == i, got_ref[4 * g + i, rows:, :].astype(F32), both)
        map_ref[g : g + 1, :] = both[0:1, :] * 64.0 + both[1:2, :]


def four_peers(got_ref, g):
    halves = []
    for r in range(2):
        halves.append(jnp.concatenate([got_ref[4 * g + i, 32 * r : 32 * r + 32, :] for i in range(4)], axis=0))
    return jnp.concatenate(halves, axis=1)


def sum_by_key(got_ref, map_ref, keys_ref):
    keys = keys_ref[...]
    total = jnp.zeros((keys.shape[0], 256), F32)
    for g in range(0, got_ref.shape[0] // 4, 2):
        match = jnp.concatenate([(keys == map_ref[g + i : g + i + 1, :]).astype(F32) for i in range(2)], axis=1)
        values = jnp.concatenate([four_peers(got_ref, g + i) for i in range(2)], axis=0)
        total = total + jnp.dot(match.astype(BF16), values, preferred_element_type=F32)
    return total


def products(held_ref, tile_ref, out_ref, adjoint):
    pair = iota((8, 128), 0) // 2
    for j in range(tile_ref.shape[0] // 4):
        rows = held_ref[8 * j : 8 * j + 8, :]
        left = jnp.concatenate([jnp.where(pair == i, rows, 0.0) for i in range(4)], axis=1).astype(BF16)
        blocks = [tile_ref[4 * j + i] for i in range(4)]
        right = jnp.concatenate(blocks, axis=0 if adjoint else 1)
        dims = (((1,), (0 if adjoint else 1,)), ((), ()))
        out_ref[8 * j : 8 * j + 8, :] = lax.dot_general(left, right, dims, preferred_element_type=F32)


def split_rows(ref):
    half = ref.shape[0] // 2
    return jnp.concatenate([ref[pl.ds(r, half, stride=2), :] for r in range(2)], axis=0)


def hold(held_ref, own):
    half = held_ref.shape[0] // 2
    for r in range(2):
        held_ref[pl.ds(r, half, stride=2), :] = own[:, 128 * r : 128 * r + 128].astype(F32)


def send_all(sent_ref, values, extra):
    rows = values.shape[0]
    for peer in range(sent_ref.shape[0]):
        sent_ref[peer, 0:rows, :] = values
        if extra is not None:
            sent_ref[peer, rows:, :] = extra


def begin(rhs_ref, sent_ref, piece_ref, rows):
    for b in range(rows.shape[0] // 2):
        rows[2 * b : 2 * b + 2, :] = rhs_ref[:, 128 * b : 128 * b + 128]
    send_all(sent_ref, rows[...].astype(BF16), None)
    half = rows.shape[0] // 2
    piece_ref[...] = jnp.concatenate([rows[pl.ds(r, half, stride=2), :] for r in range(2)], axis=1).astype(BF16)


def first_adjoint(places_ref, counts_ref, u_ref, tile_ref, sent_ref, own_u_ref, held, out):
    count = counts_ref[0, 0]
    cores = lax.axis_size("core")
    chips = lax.axis_size("y")
    span = u_ref.shape[0] // (cores * chips)
    for k in range(places_ref.shape[1]):
        block = places_ref[0, k]
        owner = block // span
        row = ((owner % cores) * chips + owner // cores) * span + block % span
        held[2 * k : 2 * k + 2, :] = u_ref[row].astype(F32) * (k < count).astype(F32)
    own_u_ref[...] = split_rows(held).astype(BF16)
    products(held, tile_ref, out, True)
    send_all(sent_ref, split_rows(out).astype(BF16), lane_keys(places_ref, count, 1))


def keep(w, w_ref, piece_ref, held):
    slots = held.shape[0] // 2
    w = w.astype(BF16)
    own = w[0:slots, :]
    piece_ref[...] = w[slots:, :]
    hold(held, own)
    if w_ref is not None:
        w_ref[...] = jnp.concatenate([own[:, 0:128], own[:, 128:256]], axis=0)


def first_forward(places_ref, counts_ref, got_ref, tile_ref, sent_ref, piece_ref, map_ref, keys, held, out):
    count = counts_ref[0, 0]
    fill_keys(keys, places_ref, count, 1, row_index())
    read_keys(got_ref, map_ref)
    keep(sum_by_key(got_ref, map_ref, keys), None, piece_ref, held)
    products(held, tile_ref, out, False)
    send_all(sent_ref, split_rows(out).astype(BF16), lane_keys(places_ref, count, 0))


def second_adjoint(places_ref, counts_ref, got_ref, tile_ref, sent_ref, w_ref, piece_ref, map_ref, keys, held, out):
    fill_keys(keys, places_ref, counts_ref[0, 0], 0, col_index())
    read_keys(got_ref, map_ref)
    keep(sum_by_key(got_ref, map_ref, keys), w_ref, piece_ref, held)
    products(held, tile_ref, out, True)
    send_all(sent_ref, split_rows(out).astype(BF16), None)


def sum_halves(first, second):
    folds = []
    for values in (first, second):
        fold = jnp.sum(values.reshape(values.shape[0] // 8, 8, 128), axis=0)
        folds.append(fold + pltpu.roll(fold, 4, 0))
    return jnp.sum(jnp.where(iota((8, 128), 0) < 4, folds[0], folds[1]), axis=1, keepdims=True)


def sum_piece(values):
    return sum_halves(values[:, 0:128], values[:, 128:256])


def sum_slots(values):
    half = values.shape[0] // 2
    return sum_halves(values[0:half, :], values[half:, :])


def three_parts(values):
    values = jnp.where(iota(values.shape, 1) < 16, values, 0.0)
    high = values.astype(BF16).astype(F32)
    middle = (values - high).astype(BF16).astype(F32)
    low = (values - high - middle).astype(BF16).astype(F32)
    return high + pltpu.roll(middle, 16, 1) + pltpu.roll(low, 32, 1)


def whole_sums(parts):
    return parts + pltpu.roll(parts, 112, 1) + pltpu.roll(parts, 96, 1)


def second_forward(
    places_ref, counts_ref, got_ref, tile_ref, map_ref, w1_ref, w2_ref, u0_ref, own_w2_ref, own_u_ref,
    sent_ref, piece_ref, keys, held, out,
):
    fill_keys(keys, places_ref, counts_ref[0, 0], 1, row_index())
    keep(sum_by_key(got_ref, map_ref, keys), None, piece_ref, held)
    products(held, tile_ref, out, False)
    sent = split_rows(out).astype(BF16)
    w1 = w1_ref[...].astype(F32)
    w2 = w2_ref[...].astype(F32)
    u0 = u0_ref[...].astype(F32)
    w3 = piece_ref[...].astype(F32)
    c4 = sent.astype(F32)
    sums = [
        sum_piece(w1 * w1),
        sum_piece(w1 * w3),
        sum_piece(w3 * w3),
        sum_piece(u0 * u0),
        sum_piece(u0 * w2),
        sum_piece(w2 * w2),
        sum_slots(c4 * own_w2_ref[...].astype(F32)),
        sum_slots(c4 * own_u_ref[...].astype(F32)),
    ]
    lane = iota((8, 128), 1)
    block = jnp.zeros((8, 128), F32)
    for j, value in enumerate(sums):
        block = jnp.where(lane == j, value, block)
    send_all(sent_ref, sent, three_parts(block).astype(BF16))


def gather_sums(got_ref, map_ref, sent_ref):
    peers = got_ref.shape[0]
    rows = got_ref.shape[1] - 8
    partial = got_ref[0, rows:, :].astype(F32)
    for peer in range(1, peers):
        partial = partial + got_ref[peer, rows:, :].astype(F32)
    groups = peers // 4
    values = jnp.concatenate([four_peers(got_ref, g) for g in range(groups)], axis=0)
    square = jnp.zeros((8, 256), F32)
    for g in range(groups):
        column = jnp.transpose(jnp.broadcast_to(map_ref[g : g + 1, :], (128, 128)))
        match = [jnp.where(column == map_ref[h : h + 1, :], 1.0 if h == g else 2.0, 0.0) for h in range(g, groups)]
        total = jnp.dot(jnp.concatenate(match, axis=1).astype(BF16), values[128 * g :, :], preferred_element_type=F32)
        square = square + jnp.sum((values[128 * g : 128 * g + 128, :].astype(F32) * total).reshape(16, 8, 256), axis=0)
    last = sum_piece(square)
    lane = iota((8, 128), 1)
    block = jnp.where(lane == 8, last, whole_sums(partial))
    block = block + pltpu.roll(block, 1, 0)
    block = three_parts(block + pltpu.roll(block, 2, 0)).astype(BF16).astype(F32)
    block = jnp.concatenate([block[3:4, :], block[7:8, :]], axis=0).astype(BF16)
    for peer in range(sent_ref.shape[0]):
        sent_ref[peer] = block


def finish(got_ref, w1_ref, w3_ref, solution_ref, phi_ref):
    total = jnp.sum(got_ref[...].astype(F32), axis=0)
    first = iota((8, 128), 0) < 4
    sums = whole_sums(jnp.where(first, total[0:1, :], total[1:2, :]))

    def pick(j):
        return jnp.broadcast_to(sums[:, j : j + 1], (8, 128))

    t11, t13, t33, s00, s02, s22, s24, s04, s44 = [pick(j) for j in range(9)]

    def norm(square):
        return jnp.sqrt(jnp.maximum(square, 0.0) + EPS)

    beta0 = norm(s00)
    alpha1 = norm(t11 / (beta0 * beta0))
    x2 = 1.0 / (beta0 * alpha1)
    x0 = -alpha1 / beta0
    beta1 = norm(x2 * x2 * s22 + 2.0 * x2 * x0 * s02 + x0 * x0 * s00)
    y3 = x2 / beta1
    y1 = x0 / beta1 - beta1 * x2
    alpha2 = norm(y3 * y3 * t33 + 2.0 * y3 * y1 * t13 + y1 * y1 * t11)
    ratio = alpha2 / beta1
    z4 = y3 / alpha2
    z2 = y1 / alpha2 - ratio * x2
    z0 = -ratio * x0
    beta2 = norm(
        z4 * z4 * s44 + z2 * z2 * s22 + z0 * z0 * s00 + 2.0 * (z4 * z2 * s24 + z4 * z0 * s04 + z2 * z0 * s02)
    )
    rho1 = jnp.sqrt(alpha1 * alpha1 + beta1 * beta1)
    cosine1 = alpha1 / rho1
    sine1 = beta1 / rho1
    phi1 = cosine1 * beta0
    phi_bar1 = sine1 * beta0
    theta = sine1 * alpha2
    rho_bar2 = -cosine1 * alpha2
    rho2 = jnp.sqrt(rho_bar2 * rho_bar2 + beta2 * beta2)
    cosine2 = rho_bar2 / rho2
    sine2 = beta2 / rho2
    phi2 = cosine2 * phi_bar1
    phi_bar2 = sine2 * phi_bar1
    share1 = phi1 / rho1
    share2 = phi2 / rho2
    k1 = share1 * x2 + share2 * (y1 / alpha2 - (theta / rho1) * x2)
    k3 = share2 * y3 / alpha2

    phi_ref[...] = jnp.where(iota((1, 128), 1) == 0, phi_bar2[0:1, :], phi_bar2[4:5, :])[:, 0:2]
    half = w1_ref.shape[0]
    for r in range(2):
        w1 = w1_ref[:, 128 * r : 128 * r + 128].astype(F32)
        w3 = w3_ref[:, 128 * r : 128 * r + 128].astype(F32)
        solution_ref[pl.ds(r, half, stride=2), :] = w1 * k1[4 * r : 4 * r + 1, :] + w3 * k3[4 * r : 4 * r + 1, :]


def struct(shape, dtype):
    return jax.ShapeDtypeStruct(shape, dtype)


def on_device(tiles, coords, counts, rhs):
    chips = lax.axis_size("y")
    n_row = lax.axis_size("z") * lax.axis_size("x")
    n_col = chips * lax.axis_size("core")
    slots = tiles.shape[2]
    rows = 2 * slots
    span = rhs.shape[1] // 128
    places = coords[0, 0].T

    def call(body, specs, outs, scratch, *operands):
        return pl.pallas_call(
            body,
            out_shape=outs,
            in_specs=specs,
            out_specs=[VMEM] * len(outs),
            scratch_shapes=scratch,
            compiler_params=pltpu.CompilerParams(vmem_limit_bytes=32 * 1024 * 1024),
        )(*operands)

    def exchange(sent, axis):
        return lax.all_to_all(sent, axis, split_axis=0, concat_axis=0, tiled=True)

    def exchange_col(sent):
        return lax.all_gather(exchange(sent, "y"), "core", axis=0, tiled=True)

    wide = pltpu.VMEM((rows, 128), F32)
    keys = pltpu.VMEM((slots + span, 128), F32)
    two = [SMEM, SMEM]
    piece = struct((span, 256), BF16)
    own = struct((rows, 128), BF16)
    tile = tiles[0, 0]
    sent, u0 = call(
        begin,
        [VMEM],
        [struct((chips, 2 * span, 128), BF16), piece],
        [pltpu.VMEM((2 * span, 128), F32)],
        rhs,
    )
    u_group = exchange_col(sent).reshape(n_col * span, 2, 128)
    sent, own_u = call(
        first_adjoint,
        two + [VMEM] * 2,
        [struct((n_row, rows + 8, 128), BF16), own],
        [wide, wide],
        places, counts, u_group, tile,
    )
    sent, w1, v_map = call(
        first_forward,
        two + [VMEM] * 2,
        [struct((chips, rows + 8, 128), BF16), piece, struct((n_row // 4, 128), F32)],
        [keys, wide, wide],
        places, counts, exchange(sent, ROW), tile,
    )
    sent, own_w2, w2, u_map = call(
        second_adjoint,
        two + [VMEM] * 2,
        [struct((n_row, rows, 128), BF16), own, piece, struct((n_col // 4, 128), F32)],
        [keys, wide, wide],
        places, counts, exchange_col(sent), tile,
    )
    sent, w3 = call(
        second_forward,
        two + [VMEM] * 8,
        [struct((chips, rows + 8, 128), BF16), piece],
        [keys, wide, wide],
        places, counts, exchange(sent, ROW), tile, v_map, w1, w2, u0, own_w2, own_u,
    )
    (sent,) = call(
        gather_sums,
        [VMEM] * 2,
        [struct((n_row, 2, 128), BF16)],
        [],
        exchange_col(sent), u_map,
    )
    result, phi_bar = call(
        finish,
        [VMEM] * 3,
        [struct((2 * span, 128), F32), struct((1, 2), F32)],
        [],
        exchange(sent, ROW), w1, w3,
    )
    result = result.reshape(span, 2, 128).transpose(1, 0, 2).reshape(2, span * 128)
    return (result, phi_bar.reshape(2))


def solution(mesh):
    n_row, n_col = mesh.devices.shape
    fine = Mesh(mesh.devices.reshape(n_row // 4, 4, n_col // 2, 2), ROW + COL)
    return jax.shard_map(
        on_device,
        mesh=fine,
        in_specs=(P(ROW, COL, None, None, None), P(ROW, COL, None, None), P(ROW, COL), P(None, ROW + COL)),
        out_specs=(P(None, COL + ROW), P()),
        check_vma=False,
    )
```

time: 929 us -> 127 us (0.14)
  blocking collectives: 515 us -> 100 us
  local copies, waits for them, and re-layouts: 301 us -> 1.51 us
  starting transfers between devices: 39.6 us -> 7.65 us
  waiting for transfers between devices: 29.3 us -> 8.76 us
  other arithmetic: 19.2 us -> 0 us
  between operations: 15 us -> 1.32 us
    psum x5 -> x0, blocking collectives: 478 us -> none  [own_norm(): lax.psum(jnp.sum(values * values, axis=1), ('row', 'col')) + EPS]
    gather x4 -> x0, local copies, waits for them, and re-layouts: 174 us -> none  [select_blocks(): jnp.take(piece, clipped.reshape(-1), axis=1)]
    all_gather x4 -> x0, local copies, waits for them, and re-layouts: 121 us -> none  [the longest x2 80.3 us: gather_v(): return fold_cols(lax.all_gather(v_rounded, 'row', axis=1, tiled=True))]
    all_to_all x0 -> x5, blocking collectives: none -> 84.8 us  [exchange(): return lax.all_to_all(sent, axis, split_axis=0, concat_axis=0, tiled=True)]
    all_to_all x6 -> x1, starting transfers between devices: 39.5 us -> 7.65 us  [exchange(): return lax.all_to_all(sent, axis, split_axis=0, concat_axis=0, tiled=True)]
    all_gather x2 -> x3, blocking collectives: 36.3 us -> 15.3 us  [exchange_col(): return lax.all_gather(exchange(sent, 'y'), 'core', axis=0, tiled=True)]
    all_to_all x6 -> x1, waiting for transfers between devices: 29.3 us -> 8.76 us  [exchange(): return lax.all_to_all(sent, axis, split_axis=0, concat_axis=0, tiled=True)]
  transfers between devices with their start and end apart: 8 -> 1, of which waited for: 4 -> 1; matrix products, arithmetic and copies ran while one was open for 8% -> 0% of each run, Pallas kernels for 0% -> 0%
where the time goes in v2:
time: 127 us; the launch traced here: 126 us
  blocking collectives  100 us (79%)
  waiting for transfers between devices  8.76 us (7%)
  starting transfers between devices  7.65 us (6%)
  Pallas kernels  6.95 us (5%)
  local copies, waits for them, and re-layouts  1.51 us (1%)
  between operations  1.32 us (1%)
    all_to_all x5, blocking collectives, exchange(): return lax.all_to_all(sent, axis, split_axis=0, concat_axis=0, tiled=True)  84.8 us
    all_gather x3, blocking collectives, exchange_col(): return lax.all_gather(exchange(sent, 'y'), 'core', axis=0, tiled=True)  15.3 us
    all_to_all x1, waiting for transfers between devices, exchange(): return lax.all_to_all(sent, axis, split_axis=0, concat_axis=0, tiled=True)  8.76 us
    all_to_all x1, starting transfers between devices, exchange(): return lax.all_to_all(sent, axis, split_axis=0, concat_axis=0, tiled=True)  7.65 us
    pallas_call x7, Pallas kernels, call(): pl.pallas_call(body, out_shape=outs, in_specs=specs, out_specs=[VMEM] * l...  6.95 us
  transfers between devices with their start and end apart: 1, of which 1 were waited for; matrix products, arithmetic and copies ran while one was open for 0% of the time, Pallas kernels for 0%

profile of v2, /device:TPU:1, one launch (start us, length us, event | category | flops | bytes accessed | tf_op | source)
XLA Modules:
  0.0 126.4 jit_solution(2585501152907857883)
XLA Ops:
  0.6 0.0 copy-start.1
  0.6 0.8 copy-done.1
  1.5 0.0 copy-start
  1.5 0.7 shard_map.59
  2.2 7.7 %all-to-all-start = ((bf16[8,128,128]{2,1,0:T(8,128)(2,1)}), bf16[8,128,128]{2,1,0:T(8,128)(2,1)S(1)}, u32[]{:S(2)}, u32[]{:S(2)}) async-start(bf16[8,128,128]{2,1,0:T(8,128)(2,1)} %get-tuple-element.17), calls=%async_computation | async-start | bytes 524288 | tf_op jit(solution)/shard_map/all_to_all | solution.py:318
  10.5 8.8 %all-to-all-done = bf16[8,128,128]{2,1,0:T(8,128)(2,1)S(1)} async-done(((bf16[8,128,128]{2,1,0:T(8,128)(2,1)}), bf16[8,128,128]{2,1,0:T(8,128)(2,1)S(1)}, u32[]{:S(2)}, u32[]{:S(2)}) %all-to-all-start) | async-done | bytes 262176 | tf_op jit(solution)/shard_map/all_to_all | solution.py:318
  19.3 5.4 %all_gather.9 = bf16[16,128,128]{2,1,0:T(8,128)(2,1)S(1)} all-gather(bf16[8,128,128]{2,1,0:T(8,128)(2,1)S(1)} %all-to-all-done), channel_id=1, replica_groups=mesh['z'=8,'x'=4,'y'=8,'core'=2] {'core'}, dimensions={0}, use_global_device_ids=true | all-gather | bytes 786432 | tf_op jit(solution)/shard_map/all_gather | solution.py:321
  24.7 0.0 copy-start.2
  24.7 0.0 copy-done
  24.7 0.7 copy-done.2
  25.4 1.1 shard_map.60
  26.5 30.1 %all_to_all.30.got_ref = bf16[32,72,128]{2,1,0:T(8,128)(2,1)S(1)} all-to-all(bf16[32,72,128]{2,1,0:T(8,128)(2,1)S(1)} %get-tuple-element.18), channel_id=1, replica_groups=mesh['z'=8,'x'=4,'y'=8,'core'=2] {'z','x'}, dimensions={0} | all-to-all | bytes 1179648 | tf_op jit(solution)/shard_map/all_to_all | solution.py:318
  56.6 1.2 shard_map.61
  57.9 10.6 %all_to_all.31 = bf16[8,72,128]{2,1,0:T(8,128)(2,1)S(1)} all-to-all(bf16[8,72,128]{2,1,0:T(8,128)(2,1)S(1)} %get-tuple-element.19), channel_id=1, replica_groups=mesh['z'=8,'x'=4,'y'=8,'core'=2] {'y'}, dimensions={0} | all-to-all | bytes 294912 | tf_op jit(solution)/shard_map/all_to_all | solution.py:318
  68.5 5.0 %all_gather.10.got_ref = bf16[16,72,128]{2,1,0:T(8,128)(2,1)S(1)} all-gather(bf16[8,72,128]{2,1,0:T(8,128)(2,1)S(1)} %all_to_all.31), channel_id=1, replica_groups=mesh['z'=8,'x'=4,'y'=8,'core'=2] {'core'}, dimensions={0}, use_global_device_ids=true | all-gather | bytes 442368 | tf_op jit(solution)/shard_map/all_gather | solution.py:321
  73.5 1.0 shard_map.62
  74.5 20.9 %all_to_all.32.got_ref = bf16[32,64,128]{2,1,0:T(8,128)(2,1)S(1)} all-to-all(bf16[32,64,128]{2,1,0:T(8,128)(2,1)S(1)} %get-tuple-element.20), channel_id=1, replica_groups=mesh['z'=8,'x'=4,'y'=8,'core'=2] {'z','x'}, dimensions={0} | all-to-all | bytes 1048576 | tf_op jit(solution)/shard_map/all_to_all | solution.py:318
  95.4 1.4 %shard_map.63 = (bf16[8,72,128]{2,1,0:T(8,128)(2,1)S(1)}, bf16[64,256]{1,0:T(8,128)(2,1)S(1)}) custom-call(s32[2,32]{1,0:T(2,128)S(1)} %bitcast.19, s32[1,1]{1,0:T(1,128)S(6)} %copy.8.counts_ref, bf16[32,64,128]{2,1,0:T(8,128)(2,1)S(1)} %all_to_all.32.got_ref, bf16[32,128,128]{2,1,0:T(8,128)(2,1)S(1)} %bitcast.14, f32[8,128]{1,0:T(8,128)S(1)} %get-tuple-element.21.map_ref, ...), custom_call_target="tpu_custom_call" | custom-call | tf_op jit(solution)/shard_map/pallas_call | solution.py:308
  96.8 10.6 %all_to_all.33 = bf16[8,72,128]{2,1,0:T(8,128)(2,1)S(1)} all-to-all(bf16[8,72,128]{2,1,0:T(8,128)(2,1)S(1)} %get-tuple-element.27), channel_id=1, replica_groups=mesh['z'=8,'x'=4,'y'=8,'core'=2] {'y'}, dimensions={0} | all-to-all | bytes 294912 | tf_op jit(solution)/shard_map/all_to_all | solution.py:318
  107.4 4.9 %all_gather.11.got_ref = bf16[16,72,128]{2,1,0:T(8,128)(2,1)S(1)} all-gather(bf16[8,72,128]{2,1,0:T(8,128)(2,1)S(1)} %all_to_all.33), channel_id=1, replica_groups=mesh['z'=8,'x'=4,'y'=8,'core'=2] {'core'}, dimensions={0}, use_global_device_ids=true | all-gather | bytes 442368 | tf_op jit(solution)/shard_map/all_gather | solution.py:321
  112.3 0.5 shard_map.64
  112.8 12.7 %all_to_all.34.got_ref = bf16[32,2,128]{2,1,0:T(2,128)(2,1)S(1)} all-to-all(bf16[32,2,128]{2,1,0:T(2,128)(2,1)S(1)} %shard_map.64), channel_id=1, replica_groups=mesh['z'=8,'x'=4,'y'=8,'core'=2] {'z','x'}, dimensions={0} | all-to-all | bytes 32768 | tf_op jit(solution)/shard_map/all_to_all | solution.py:318
  125.5 0.9 shard_map.65
Async XLA Ops:
  0.6 0.8 copy-start.1
  1.5 23.2 %copy-start = (bf16[1,1,32,128,128]{4,3,2,1,0:T(8,128)(2,1)S(1)}, bf16[1,1,32,128,128]{4,3,2,1,0:T(8,128)(2,1)}, u32[]{:S(2)}) copy-start(bf16[1,1,32,128,128]{4,3,2,1,0:T(8,128)(2,1)} %param.4) | copy-start | bytes 3145732
  2.2 17.1 %all-to-all-start = ((bf16[8,128,128]{2,1,0:T(8,128)(2,1)}), bf16[8,128,128]{2,1,0:T(8,128)(2,1)S(1)}, u32[]{:S(2)}, u32[]{:S(2)}) async-start(bf16[8,128,128]{2,1,0:T(8,128)(2,1)} %get-tuple-element.17), calls=%async_computation | async-start | bytes 524288 | tf_op jit(solution)/shard_map/all_to_all | solution.py:318
  24.7 0.7 copy-start.2

commit v3 on v2

--- a/solution.py
+++ b/solution.py
@@ -27,13 +27,17 @@
     return lax.axis_index("y") * lax.axis_size("core") + lax.axis_index("core")
 
 
-def fill_keys(keys_ref, places_ref, count, axis, me):
+def slot_keys(places_ref, count, axis):
     slots = places_ref.shape[1]
+    row = iota((slots, 128), 0)
+    keys = jnp.full((slots, 128), -8, jnp.int32)
     for k in range(slots):
-        block = jnp.where(k < count, places_ref[axis, k], -8)
-        keys_ref[k : k + 1, :] = jnp.full((1, 128), block, jnp.int32).astype(F32)
-    own = keys_ref.shape[0] - slots
-    keys_ref[slots:, :] = (me * own + iota((own, 128), 0)).astype(F32)
+        keys = jnp.where(row == k, jnp.where(k < count, places_ref[axis, k], -8), keys)
+    return keys.astype(F32)
+
+
+def with_range(slot_ref, me, span):
+    return jnp.concatenate([slot_ref[...], (me * span + iota((span, 128), 0)).astype(F32)], axis=0)
 
 
 def lane_keys(places_ref, count, axis):
@@ -65,8 +69,7 @@
     return jnp.concatenate(halves, axis=1)
 
 
-def sum_by_key(got_ref, map_ref, keys_ref):
-    keys = keys_ref[...]
+def sum_by_key(got_ref, map_ref, keys):
     total = jnp.zeros((keys.shape[0], 256), F32)
     for g in range(0, got_ref.shape[0] // 4, 2):
         match = jnp.concatenate([(keys == map_ref[g + i : g + i + 1, :]).astype(F32) for i in range(2)], axis=1)
@@ -105,15 +108,19 @@
             sent_ref[peer, rows:, :] = extra
 
 
-def begin(rhs_ref, sent_ref, piece_ref, rows):
+def begin(places_ref, counts_ref, rhs_ref, sent_ref, piece_ref, slot_v_ref, slot_u_ref, lane_v_ref, lane_u_ref, rows):
     for b in range(rows.shape[0] // 2):
         rows[2 * b : 2 * b + 2, :] = rhs_ref[:, 128 * b : 128 * b + 128]
     send_all(sent_ref, rows[...].astype(BF16), None)
     half = rows.shape[0] // 2
     piece_ref[...] = jnp.concatenate([rows[pl.ds(r, half, stride=2), :] for r in range(2)], axis=1).astype(BF16)
-
-
-def first_adjoint(places_ref, counts_ref, u_ref, tile_ref, sent_ref, own_u_ref, held, out):
+    count = counts_ref[0, 0]
+    for axis, slot_ref, lane_ref in ((0, slot_u_ref, lane_u_ref), (1, slot_v_ref, lane_v_ref)):
+        slot_ref[...] = slot_keys(places_ref, count, axis)
+        lane_ref[...] = lane_keys(places_ref, count, axis)
+
+
+def first_adjoint(places_ref, counts_ref, lane_ref, u_ref, tile_ref, sent_ref, own_u_ref, held, out):
     count = counts_ref[0, 0]
     cores = lax.axis_size("core")
     chips = lax.axis_size("y")
@@ -125,7 +132,7 @@
         held[2 * k : 2 * k + 2, :] = u_ref[row].astype(F32) * (k < count).astype(F32)
     own_u_ref[...] = split_rows(held).astype(BF16)
     products(held, tile_ref, out, True)
-    send_all(sent_ref, split_rows(out).astype(BF16), lane_keys(places_ref, count, 1))
+    send_all(sent_ref, split_rows(out).astype(BF16), lane_ref[...])
 
 
 def keep(w, w_ref, piece_ref, held):
@@ -134,25 +141,43 @@
     own = w[0:slots, :]
     piece_ref[...] = w[slots:, :]
     hold(held, own)
-    if w_ref is not None:
-        w_ref[...] = jnp.concatenate([own[:, 0:128], own[:, 128:256]], axis=0)
-
-
-def first_forward(places_ref, counts_ref, got_ref, tile_ref, sent_ref, piece_ref, map_ref, keys, held, out):
-    count = counts_ref[0, 0]
-    fill_keys(keys, places_ref, count, 1, row_index())
+    w_ref[...] = jnp.concatenate([own[:, 0:128], own[:, 128:256]], axis=0)
+
+
+def first_forward(slot_ref, lane_ref, got_ref, tile_ref, sent_ref, w_ref, piece_ref, map_ref, held, out):
     read_keys(got_ref, map_ref)
-    keep(sum_by_key(got_ref, map_ref, keys), None, piece_ref, held)
+    keys = with_range(slot_ref, row_index(), piece_ref.shape[0])
+    keep(sum_by_key(got_ref, map_ref, keys), w_ref, piece_ref, held)
     products(held, tile_ref, out, False)
-    send_all(sent_ref, split_rows(out).astype(BF16), lane_keys(places_ref, count, 0))
-
-
-def second_adjoint(places_ref, counts_ref, got_ref, tile_ref, sent_ref, w_ref, piece_ref, map_ref, keys, held, out):
-    fill_keys(keys, places_ref, counts_ref[0, 0], 0, col_index())
+    send_all(sent_ref, split_rows(out).astype(BF16), lane_ref[...])
+
+
+def second_adjoint(slot_ref, lane_ref, got_ref, tile_ref, sent_ref, w_ref, piece_ref, map_ref, held, out):
     read_keys(got_ref, map_ref)
+    keys = with_range(slot_ref, col_index(), piece_ref.shape[0])
     keep(sum_by_key(got_ref, map_ref, keys), w_ref, piece_ref, held)
     products(held, tile_ref, out, True)
-    send_all(sent_ref, split_rows(out).astype(BF16), None)
+    send_all(sent_ref, split_rows(out).astype(BF16), lane_ref[...])
+
+
+def regroup(map_ref, got_ref, sent_ref, line_ref):
+    read_keys(got_ref, line_ref)
+    target = map_ref[pl.ds(lax.axis_index("z"), 1), :]
+    column = jnp.transpose(jnp.broadcast_to(target, (128, 128)))
+    total = sum_by_key(got_ref, line_ref, column).astype(BF16)
+    for peer in range(sent_ref.shape[0]):
+        for r in range(2):
+            sent_ref[peer, 32 * r : 32 * r + 32, :] = total[32 * peer : 32 * peer + 32, 128 * r : 128 * r + 128]
+
+
+def leaders(map_ref, slot_ref, me):
+    keys = slot_ref[...]
+    quarter = iota(keys.shape, 1) // 32
+    earlier = jnp.zeros(keys.shape, F32)
+    for g in range(map_ref.shape[0]):
+        earlier = earlier + ((keys == map_ref[g : g + 1, :]) & (4 * g + quarter < me)).astype(F32)
+    count = jnp.sum(earlier, axis=1, keepdims=True)
+    return ((count == 0.0) & (keys >= 0.0)).astype(F32)
 
 
 def sum_halves(first, second):
@@ -185,22 +210,32 @@
 
 
 def second_forward(
-    places_ref, counts_ref, got_ref, tile_ref, map_ref, w1_ref, w2_ref, u0_ref, own_w2_ref, own_u_ref,
-    sent_ref, piece_ref, keys, held, out,
+    slot_ref, map_ref, got_ref, tile_ref, own_w1_ref, w2_ref, u0_ref, own_w2_ref, own_u_ref,
+    sent_ref, lead_w3_ref, lead_ref, held, out,
 ):
-    fill_keys(keys, places_ref, counts_ref[0, 0], 1, row_index())
-    keep(sum_by_key(got_ref, map_ref, keys), None, piece_ref, held)
+    w3 = got_ref[0].astype(F32)
+    for peer in range(1, got_ref.shape[0]):
+        w3 = w3 + got_ref[peer].astype(F32)
+    w3 = w3.astype(BF16).astype(F32)
+    half = w3.shape[0] // 2
+    for r in range(2):
+        held[pl.ds(r, half, stride=2), :] = w3[half * r : half * r + half, :]
     products(held, tile_ref, out, False)
     sent = split_rows(out).astype(BF16)
-    w1 = w1_ref[...].astype(F32)
+    lead = leaders(map_ref, slot_ref, row_index())
+    lead_ref[...] = lead
+    lead = jnp.concatenate([lead, lead], axis=0)
+    lead_w3 = w3 * lead
+    for r in range(2):
+        lead_w3_ref[pl.ds(r, half, stride=2), :] = lead_w3[half * r : half * r + half, :]
+    w1 = own_w1_ref[...].astype(F32)
     w2 = w2_ref[...].astype(F32)
     u0 = u0_ref[...].astype(F32)
-    w3 = piece_ref[...].astype(F32)
     c4 = sent.astype(F32)
     sums = [
-        sum_piece(w1 * w1),
-        sum_piece(w1 * w3),
-        sum_piece(w3 * w3),
+        sum_slots(w1 * w1 * lead),
+        sum_slots(w1 * lead_w3),
+        sum_slots(w3 * lead_w3),
         sum_piece(u0 * u0),
         sum_piece(u0 * w2),
         sum_piece(w2 * w2),
@@ -214,7 +249,7 @@
     send_all(sent_ref, sent, three_parts(block).astype(BF16))
 
 
-def gather_sums(got_ref, map_ref, sent_ref):
+def gather_sums(places_ref, got_ref, map_ref, lead_w3_ref, lead_ref, sent_ref):
     peers = got_ref.shape[0]
     rows = got_ref.shape[1] - 8
     partial = got_ref[0, rows:, :].astype(F32)
@@ -228,18 +263,32 @@
         match = [jnp.where(column == map_ref[h : h + 1, :], 1.0 if h == g else 2.0, 0.0) for h in range(g, groups)]
         total = jnp.dot(jnp.concatenate(match, axis=1).astype(BF16), values[128 * g :, :], preferred_element_type=F32)
         square = square + jnp.sum((values[128 * g : 128 * g + 128, :].astype(F32) * total).reshape(16, 8, 256), axis=0)
-    last = sum_piece(square)
     lane = iota((8, 128), 1)
-    block = jnp.where(lane == 8, last, whole_sums(partial))
+    block = jnp.where(lane == 8, sum_piece(square), whole_sums(partial))
     block = block + pltpu.roll(block, 1, 0)
-    block = three_parts(block + pltpu.roll(block, 2, 0)).astype(BF16).astype(F32)
-    block = jnp.concatenate([block[3:4, :], block[7:8, :]], axis=0).astype(BF16)
-    for peer in range(sent_ref.shape[0]):
-        sent_ref[peer] = block
-
-
-def finish(got_ref, w1_ref, w3_ref, solution_ref, phi_ref):
-    total = jnp.sum(got_ref[...].astype(F32), axis=0)
+    block = three_parts(block + pltpu.roll(block, 2, 0))
+    block = jnp.concatenate([block[3:4, :], block[7:8, :]], axis=0)
+    span = 64
+    here = (iota((2, 128), 1) == 64 + row_index()) & (iota((2, 128), 0) == 0)
+    for k in range(places_ref.shape[1]):
+        place = places_ref[1, k]
+        label = (place % span + 1).astype(F32) * lead_ref[k : k + 1, :]
+        second = block + jnp.where(here, label, 0.0)
+        whole = jnp.concatenate([lead_w3_ref[2 * k : 2 * k + 2, :], second], axis=0)
+        sent_ref[place // span] = whole.astype(BF16)
+
+
+def finish(got_ref, w1_ref, solution_ref, phi_ref, wide):
+    wide[...] = got_ref[...].astype(F32)
+    peers = got_ref.shape[0] // 4
+    parts = [wide[pl.ds(i, peers, stride=4), :] for i in range(4)]
+    total = jnp.concatenate([jnp.sum(parts[i], axis=0, keepdims=True) for i in (2, 3)], axis=0)
+    half = w1_ref.shape[0]
+    labels = pltpu.roll(jnp.broadcast_to(total[0:1, :], (half, 128)), 64, 1)
+    match = (labels == (iota((half, 128), 0) + 1).astype(F32)) & (iota((half, 128), 1) < peers)
+    values = jnp.concatenate(parts[0:2], axis=1)
+    values = jnp.concatenate([values, jnp.zeros((128 - peers, 256), F32)], axis=0).astype(BF16)
+    w3 = jnp.dot(match.astype(F32).astype(BF16), values, preferred_element_type=F32)
     first = iota((8, 128), 0) < 4
     sums = whole_sums(jnp.where(first, total[0:1, :], total[1:2, :]))
 
@@ -284,11 +333,10 @@
     k3 = share2 * y3 / alpha2
 
     phi_ref[...] = jnp.where(iota((1, 128), 1) == 0, phi_bar2[0:1, :], phi_bar2[4:5, :])[:, 0:2]
-    half = w1_ref.shape[0]
     for r in range(2):
-        w1 = w1_ref[:, 128 * r : 128 * r + 128].astype(F32)
-        w3 = w3_ref[:, 128 * r : 128 * r + 128].astype(F32)
-        solution_ref[pl.ds(r, half, stride=2), :] = w1 * k1[4 * r : 4 * r + 1, :] + w3 * k3[4 * r : 4 * r + 1, :]
+        lanes = slice(128 * r, 128 * r + 128)
+        scale1, scale3 = k1[4 * r : 4 * r + 1, :], k3[4 * r : 4 * r + 1, :]
+        solution_ref[pl.ds(r, half, stride=2), :] = w1_ref[:, lanes].astype(F32) * scale1 + w3[:, lanes] * scale3
 
 
 def struct(shape, dtype):
@@ -321,60 +369,68 @@
         return lax.all_gather(exchange(sent, "y"), "core", axis=0, tiled=True)
 
     wide = pltpu.VMEM((rows, 128), F32)
-    keys = pltpu.VMEM((slots + span, 128), F32)
-    two = [SMEM, SMEM]
     piece = struct((span, 256), BF16)
     own = struct((rows, 128), BF16)
+    own_wide = struct((rows, 128), F32)
+    slot_table = struct((slots, 128), F32)
+    lane_table = struct((8, 128), BF16)
     tile = tiles[0, 0]
-    sent, u0 = call(
+    sent, u0, slot_v, slot_u, lane_v, lane_u = call(
         begin,
-        [VMEM],
-        [struct((chips, 2 * span, 128), BF16), piece],
+        [SMEM, SMEM, VMEM],
+        [struct((chips, 2 * span, 128), BF16), piece, slot_table, slot_table, lane_table, lane_table],
         [pltpu.VMEM((2 * span, 128), F32)],
-        rhs,
+        places, counts, rhs,
     )
     u_group = exchange_col(sent).reshape(n_col * span, 2, 128)
     sent, own_u = call(
         first_adjoint,
-        two + [VMEM] * 2,
+        [SMEM, SMEM] + [VMEM] * 3,
         [struct((n_row, rows + 8, 128), BF16), own],
         [wide, wide],
-        places, counts, u_group, tile,
-    )
-    sent, w1, v_map = call(
+        places, counts, lane_v, u_group, tile,
+    )
+    sent, own_w1, w1, v_map = call(
         first_forward,
-        two + [VMEM] * 2,
-        [struct((chips, rows + 8, 128), BF16), piece, struct((n_row // 4, 128), F32)],
-        [keys, wide, wide],
-        places, counts, exchange(sent, ROW), tile,
+        [VMEM] * 4,
+        [struct((chips, rows + 8, 128), BF16), own, piece, struct((n_row // 4, 128), F32)],
+        [wide, wide],
+        slot_v, lane_u, exchange(sent, ROW), tile,
     )
     sent, own_w2, w2, u_map = call(
         second_adjoint,
-        two + [VMEM] * 2,
-        [struct((n_row, rows, 128), BF16), own, piece, struct((n_col // 4, 128), F32)],
-        [keys, wide, wide],
-        places, counts, exchange_col(sent), tile,
-    )
-    sent, w3 = call(
+        [VMEM] * 4,
+        [struct((lax.axis_size("z"), rows + 8, 128), BF16), own, piece, struct((n_col // 4, 128), F32)],
+        [wide, wide],
+        slot_u, lane_v, exchange_col(sent), tile,
+    )
+    (sent,) = call(
+        regroup,
+        [VMEM] * 2,
+        [struct((lax.axis_size("x"), rows, 128), BF16)],
+        [pltpu.VMEM((lax.axis_size("z") // 4, 128), F32)],
+        v_map, exchange(sent, "z"),
+    )
+    sent, lead_w3, lead = call(
         second_forward,
-        two + [VMEM] * 8,
-        [struct((chips, rows + 8, 128), BF16), piece],
-        [keys, wide, wide],
-        places, counts, exchange(sent, ROW), tile, v_map, w1, w2, u0, own_w2, own_u,
+        [VMEM] * 9,
+        [struct((chips, rows + 8, 128), BF16), own_wide, slot_table],
+        [wide, wide],
+        slot_v, v_map, exchange(sent, "x"), tile, own_w1, w2, u0, own_w2, own_u,
     )
     (sent,) = call(
         gather_sums,
-        [VMEM] * 2,
-        [struct((n_row, 2, 128), BF16)],
+        [SMEM] + [VMEM] * 4,
+        [struct((n_row, 4, 128), BF16)],
         [],
-        exchange_col(sent), u_map,
+        places, exchange_col(sent), u_map, lead_w3, lead,
     )
     result, phi_bar = call(
         finish,
-        [VMEM] * 3,
+        [VMEM] * 2,
         [struct((2 * span, 128), F32), struct((1, 2), F32)],
-        [],
-        exchange(sent, ROW), w1, w3,
+        [pltpu.VMEM((n_row * 4, 128), F32)],
+        exchange(sent, ROW).reshape(n_row * 4, 128), w1,
     )
     result = result.reshape(span, 2, 128).transpose(1, 0, 2).reshape(2, span * 128)
     return (result, phi_bar.reshape(2))

time: 127 us -> 125 us (0.984)
  blocking collectives: 100 us -> 115 us
  waiting for transfers between devices: 8.76 us -> 0 us
  starting transfers between devices: 7.65 us -> 0 us
  Pallas kernels: 6.95 us -> 5.68 us
    all_to_all x5 -> x7, blocking collectives: 84.8 us -> 98.7 us  [exchange(): return lax.all_to_all(sent, axis, split_axis=0, concat_axis=0, tiled=True)]
    all_to_all x1 -> x0, waiting for transfers between devices: 8.76 us -> none  [exchange(): return lax.all_to_all(sent, axis, split_axis=0, concat_axis=0, tiled=True)]
    all_to_all x1 -> x0, starting transfers between devices: 7.65 us -> none  [exchange(): return lax.all_to_all(sent, axis, split_axis=0, concat_axis=0, tiled=True)]
    pallas_call x7 -> x8, Pallas kernels: 6.95 us -> 5.68 us  [call(): pl.pallas_call(body, out_shape=outs, in_specs=specs, out_specs=[VMEM] * l...]
  transfers between devices with their start and end apart: 1 -> 0, of which waited for: 1 -> 0; matrix products, arithmetic and copies ran while one was open for 0% -> 0% of each run, Pallas kernels for 0% -> 0%
where the time goes in v3:
time: 125 us; the launch traced here: 124 us
  blocking collectives  115 us (92%)
  Pallas kernels  5.68 us (5%)
  local copies, waits for them, and re-layouts  2.19 us (2%)
  between operations  1.42 us (1%)
    all_to_all x7, blocking collectives, exchange(): return lax.all_to_all(sent, axis, split_axis=0, concat_axis=0, tiled=True)  98.7 us
    all_gather x3, blocking collectives, exchange_col(): return lax.all_gather(exchange(sent, 'y'), 'core', axis=0, tiled=True)  16.2 us
    pallas_call x8, Pallas kernels, call(): pl.pallas_call(body, out_shape=outs, in_specs=specs, out_specs=[VMEM] * l...  5.68 us

profile of v3, /device:TPU:1, one launch (start us, length us, event | category | flops | bytes accessed | tf_op | source)
XLA Modules:
  0.0 124.2 jit_solution(5332367813638198591)
XLA Ops:
  0.6 0.0 copy-start
  1.4 0.0 copy-start.1
  1.4 0.8 copy-done.1
  2.2 0.0 copy-start.2
  2.2 0.7 copy-done.2
  2.9 0.7 shard_map.59
  3.6 16.7 %all_to_all.35 = bf16[8,128,128]{2,1,0:T(8,128)(2,1)S(1)} all-to-all(bf16[8,128,128]{2,1,0:T(8,128)(2,1)S(1)} %get-tuple-element.26), channel_id=1, replica_groups=mesh['z'=8,'x'=4,'y'=8,'core'=2] {'y'}, dimensions={0} | all-to-all | bytes 524288 | tf_op jit(solution)/shard_map/all_to_all | solution.py:366
  20.3 5.3 %all_gather.9 = bf16[16,128,128]{2,1,0:T(8,128)(2,1)S(1)} all-gather(bf16[8,128,128]{2,1,0:T(8,128)(2,1)S(1)} %all_to_all.35), channel_id=1, replica_groups=mesh['z'=8,'x'=4,'y'=8,'core'=2] {'core'}, dimensions={0}, use_global_device_ids=true | all-gather | bytes 786432 | tf_op jit(solution)/shard_map/all_gather | solution.py:369
  25.6 0.0 copy-done
  25.6 1.1 shard_map.60
  26.8 30.3 %all_to_all.36.got_ref = bf16[32,72,128]{2,1,0:T(8,128)(2,1)S(1)} all-to-all(bf16[32,72,128]{2,1,0:T(8,128)(2,1)S(1)} %get-tuple-element.27), channel_id=1, replica_groups=mesh['z'=8,'x'=4,'y'=8,'core'=2] {'z','x'}, dimensions={0} | all-to-all | bytes 1179648 | tf_op jit(solution)/shard_map/all_to_all | solution.py:366
  57.1 0.7 shard_map.61
  57.8 10.6 %all_to_all.37 = bf16[8,72,128]{2,1,0:T(8,128)(2,1)S(1)} all-to-all(bf16[8,72,128]{2,1,0:T(8,128)(2,1)S(1)} %get-tuple-element.30), channel_id=1, replica_groups=mesh['z'=8,'x'=4,'y'=8,'core'=2] {'y'}, dimensions={0} | all-to-all | bytes 294912 | tf_op jit(solution)/shard_map/all_to_all | solution.py:366
  68.4 5.0 %all_gather.10.got_ref = bf16[16,72,128]{2,1,0:T(8,128)(2,1)S(1)} all-gather(bf16[8,72,128]{2,1,0:T(8,128)(2,1)S(1)} %all_to_all.37), channel_id=1, replica_groups=mesh['z'=8,'x'=4,'y'=8,'core'=2] {'core'}, dimensions={0}, use_global_device_ids=true | all-gather | bytes 442368 | tf_op jit(solution)/shard_map/all_gather | solution.py:369
  73.4 0.5 shard_map.62
  73.9 11.1 %all_to_all.38.got_ref = bf16[8,72,128]{2,1,0:T(8,128)(2,1)S(1)} all-to-all(bf16[8,72,128]{2,1,0:T(8,128)(2,1)S(1)} %get-tuple-element.31), channel_id=1, replica_groups=mesh['z'=8,'x'=4,'y'=8,'core'=2] {'z'}, dimensions={0} | all-to-all | bytes 294912 | tf_op jit(solution)/shard_map/all_to_all | solution.py:366
  85.0 0.2 shard_map.63
  85.3 7.8 %all_to_all.39.got_ref = bf16[4,64,128]{2,1,0:T(8,128)(2,1)S(1)} all-to-all(bf16[4,64,128]{2,1,0:T(8,128)(2,1)S(1)} %shard_map.63), channel_id=1, replica_groups=mesh['z'=8,'x'=4,'y'=8,'core'=2] {'x'}, dimensions={0} | all-to-all | bytes 131072 | tf_op jit(solution)/shard_map/all_to_all | solution.py:366
  93.0 0.6 shard_map.64
  93.6 10.5 %all_to_all.40 = bf16[8,72,128]{2,1,0:T(8,128)(2,1)S(1)} all-to-all(bf16[8,72,128]{2,1,0:T(8,128)(2,1)S(1)} %get-tuple-element.37), channel_id=1, replica_groups=mesh['z'=8,'x'=4,'y'=8,'core'=2] {'y'}, dimensions={0} | all-to-all | bytes 294912 | tf_op jit(solution)/shard_map/all_to_all | solution.py:366
  104.1 5.8 %all_gather.11.got_ref = bf16[16,72,128]{2,1,0:T(8,128)(2,1)S(1)} all-gather(bf16[8,72,128]{2,1,0:T(8,128)(2,1)S(1)} %all_to_all.40), channel_id=1, replica_groups=mesh['z'=8,'x'=4,'y'=8,'core'=2] {'core'}, dimensions={0}, use_global_device_ids=true | all-gather | bytes 442368 | tf_op jit(solution)/shard_map/all_gather | solution.py:369
  109.9 0.0 copy-start.3
  109.9 0.7 copy-done.3
  110.6 1.1 shard_map.65
  111.6 11.7 %all_to_all.41 = bf16[32,4,128]{2,1,0:T(4,128)(2,1)S(1)} all-to-all(bf16[32,4,128]{2,1,0:T(4,128)(2,1)S(1)} %shard_map.65), channel_id=1, replica_groups=mesh['z'=8,'x'=4,'y'=8,'core'=2] {'z','x'}, dimensions={0} | all-to-all | bytes 65536 | tf_op jit(solution)/shard_map/all_to_all | solution.py:366
  123.3 0.9 shard_map.66
Async XLA Ops:
  0.6 25.0 %copy-start = (bf16[1,1,32,128,128]{4,3,2,1,0:T(8,128)(2,1)S(1)}, bf16[1,1,32,128,128]{4,3,2,1,0:T(8,128)(2,1)}, u32[]{:S(2)}) copy-start(bf16[1,1,32,128,128]{4,3,2,1,0:T(8,128)(2,1)} %param.4) | copy-start | bytes 3145732
  1.4 0.8 copy-start.1
  2.2 0.7 copy-start.2
  109.9 0.7 copy-start.3

commit v4 on v3

--- a/solution.py
+++ b/solution.py
@@ -1,3 +1,5 @@
+import functools
+
 import jax
 import jax.numpy as jnp
 from jax import lax
@@ -108,28 +110,30 @@
             sent_ref[peer, rows:, :] = extra
 
 
-def begin(places_ref, counts_ref, rhs_ref, sent_ref, piece_ref, slot_v_ref, slot_u_ref, lane_v_ref, lane_u_ref, rows):
+def begin(rhs_ref, sent_ref, piece_ref, rows):
     for b in range(rows.shape[0] // 2):
         rows[2 * b : 2 * b + 2, :] = rhs_ref[:, 128 * b : 128 * b + 128]
     send_all(sent_ref, rows[...].astype(BF16), None)
     half = rows.shape[0] // 2
     piece_ref[...] = jnp.concatenate([rows[pl.ds(r, half, stride=2), :] for r in range(2)], axis=1).astype(BF16)
+
+
+def tables(places_ref, counts_ref, slot_v_ref, slot_u_ref, lane_v_ref, lane_u_ref, fetch_ref, spans):
     count = counts_ref[0, 0]
     for axis, slot_ref, lane_ref in ((0, slot_u_ref, lane_u_ref), (1, slot_v_ref, lane_v_ref)):
         slot_ref[...] = slot_keys(places_ref, count, axis)
         lane_ref[...] = lane_keys(places_ref, count, axis)
-
-
-def first_adjoint(places_ref, counts_ref, lane_ref, u_ref, tile_ref, sent_ref, own_u_ref, held, out):
-    count = counts_ref[0, 0]
-    cores = lax.axis_size("core")
-    chips = lax.axis_size("y")
-    span = u_ref.shape[0] // (cores * chips)
+    span, chips, cores = spans
     for k in range(places_ref.shape[1]):
         block = places_ref[0, k]
         owner = block // span
-        row = ((owner % cores) * chips + owner // cores) * span + block % span
-        held[2 * k : 2 * k + 2, :] = u_ref[row].astype(F32) * (k < count).astype(F32)
+        fetch_ref[0, k] = ((owner % cores) * chips + owner // cores) * span + block % span
+        fetch_ref[1, k] = (k < count).astype(jnp.int32)
+
+
+def first_adjoint(fetch_ref, lane_ref, u_ref, tile_ref, sent_ref, own_u_ref, held, out):
+    for k in range(fetch_ref.shape[1]):
+        held[2 * k : 2 * k + 2, :] = u_ref[fetch_ref[0, k]].astype(F32) * fetch_ref[1, k].astype(F32)
     own_u_ref[...] = split_rows(held).astype(BF16)
     products(held, tile_ref, out, True)
     send_all(sent_ref, split_rows(out).astype(BF16), lane_ref[...])
@@ -226,8 +230,7 @@
     lead_ref[...] = lead
     lead = jnp.concatenate([lead, lead], axis=0)
     lead_w3 = w3 * lead
-    for r in range(2):
-        lead_w3_ref[pl.ds(r, half, stride=2), :] = lead_w3[half * r : half * r + half, :]
+    lead_w3_ref[...] = lead_w3.astype(BF16)
     w1 = own_w1_ref[...].astype(F32)
     w2 = w2_ref[...].astype(F32)
     u0 = u0_ref[...].astype(F32)
@@ -249,7 +252,7 @@
     send_all(sent_ref, sent, three_parts(block).astype(BF16))
 
 
-def gather_sums(places_ref, got_ref, map_ref, lead_w3_ref, lead_ref, sent_ref):
+def gather_sums(got_ref, map_ref, lane_ref, slot_ref, lead_w3_ref, lead_ref, sent_ref, wide, span):
     peers = got_ref.shape[0]
     rows = got_ref.shape[1] - 8
     partial = got_ref[0, rows:, :].astype(F32)
@@ -267,15 +270,21 @@
     block = jnp.where(lane == 8, sum_piece(square), whole_sums(partial))
     block = block + pltpu.roll(block, 1, 0)
     block = three_parts(block + pltpu.roll(block, 2, 0))
-    block = jnp.concatenate([block[3:4, :], block[7:8, :]], axis=0)
-    span = 64
-    here = (iota((2, 128), 1) == 64 + row_index()) & (iota((2, 128), 0) == 0)
-    for k in range(places_ref.shape[1]):
-        place = places_ref[1, k]
-        label = (place % span + 1).astype(F32) * lead_ref[k : k + 1, :]
-        second = block + jnp.where(here, label, 0.0)
-        whole = jnp.concatenate([lead_w3_ref[2 * k : 2 * k + 2, :], second], axis=0)
-        sent_ref[place // span] = whole.astype(BF16)
+    owners = sent_ref.shape[0] // 4
+    slots = slot_ref.shape[0]
+    keys = slot_ref[...]
+    label = (keys - span * jnp.floor(keys * (1.0 / span)) + 1.0) * lead_ref[...]
+    here = iota((slots, 128), 1) == 64 + row_index()
+    values = [lead_w3_ref[0:slots, :], lead_w3_ref[slots:, :], jnp.where(here, label, 0.0).astype(BF16)]
+    values = jnp.concatenate(values, axis=1)
+    values = jnp.concatenate([values, jnp.zeros((128 - slots, 384), BF16)], axis=0)
+    match = (iota((owners, 128), 0) == lane_ref[...].astype(jnp.int32)[0:1, :]) & (iota((owners, 128), 1) < slots)
+    placed = jnp.dot(match.astype(F32).astype(BF16), values, preferred_element_type=F32)
+    wide[pl.ds(0, owners, stride=4), :] = placed[:, 0:128]
+    wide[pl.ds(1, owners, stride=4), :] = placed[:, 128:256]
+    wide[pl.ds(2, owners, stride=4), :] = placed[:, 256:384] + block[3:4, :]
+    wide[pl.ds(3, owners, stride=4), :] = jnp.broadcast_to(block[7:8, :], (owners, 128))
+    sent_ref[...] = wide[...].astype(BF16)
 
 
 def finish(got_ref, w1_ref, solution_ref, phi_ref, wide):
@@ -352,12 +361,12 @@
     span = rhs.shape[1] // 128
     places = coords[0, 0].T
 
-    def call(body, specs, outs, scratch, *operands):
+    def call(body, specs, outs, scratch, *operands, out_specs=None):
         return pl.pallas_call(
             body,
             out_shape=outs,
             in_specs=specs,
-            out_specs=[VMEM] * len(outs),
+            out_specs=[VMEM] * len(outs) if out_specs is None else out_specs,
             scratch_shapes=scratch,
             compiler_params=pltpu.CompilerParams(vmem_limit_bytes=32 * 1024 * 1024),
         )(*operands)
@@ -371,24 +380,31 @@
     wide = pltpu.VMEM((rows, 128), F32)
     piece = struct((span, 256), BF16)
     own = struct((rows, 128), BF16)
-    own_wide = struct((rows, 128), F32)
     slot_table = struct((slots, 128), F32)
     lane_table = struct((8, 128), BF16)
     tile = tiles[0, 0]
-    sent, u0, slot_v, slot_u, lane_v, lane_u = call(
+    sent, u0 = call(
         begin,
-        [SMEM, SMEM, VMEM],
-        [struct((chips, 2 * span, 128), BF16), piece, slot_table, slot_table, lane_table, lane_table],
+        [VMEM],
+        [struct((chips, 2 * span, 128), BF16), piece],
         [pltpu.VMEM((2 * span, 128), F32)],
-        places, counts, rhs,
+        rhs,
+    )
+    slot_v, slot_u, lane_v, lane_u, fetch = call(
+        functools.partial(tables, spans=(span, chips, lax.axis_size("core"))),
+        [SMEM, SMEM],
+        [slot_table, slot_table, lane_table, lane_table, struct((2, slots), jnp.int32)],
+        [],
+        places, counts,
+        out_specs=[VMEM] * 4 + [SMEM],
     )
     u_group = exchange_col(sent).reshape(n_col * span, 2, 128)
     sent, own_u = call(
         first_adjoint,
-        [SMEM, SMEM] + [VMEM] * 3,
+        [SMEM] + [VMEM] * 3,
         [struct((n_row, rows + 8, 128), BF16), own],
         [wide, wide],
-        places, counts, lane_v, u_group, tile,
+        fetch, lane_v, u_group, tile,
     )
     sent, own_w1, w1, v_map = call(
         first_forward,
@@ -414,23 +430,23 @@
     sent, lead_w3, lead = call(
         second_forward,
         [VMEM] * 9,
-        [struct((chips, rows + 8, 128), BF16), own_wide, slot_table],
+        [struct((chips, rows + 8, 128), BF16), own, slot_table],
         [wide, wide],
         slot_v, v_map, exchange(sent, "x"), tile, own_w1, w2, u0, own_w2, own_u,
     )
     (sent,) = call(
-        gather_sums,
-        [SMEM] + [VMEM] * 4,
-        [struct((n_row, 4, 128), BF16)],
-        [],
-        places, exchange_col(sent), u_map, lead_w3, lead,
+        functools.partial(gather_sums, span=span),
+        [VMEM] * 6,
+        [struct((n_row * 4, 128), BF16)],
+        [pltpu.VMEM((n_row * 4, 128), F32)],
+        exchange_col(sent), u_map, lane_v, slot_v, lead_w3, lead,
     )
     result, phi_bar = call(
         finish,
         [VMEM] * 2,
         [struct((2 * span, 128), F32), struct((1, 2), F32)],
         [pltpu.VMEM((n_row * 4, 128), F32)],
-        exchange(sent, ROW).reshape(n_row * 4, 128), w1,
+        exchange(sent.reshape(n_row, 4, 128), ROW).reshape(n_row * 4, 128), w1,
     )
     result = result.reshape(span, 2, 128).transpose(1, 0, 2).reshape(2, span * 128)
     return (result, phi_bar.reshape(2))

time: 125 us -> 122 us (0.976)
  blocking collectives: 115 us -> 98.1 us
  starting transfers between devices: 0 us -> 7.65 us
  waiting for transfers between devices: 0 us -> 6.42 us
    all_to_all x7 -> x6, blocking collectives: 98.7 us -> 81.8 us  [exchange(): return lax.all_to_all(sent, axis, split_axis=0, concat_axis=0, tiled=True)]
    all_to_all x0 -> x1, starting transfers between devices: none -> 7.65 us  [exchange(): return lax.all_to_all(sent, axis, split_axis=0, concat_axis=0, tiled=True)]
    all_to_all x0 -> x1, waiting for transfers between devices: none -> 6.42 us  [exchange(): return lax.all_to_all(sent, axis, split_axis=0, concat_axis=0, tiled=True)]
    pallas_call x8 -> x9, Pallas kernels: 5.68 us -> 6.55 us  [call(): pl.pallas_call(body, out_shape=outs, in_specs=specs, out_specs=[VMEM] * l...]
  transfers between devices with their start and end apart: 0 -> 1, of which waited for: 0 -> 1; matrix products, arithmetic and copies ran while one was open for 0% -> 0% of each run, Pallas kernels for 0% -> 1%
where the time goes in v4:
time: 122 us
  blocking collectives  98.1 us (80%)
  starting transfers between devices  7.65 us (6%)
  Pallas kernels  6.55 us (5%)
  waiting for transfers between devices  6.42 us (5%)
  local copies, waits for them, and re-layouts  1.51 us (1%)
  between operations  1.33 us (1%)
    all_to_all x6, blocking collectives, exchange(): return lax.all_to_all(sent, axis, split_axis=0, concat_axis=0, tiled=True)  81.8 us
    all_gather x3, blocking collectives, exchange_col(): return lax.all_gather(exchange(sent, 'y'), 'core', axis=0, tiled=True)  16.3 us
    all_to_all x1, starting transfers between devices, exchange(): return lax.all_to_all(sent, axis, split_axis=0, concat_axis=0, tiled=True)  7.65 us
    pallas_call x9, Pallas kernels, call(): pl.pallas_call(body, out_shape=outs, in_specs=specs, out_specs=[VMEM] * l...  6.55 us
    all_to_all x1, waiting for transfers between devices, exchange(): return lax.all_to_all(sent, axis, split_axis=0, concat_axis=0, tiled=True)  6.42 us
  transfers between devices with their start and end apart: 1, of which 1 were waited for; matrix products, arithmetic and copies ran while one was open for 0% of the time, Pallas kernels for 1%

profile of v4, /device:TPU:1, one launch (start us, length us, event | category | flops | bytes accessed | tf_op | source)
XLA Modules:
  0.0 121.5 jit_solution(7744539297679534319)
XLA Ops:
  0.6 0.0 copy-start.1
  0.6 0.8 copy-done.1
  1.5 0.0 copy-start
  1.5 0.7 shard_map.60
  2.2 7.7 %all-to-all-start = ((bf16[8,128,128]{2,1,0:T(8,128)(2,1)}), bf16[8,128,128]{2,1,0:T(8,128)(2,1)S(1)}, u32[]{:S(2)}, u32[]{:S(2)}) async-start(bf16[8,128,128]{2,1,0:T(8,128)(2,1)} %get-tuple-element.28), calls=%async_computation | async-start | bytes 524288 | tf_op jit(solution)/shard_map/all_to_all | solution.py:375
  10.5 0.0 copy-start.2
  10.5 0.7 copy-done.2
  11.2 1.7 %shard_map.59 = (f32[32,128]{1,0:T(8,128)S(1)}, f32[32,128]{1,0:T(8,128)S(1)}, bf16[8,128]{1,0:T(8,128)(2,1)S(1)}, bf16[8,128]{1,0:T(8,128)(2,1)S(1)}, s32[2,32]{1,0:T(2,128)S(1)}) custom-call(s32[2,32]{1,0:T(2,128)S(1)} %bitcast.20, s32[1,1]{1,0:T(1,128)S(6)} %copy.8.counts_ref), custom_call_target="tpu_custom_call" | custom-call | tf_op jit(solution)/shard_map/pallas_call | solution.py:365
  12.9 6.4 %all-to-all-done = bf16[8,128,128]{2,1,0:T(8,128)(2,1)S(1)} async-done(((bf16[8,128,128]{2,1,0:T(8,128)(2,1)}), bf16[8,128,128]{2,1,0:T(8,128)(2,1)S(1)}, u32[]{:S(2)}, u32[]{:S(2)}) %all-to-all-start) | async-done | bytes 262176 | tf_op jit(solution)/shard_map/all_to_all | solution.py:375
  19.3 5.4 %all_gather.9 = bf16[16,128,128]{2,1,0:T(8,128)(2,1)S(1)} all-gather(bf16[8,128,128]{2,1,0:T(8,128)(2,1)S(1)} %all-to-all-done), channel_id=1, replica_groups=mesh['z'=8,'x'=4,'y'=8,'core'=2] {'core'}, dimensions={0}, use_global_device_ids=true | all-gather | bytes 786432 | tf_op jit(solution)/shard_map/all_gather | solution.py:378
  24.7 0.0 copy-done
  24.7 0.8 shard_map.61
  25.5 30.1 %all_to_all.35.got_ref = bf16[32,72,128]{2,1,0:T(8,128)(2,1)S(1)} all-to-all(bf16[32,72,128]{2,1,0:T(8,128)(2,1)S(1)} %get-tuple-element.29), channel_id=1, replica_groups=mesh['z'=8,'x'=4,'y'=8,'core'=2] {'z','x'}, dimensions={0} | all-to-all | bytes 1179648 | tf_op jit(solution)/shard_map/all_to_all | solution.py:375
  55.6 0.7 shard_map.62
  56.3 10.6 %all_to_all.36 = bf16[8,72,128]{2,1,0:T(8,128)(2,1)S(1)} all-to-all(bf16[8,72,128]{2,1,0:T(8,128)(2,1)S(1)} %get-tuple-element.32), channel_id=1, replica_groups=mesh['z'=8,'x'=4,'y'=8,'core'=2] {'y'}, dimensions={0} | all-to-all | bytes 294912 | tf_op jit(solution)/shard_map/all_to_all | solution.py:375
  66.9 5.0 %all_gather.10.got_ref = bf16[16,72,128]{2,1,0:T(8,128)(2,1)S(1)} all-gather(bf16[8,72,128]{2,1,0:T(8,128)(2,1)S(1)} %all_to_all.36), channel_id=1, replica_groups=mesh['z'=8,'x'=4,'y'=8,'core'=2] {'core'}, dimensions={0}, use_global_device_ids=true | all-gather | bytes 442368 | tf_op jit(solution)/shard_map/all_gather | solution.py:378
  72.0 0.5 shard_map.63
  72.4 11.1 %all_to_all.37.got_ref = bf16[8,72,128]{2,1,0:T(8,128)(2,1)S(1)} all-to-all(bf16[8,72,128]{2,1,0:T(8,128)(2,1)S(1)} %get-tuple-element.33), channel_id=1, replica_groups=mesh['z'=8,'x'=4,'y'=8,'core'=2] {'z'}, dimensions={0} | all-to-all | bytes 294912 | tf_op jit(solution)/shard_map/all_to_all | solution.py:375
  83.6 0.2 shard_map.64
  83.8 7.8 %all_to_all.38.got_ref = bf16[4,64,128]{2,1,0:T(8,128)(2,1)S(1)} all-to-all(bf16[4,64,128]{2,1,0:T(8,128)(2,1)S(1)} %shard_map.64), channel_id=1, replica_groups=mesh['z'=8,'x'=4,'y'=8,'core'=2] {'x'}, dimensions={0} | all-to-all | bytes 131072 | tf_op jit(solution)/shard_map/all_to_all | solution.py:375
  91.6 0.6 shard_map.65
  92.1 10.5 %all_to_all.39 = bf16[8,72,128]{2,1,0:T(8,128)(2,1)S(1)} all-to-all(bf16[8,72,128]{2,1,0:T(8,128)(2,1)S(1)} %get-tuple-element.39), channel_id=1, replica_groups=mesh['z'=8,'x'=4,'y'=8,'core'=2] {'y'}, dimensions={0} | all-to-all | bytes 294912 | tf_op jit(solution)/shard_map/all_to_all | solution.py:375
  102.7 5.8 %all_gather.11.got_ref = bf16[16,72,128]{2,1,0:T(8,128)(2,1)S(1)} all-gather(bf16[8,72,128]{2,1,0:T(8,128)(2,1)S(1)} %all_to_all.39), channel_id=1, replica_groups=mesh['z'=8,'x'=4,'y'=8,'core'=2] {'core'}, dimensions={0}, use_global_device_ids=true | all-gather | bytes 442368 | tf_op jit(solution)/shard_map/all_gather | solution.py:378
  108.5 0.5 shard_map.66
  108.9 11.7 %all_to_all.40 = bf16[32,4,128]{2,1,0:T(4,128)(2,1)S(1)} all-to-all(bf16[32,4,128]{2,1,0:T(4,128)(2,1)S(1)} %bitcast.18), channel_id=1, replica_groups=mesh['z'=8,'x'=4,'y'=8,'core'=2] {'z','x'}, dimensions={0} | all-to-all | bytes 65536 | tf_op jit(solution)/shard_map/all_to_all | solution.py:375
  120.6 0.9 shard_map.67
Async XLA Ops:
  0.6 0.8 copy-start.1
  1.5 23.2 %copy-start = (bf16[1,1,32,128,128]{4,3,2,1,0:T(8,128)(2,1)S(1)}, bf16[1,1,32,128,128]{4,3,2,1,0:T(8,128)(2,1)}, u32[]{:S(2)}) copy-start(bf16[1,1,32,128,128]{4,3,2,1,0:T(8,128)(2,1)} %param.4) | copy-start | bytes 3145732
  2.2 17.1 %all-to-all-start = ((bf16[8,128,128]{2,1,0:T(8,128)(2,1)}), bf16[8,128,128]{2,1,0:T(8,128)(2,1)S(1)}, u32[]{:S(2)}, u32[]{:S(2)}) async-start(bf16[8,128,128]{2,1,0:T(8,128)(2,1)} %get-tuple-element.28), calls=%async_computation | async-start | bytes 524288 | tf_op jit(solution)/shard_map/all_to_all | solution.py:375
  10.5 0.7 copy-start.2

commit v5 on v4

--- a/solution.py
+++ b/solution.py
@@ -110,15 +110,12 @@
             sent_ref[peer, rows:, :] = extra
 
 
-def begin(rhs_ref, sent_ref, piece_ref, rows):
-    for b in range(rows.shape[0] // 2):
-        rows[2 * b : 2 * b + 2, :] = rhs_ref[:, 128 * b : 128 * b + 128]
-    send_all(sent_ref, rows[...].astype(BF16), None)
+def tables(
+    places_ref, counts_ref, piece_ref, slot_v_ref, slot_u_ref, lane_v_ref, lane_u_ref, u0_ref, fetch_ref, rows, spans
+):
+    rows[...] = piece_ref[...].astype(F32)
     half = rows.shape[0] // 2
-    piece_ref[...] = jnp.concatenate([rows[pl.ds(r, half, stride=2), :] for r in range(2)], axis=1).astype(BF16)
-
-
-def tables(places_ref, counts_ref, slot_v_ref, slot_u_ref, lane_v_ref, lane_u_ref, fetch_ref, spans):
+    u0_ref[...] = jnp.concatenate([rows[pl.ds(r, half, stride=2), :] for r in range(2)], axis=1).astype(BF16)
     count = counts_ref[0, 0]
     for axis, slot_ref, lane_ref in ((0, slot_u_ref, lane_u_ref), (1, slot_v_ref, lane_v_ref)):
         slot_ref[...] = slot_keys(places_ref, count, axis)
@@ -307,39 +304,34 @@
     t11, t13, t33, s00, s02, s22, s24, s04, s44 = [pick(j) for j in range(9)]
 
     def norm(square):
-        return jnp.sqrt(jnp.maximum(square, 0.0) + EPS)
-
-    beta0 = norm(s00)
-    alpha1 = norm(t11 / (beta0 * beta0))
-    x2 = 1.0 / (beta0 * alpha1)
-    x0 = -alpha1 / beta0
-    beta1 = norm(x2 * x2 * s22 + 2.0 * x2 * x0 * s02 + x0 * x0 * s00)
-    y3 = x2 / beta1
-    y1 = x0 / beta1 - beta1 * x2
-    alpha2 = norm(y3 * y3 * t33 + 2.0 * y3 * y1 * t13 + y1 * y1 * t11)
-    ratio = alpha2 / beta1
-    z4 = y3 / alpha2
-    z2 = y1 / alpha2 - ratio * x2
-    z0 = -ratio * x0
-    beta2 = norm(
-        z4 * z4 * s44 + z2 * z2 * s22 + z0 * z0 * s00 + 2.0 * (z4 * z2 * s24 + z4 * z0 * s04 + z2 * z0 * s02)
-    )
-    rho1 = jnp.sqrt(alpha1 * alpha1 + beta1 * beta1)
-    cosine1 = alpha1 / rho1
-    sine1 = beta1 / rho1
-    phi1 = cosine1 * beta0
-    phi_bar1 = sine1 * beta0
-    theta = sine1 * alpha2
-    rho_bar2 = -cosine1 * alpha2
-    rho2 = jnp.sqrt(rho_bar2 * rho_bar2 + beta2 * beta2)
-    cosine2 = rho_bar2 / rho2
-    sine2 = beta2 / rho2
-    phi2 = cosine2 * phi_bar1
-    phi_bar2 = sine2 * phi_bar1
-    share1 = phi1 / rho1
-    share2 = phi2 / rho2
-    k1 = share1 * x2 + share2 * (y1 / alpha2 - (theta / rho1) * x2)
-    k3 = share2 * y3 / alpha2
+        return jnp.maximum(square, 0.0) + EPS
+
+    b0 = norm(s00)
+    ib0 = 1.0 / b0
+    a1 = norm(t11 * ib0)
+    x22 = ib0 / a1
+    x20 = -ib0
+    x00 = a1 * ib0
+    b1 = norm(x22 * s22 + 2.0 * x20 * s02 + x00 * s00)
+    ib1 = 1.0 / b1
+    y33 = x22 * ib1
+    y31 = x20 * ib1 - x22
+    y11 = x00 * ib1 - 2.0 * x20 + b1 * x22
+    a2 = norm(y33 * t33 + 2.0 * y31 * t13 + y11 * t11)
+    ia2 = 1.0 / a2
+    ratio = a2 * ib1
+    z44 = y33 * ia2
+    z22 = y11 * ia2 - 2.0 * y31 + ratio * x22
+    z00 = ratio * x00
+    z42 = y31 * ia2 - y33
+    z40 = -x20 * ib1
+    z20 = x20 + (a2 * x20 - x00) * ib1
+    b2 = norm(z44 * s44 + z22 * s22 + z00 * s00 + 2.0 * (z42 * s24 + z40 * s04 + z20 * s02))
+    ir1 = 1.0 / (a1 + b1)
+    ir2 = 1.0 / (a1 * a2 * ir1 + b2)
+    k1 = ir1 + (1.0 + a2 * ir1 * (b1 * ir1)) * ir2
+    k3 = -ir1 * ir2
+    phi_bar2 = jnp.sqrt(b0 * (b1 * ir1) * (b2 * ir2))
 
     phi_ref[...] = jnp.where(iota((1, 128), 1) == 0, phi_bar2[0:1, :], phi_bar2[4:5, :])[:, 0:2]
     for r in range(2):
@@ -383,21 +375,16 @@
     slot_table = struct((slots, 128), F32)
     lane_table = struct((8, 128), BF16)
     tile = tiles[0, 0]
-    sent, u0 = call(
-        begin,
-        [VMEM],
-        [struct((chips, 2 * span, 128), BF16), piece],
+    pairs = rhs.reshape(2, span, 128).transpose(1, 0, 2).reshape(2 * span, 128).astype(BF16)
+    slot_v, slot_u, lane_v, lane_u, u0, fetch = call(
+        functools.partial(tables, spans=(span, chips, lax.axis_size("core"))),
+        [SMEM, SMEM, VMEM],
+        [slot_table, slot_table, lane_table, lane_table, piece, struct((2, slots), jnp.int32)],
         [pltpu.VMEM((2 * span, 128), F32)],
-        rhs,
-    )
-    slot_v, slot_u, lane_v, lane_u, fetch = call(
-        functools.partial(tables, spans=(span, chips, lax.axis_size("core"))),
-        [SMEM, SMEM],
-        [slot_table, slot_table, lane_table, lane_table, struct((2, slots), jnp.int32)],
-        [],
-        places, counts,
-        out_specs=[VMEM] * 4 + [SMEM],
-    )
+        places, counts, pairs,
+        out_specs=[VMEM] * 5 + [SMEM],
+    )
+    sent = jnp.broadcast_to(pairs[None], (chips, 2 * span, 128))
     u_group = exchange_col(sent).reshape(n_col * span, 2, 128)
     sent, own_u = call(
         first_adjoint,

time: 122 us -> 122 us (level)
    pallas_call x9 -> x8, Pallas kernels: 6.55 us -> 5.78 us  [call(): pl.pallas_call(body, out_shape=outs, in_specs=specs, out_specs=[VMEM] * l...]
where the time goes in v5:
time: 122 us
  blocking collectives  98.1 us (80%)
  starting transfers between devices  7.65 us (6%)
  waiting for transfers between devices  6.41 us (5%)
  Pallas kernels  5.78 us (5%)
  local copies, waits for them, and re-layouts  1.41 us (1%)
  between operations  1.33 us (1%)
    all_to_all x6, blocking collectives, exchange(): return lax.all_to_all(sent, axis, split_axis=0, concat_axis=0, tiled=True)  81.8 us
    all_gather x3, blocking collectives, exchange_col(): return lax.all_gather(exchange(sent, 'y'), 'core', axis=0, tiled=True)  16.3 us
    all_to_all x1, starting transfers between devices, exchange(): return lax.all_to_all(sent, axis, split_axis=0, concat_axis=0, tiled=True)  7.65 us
    all_to_all x1, waiting for transfers between devices, exchange(): return lax.all_to_all(sent, axis, split_axis=0, concat_axis=0, tiled=True)  6.41 us
    pallas_call x8, Pallas kernels, call(): pl.pallas_call(body, out_shape=outs, in_specs=specs, out_specs=[VMEM] * l...  5.78 us
  transfers between devices with their start and end apart: 1, of which 1 were waited for; matrix products, arithmetic and copies ran while one was open for 0% of the time, Pallas kernels for 1%

profile of v5, /device:TPU:1, one launch (start us, length us, event | category | flops | bytes accessed | tf_op | source)
XLA Modules:
  0.0 121.6 jit_solution(1650719916455812669)
XLA Ops:
  0.6 0.0 copy-start
  0.6 1.0 convert_element_type.9
  1.6 0.7 broadcast_in_dim.2
  2.3 7.7 %all-to-all-start = ((bf16[8,128,128]{2,1,0:T(8,128)(2,1)}), bf16[8,128,128]{2,1,0:T(8,128)(2,1)S(1)}, u32[]{:S(2)}, u32[]{:S(2)}) async-start(bf16[8,128,128]{2,1,0:T(8,128)(2,1)} %broadcast_in_dim.2), calls=%async_computation | async-start | bytes 524288 | tf_op jit(solution)/shard_map/all_to_all | solution.py:367
  10.6 0.0 copy-start.1
  10.6 0.7 copy-done.1
  11.3 1.7 %shard_map.59 = (f32[32,128]{1,0:T(8,128)S(1)}, f32[32,128]{1,0:T(8,128)S(1)}, bf16[8,128]{1,0:T(8,128)(2,1)S(1)}, bf16[8,128]{1,0:T(8,128)(2,1)S(1)}, bf16[64,256]{1,0:T(8,128)(2,1)S(1)}, /*index=5*/s32[2,32]{1,0:T(2,128)S(1)}) custom-call(s32[2,32]{1,0:T(2,128)S(1)} %bitcast.27, s32[1,1]{1,0:T(1,128)S(6)} %copy.10.counts_ref, bf16[128,128]{1,0:T(8,128)(2,1)S(1)} %bitcast.24), custom_call_target="tpu_custom_call" | custom-call | tf_op jit(solution)/shard_map/pallas_call | solution.py:357
  13.0 6.4 %all-to-all-done = bf16[8,128,128]{2,1,0:T(8,128)(2,1)S(1)} async-done(((bf16[8,128,128]{2,1,0:T(8,128)(2,1)}), bf16[8,128,128]{2,1,0:T(8,128)(2,1)S(1)}, u32[]{:S(2)}, u32[]{:S(2)}) %all-to-all-start) | async-done | bytes 262176 | tf_op jit(solution)/shard_map/all_to_all | solution.py:367
  19.4 5.4 %all_gather.9 = bf16[16,128,128]{2,1,0:T(8,128)(2,1)S(1)} all-gather(bf16[8,128,128]{2,1,0:T(8,128)(2,1)S(1)} %all-to-all-done), channel_id=1, replica_groups=mesh['z'=8,'x'=4,'y'=8,'core'=2] {'core'}, dimensions={0}, use_global_device_ids=true | all-gather | bytes 786432 | tf_op jit(solution)/shard_map/all_gather | solution.py:370
  24.8 0.0 copy-done
  24.8 0.8 shard_map.60
  25.7 30.1 %all_to_all.35.got_ref = bf16[32,72,128]{2,1,0:T(8,128)(2,1)S(1)} all-to-all(bf16[32,72,128]{2,1,0:T(8,128)(2,1)S(1)} %get-tuple-element.27), channel_id=1, replica_groups=mesh['z'=8,'x'=4,'y'=8,'core'=2] {'z','x'}, dimensions={0} | all-to-all | bytes 1179648 | tf_op jit(solution)/shard_map/all_to_all | solution.py:367
  55.8 0.7 shard_map.61
  56.4 10.6 %all_to_all.36 = bf16[8,72,128]{2,1,0:T(8,128)(2,1)S(1)} all-to-all(bf16[8,72,128]{2,1,0:T(8,128)(2,1)S(1)} %get-tuple-element.30), channel_id=1, replica_groups=mesh['z'=8,'x'=4,'y'=8,'core'=2] {'y'}, dimensions={0} | all-to-all | bytes 294912 | tf_op jit(solution)/shard_map/all_to_all | solution.py:367
  67.0 5.0 %all_gather.10.got_ref = bf16[16,72,128]{2,1,0:T(8,128)(2,1)S(1)} all-gather(bf16[8,72,128]{2,1,0:T(8,128)(2,1)S(1)} %all_to_all.36), channel_id=1, replica_groups=mesh['z'=8,'x'=4,'y'=8,'core'=2] {'core'}, dimensions={0}, use_global_device_ids=true | all-gather | bytes 442368 | tf_op jit(solution)/shard_map/all_gather | solution.py:370
  72.1 0.5 shard_map.62
  72.6 11.2 %all_to_all.37.got_ref = bf16[8,72,128]{2,1,0:T(8,128)(2,1)S(1)} all-to-all(bf16[8,72,128]{2,1,0:T(8,128)(2,1)S(1)} %get-tuple-element.31), channel_id=1, replica_groups=mesh['z'=8,'x'=4,'y'=8,'core'=2] {'z'}, dimensions={0} | all-to-all | bytes 294912 | tf_op jit(solution)/shard_map/all_to_all | solution.py:367
  83.7 0.2 shard_map.63
  83.9 7.8 %all_to_all.38.got_ref = bf16[4,64,128]{2,1,0:T(8,128)(2,1)S(1)} all-to-all(bf16[4,64,128]{2,1,0:T(8,128)(2,1)S(1)} %shard_map.63), channel_id=1, replica_groups=mesh['z'=8,'x'=4,'y'=8,'core'=2] {'x'}, dimensions={0} | all-to-all | bytes 131072 | tf_op jit(solution)/shard_map/all_to_all | solution.py:367
  91.7 0.6 shard_map.64
  92.3 10.5 %all_to_all.39 = bf16[8,72,128]{2,1,0:T(8,128)(2,1)S(1)} all-to-all(bf16[8,72,128]{2,1,0:T(8,128)(2,1)S(1)} %get-tuple-element.37), channel_id=1, replica_groups=mesh['z'=8,'x'=4,'y'=8,'core'=2] {'y'}, dimensions={0} | all-to-all | bytes 294912 | tf_op jit(solution)/shard_map/all_to_all | solution.py:367
  102.8 5.8 %all_gather.11.got_ref = bf16[16,72,128]{2,1,0:T(8,128)(2,1)S(1)} all-gather(bf16[8,72,128]{2,1,0:T(8,128)(2,1)S(1)} %all_to_all.39), channel_id=1, replica_groups=mesh['z'=8,'x'=4,'y'=8,'core'=2] {'core'}, dimensions={0}, use_global_device_ids=true | all-gather | bytes 442368 | tf_op jit(solution)/shard_map/all_gather | solution.py:370
  108.6 0.5 shard_map.65
  109.1 11.7 %all_to_all.40 = bf16[32,4,128]{2,1,0:T(4,128)(2,1)S(1)} all-to-all(bf16[32,4,128]{2,1,0:T(4,128)(2,1)S(1)} %bitcast.25), channel_id=1, replica_groups=mesh['z'=8,'x'=4,'y'=8,'core'=2] {'z','x'}, dimensions={0} | all-to-all | bytes 65536 | tf_op jit(solution)/shard_map/all_to_all | solution.py:367
  120.7 0.9 shard_map.66
Async XLA Ops:
  0.6 24.2 %copy-start = (bf16[1,1,32,128,128]{4,3,2,1,0:T(8,128)(2,1)S(1)}, bf16[1,1,32,128,128]{4,3,2,1,0:T(8,128)(2,1)}, u32[]{:S(2)}) copy-start(bf16[1,1,32,128,128]{4,3,2,1,0:T(8,128)(2,1)} %param.4) | copy-start | bytes 3145732
  2.3 17.1 %all-to-all-start = ((bf16[8,128,128]{2,1,0:T(8,128)(2,1)}), bf16[8,128,128]{2,1,0:T(8,128)(2,1)S(1)}, u32[]{:S(2)}, u32[]{:S(2)}) async-start(bf16[8,128,128]{2,1,0:T(8,128)(2,1)} %broadcast_in_dim.2), calls=%async_computation | async-start | bytes 524288 | tf_op jit(solution)/shard_map/all_to_all | solution.py:367
  10.6 0.7 copy-start.1

commit v6 on v5

--- a/solution.py
+++ b/solution.py
@@ -110,16 +110,23 @@
             sent_ref[peer, rows:, :] = extra
 
 
-def tables(
-    places_ref, counts_ref, piece_ref, slot_v_ref, slot_u_ref, lane_v_ref, lane_u_ref, u0_ref, fetch_ref, rows, spans
-):
-    rows[...] = piece_ref[...].astype(F32)
+def begin(rhs_ref, sent_ref, piece_ref, rows):
+    for b in range(rows.shape[0] // 2):
+        rows[2 * b : 2 * b + 2, :] = rhs_ref[:, 128 * b : 128 * b + 128]
+    send_all(sent_ref, rows[...].astype(BF16), None)
     half = rows.shape[0] // 2
-    u0_ref[...] = jnp.concatenate([rows[pl.ds(r, half, stride=2), :] for r in range(2)], axis=1).astype(BF16)
+    piece_ref[...] = jnp.concatenate([rows[pl.ds(r, half, stride=2), :] for r in range(2)], axis=1).astype(BF16)
+
+
+def own_lanes(places_ref, counts_ref, lane_ref):
+    lane_ref[...] = lane_keys(places_ref, counts_ref[0, 0], 1)
+
+
+def tables(places_ref, counts_ref, slot_v_ref, slot_u_ref, lane_u_ref, fetch_ref, spans):
     count = counts_ref[0, 0]
-    for axis, slot_ref, lane_ref in ((0, slot_u_ref, lane_u_ref), (1, slot_v_ref, lane_v_ref)):
-        slot_ref[...] = slot_keys(places_ref, count, axis)
-        lane_ref[...] = lane_keys(places_ref, count, axis)
+    slot_u_ref[...] = slot_keys(places_ref, count, 0)
+    slot_v_ref[...] = slot_keys(places_ref, count, 1)
+    lane_u_ref[...] = lane_keys(places_ref, count, 0)
     span, chips, cores = spans
     for k in range(places_ref.shape[1]):
         block = places_ref[0, k]
@@ -145,10 +152,28 @@
     w_ref[...] = jnp.concatenate([own[:, 0:128], own[:, 128:256]], axis=0)
 
 
-def first_forward(slot_ref, lane_ref, got_ref, tile_ref, sent_ref, w_ref, piece_ref, map_ref, held, out):
-    read_keys(got_ref, map_ref)
-    keys = with_range(slot_ref, row_index(), piece_ref.shape[0])
-    keep(sum_by_key(got_ref, map_ref, keys), w_ref, piece_ref, held)
+def peers_sum(got_ref, rows):
+    total = got_ref[0, 0:rows, :].astype(F32)
+    for peer in range(1, got_ref.shape[0]):
+        total = total + got_ref[peer, 0:rows, :].astype(F32)
+    return total.astype(BF16)
+
+
+def hold_rows(held_ref, own):
+    half = own.shape[0] // 2
+    for r in range(2):
+        held_ref[pl.ds(r, half, stride=2), :] = own[half * r : half * r + half, :].astype(F32)
+
+
+def first_forward(lane_ref, got_ref, tile_ref, sent_ref, w_ref, map_ref, held, out):
+    rows = w_ref.shape[0]
+    for peer in range(got_ref.shape[0]):
+        digits = got_ref[peer, rows:, :].astype(F32)
+        for g in range(2):
+            map_ref[2 * peer + g : 2 * peer + g + 1, :] = digits[2 * g : 2 * g + 1, :] * 64.0 + digits[2 * g + 1 : 2 * g + 2, :]
+    w = peers_sum(got_ref, rows)
+    w_ref[...] = w
+    hold_rows(held, w)
     products(held, tile_ref, out, False)
     send_all(sent_ref, split_rows(out).astype(BF16), lane_ref[...])
 
@@ -161,14 +186,35 @@
     send_all(sent_ref, split_rows(out).astype(BF16), lane_ref[...])
 
 
-def regroup(map_ref, got_ref, sent_ref, line_ref):
+def regroup(target, got_ref, sent_ref, line_ref):
     read_keys(got_ref, line_ref)
-    target = map_ref[pl.ds(lax.axis_index("z"), 1), :]
     column = jnp.transpose(jnp.broadcast_to(target, (128, 128)))
     total = sum_by_key(got_ref, line_ref, column).astype(BF16)
     for peer in range(sent_ref.shape[0]):
         for r in range(2):
             sent_ref[peer, 32 * r : 32 * r + 32, :] = total[32 * peer : 32 * peer + 32, 128 * r : 128 * r + 128]
+
+
+def first_regroup(lane_ref, near1_ref, near2_ref, near3_ref, got_ref, sent_ref, target_ref, line_ref):
+    peers = sent_ref.shape[0]
+    me = lax.axis_index("x")
+    quarter = iota((8, 128), 1) // 32
+    digits = lane_ref[...].astype(F32)
+    for shift, near_ref in enumerate((near1_ref, near2_ref, near3_ref), 1):
+        digits = jnp.where(quarter == (me + peers - shift) % peers, near_ref[...].astype(F32), digits)
+    target = digits[0:1, :] * 64.0 + digits[1:2, :]
+    target_ref[...] = jnp.broadcast_to(target, target_ref.shape)
+    regroup(target, got_ref, sent_ref, line_ref)
+    line = line_ref[...]
+    high = jnp.floor(line * (1.0 / 64.0))
+    low = line - 64.0 * high
+    extra = jnp.concatenate([high[0:1], low[0:1], high[1:2], low[1:2], jnp.zeros((4, 128), F32)], axis=0).astype(BF16)
+    for peer in range(peers):
+        sent_ref[peer, 64:, :] = extra
+
+
+def second_regroup(target_ref, got_ref, sent_ref, line_ref):
+    regroup(target_ref[0:1, :], got_ref, sent_ref, line_ref)
 
 
 def leaders(map_ref, slot_ref, me):
@@ -212,28 +258,26 @@
 
 def second_forward(
     slot_ref, map_ref, got_ref, tile_ref, own_w1_ref, w2_ref, u0_ref, own_w2_ref, own_u_ref,
-    sent_ref, lead_w3_ref, lead_ref, held, out,
+    sent_ref, lead_w1_ref, lead_w3_ref, lead_ref, held, out,
 ):
-    w3 = got_ref[0].astype(F32)
-    for peer in range(1, got_ref.shape[0]):
-        w3 = w3 + got_ref[peer].astype(F32)
-    w3 = w3.astype(BF16).astype(F32)
-    half = w3.shape[0] // 2
-    for r in range(2):
-        held[pl.ds(r, half, stride=2), :] = w3[half * r : half * r + half, :]
+    w3 = peers_sum(got_ref, own_w1_ref.shape[0])
+    hold_rows(held, w3)
     products(held, tile_ref, out, False)
     sent = split_rows(out).astype(BF16)
-    lead = leaders(map_ref, slot_ref, row_index())
+    lead = leaders(map_ref, slot_ref, lax.axis_index("x") * lax.axis_size("z") + lax.axis_index("z"))
     lead_ref[...] = lead
     lead = jnp.concatenate([lead, lead], axis=0)
+    w3 = w3.astype(F32)
     lead_w3 = w3 * lead
     lead_w3_ref[...] = lead_w3.astype(BF16)
     w1 = own_w1_ref[...].astype(F32)
+    lead_w1 = w1 * lead
+    lead_w1_ref[...] = lead_w1.astype(BF16)
     w2 = w2_ref[...].astype(F32)
     u0 = u0_ref[...].astype(F32)
     c4 = sent.astype(F32)
     sums = [
-        sum_slots(w1 * w1 * lead),
+        sum_slots(w1 * lead_w1),
         sum_slots(w1 * lead_w3),
         sum_slots(w3 * lead_w3),
         sum_piece(u0 * u0),
@@ -249,7 +293,7 @@
     send_all(sent_ref, sent, three_parts(block).astype(BF16))
 
 
-def gather_sums(got_ref, map_ref, lane_ref, slot_ref, lead_w3_ref, lead_ref, sent_ref, wide, span):
+def gather_sums(got_ref, map_ref, lane_ref, slot_ref, lead_w1_ref, lead_w3_ref, lead_ref, sent_ref, wide, span):
     peers = got_ref.shape[0]
     rows = got_ref.shape[1] - 8
     partial = got_ref[0, rows:, :].astype(F32)
@@ -267,34 +311,36 @@
     block = jnp.where(lane == 8, sum_piece(square), whole_sums(partial))
     block = block + pltpu.roll(block, 1, 0)
     block = three_parts(block + pltpu.roll(block, 2, 0))
-    owners = sent_ref.shape[0] // 4
+    owners = sent_ref.shape[0] // 8
     slots = slot_ref.shape[0]
     keys = slot_ref[...]
     label = (keys - span * jnp.floor(keys * (1.0 / span)) + 1.0) * lead_ref[...]
     here = iota((slots, 128), 1) == 64 + row_index()
-    values = [lead_w3_ref[0:slots, :], lead_w3_ref[slots:, :], jnp.where(here, label, 0.0).astype(BF16)]
-    values = jnp.concatenate(values, axis=1)
-    values = jnp.concatenate([values, jnp.zeros((128 - slots, 384), BF16)], axis=0)
+    values = [ref[slots * r : slots * r + slots, :] for ref in (lead_w1_ref, lead_w3_ref) for r in range(2)]
+    values = jnp.concatenate(values + [jnp.where(here, label, 0.0).astype(BF16)], axis=1)
+    values = jnp.concatenate([values, jnp.zeros((128 - slots, 640), BF16)], axis=0)
     match = (iota((owners, 128), 0) == lane_ref[...].astype(jnp.int32)[0:1, :]) & (iota((owners, 128), 1) < slots)
     placed = jnp.dot(match.astype(F32).astype(BF16), values, preferred_element_type=F32)
-    wide[pl.ds(0, owners, stride=4), :] = placed[:, 0:128]
-    wide[pl.ds(1, owners, stride=4), :] = placed[:, 128:256]
-    wide[pl.ds(2, owners, stride=4), :] = placed[:, 256:384] + block[3:4, :]
-    wide[pl.ds(3, owners, stride=4), :] = jnp.broadcast_to(block[7:8, :], (owners, 128))
+    for i in range(4):
+        wide[pl.ds(i, owners, stride=8), :] = placed[:, 128 * i : 128 * i + 128]
+    wide[pl.ds(4, owners, stride=8), :] = placed[:, 512:640] + block[3:4, :]
+    wide[pl.ds(5, owners, stride=8), :] = jnp.broadcast_to(block[7:8, :], (owners, 128))
+    for i in (6, 7):
+        wide[pl.ds(i, owners, stride=8), :] = jnp.zeros((owners, 128), F32)
     sent_ref[...] = wide[...].astype(BF16)
 
 
-def finish(got_ref, w1_ref, solution_ref, phi_ref, wide):
+def finish(got_ref, solution_ref, phi_ref, wide):
     wide[...] = got_ref[...].astype(F32)
-    peers = got_ref.shape[0] // 4
-    parts = [wide[pl.ds(i, peers, stride=4), :] for i in range(4)]
-    total = jnp.concatenate([jnp.sum(parts[i], axis=0, keepdims=True) for i in (2, 3)], axis=0)
-    half = w1_ref.shape[0]
+    peers = got_ref.shape[0] // 8
+    parts = [wide[pl.ds(i, peers, stride=8), :] for i in range(6)]
+    total = jnp.concatenate([jnp.sum(parts[i], axis=0, keepdims=True) for i in (4, 5)], axis=0)
+    half = solution_ref.shape[0] // 2
     labels = pltpu.roll(jnp.broadcast_to(total[0:1, :], (half, 128)), 64, 1)
     match = (labels == (iota((half, 128), 0) + 1).astype(F32)) & (iota((half, 128), 1) < peers)
-    values = jnp.concatenate(parts[0:2], axis=1)
-    values = jnp.concatenate([values, jnp.zeros((128 - peers, 256), F32)], axis=0).astype(BF16)
-    w3 = jnp.dot(match.astype(F32).astype(BF16), values, preferred_element_type=F32)
+    values = jnp.concatenate(parts[0:4], axis=1)
+    values = jnp.concatenate([values, jnp.zeros((128 - peers, 512), F32)], axis=0).astype(BF16)
+    placed = jnp.dot(match.astype(F32).astype(BF16), values, preferred_element_type=F32)
     first = iota((8, 128), 0) < 4
     sums = whole_sums(jnp.where(first, total[0:1, :], total[1:2, :]))
 
@@ -335,9 +381,10 @@
 
     phi_ref[...] = jnp.where(iota((1, 128), 1) == 0, phi_bar2[0:1, :], phi_bar2[4:5, :])[:, 0:2]
     for r in range(2):
-        lanes = slice(128 * r, 128 * r + 128)
         scale1, scale3 = k1[4 * r : 4 * r + 1, :], k3[4 * r : 4 * r + 1, :]
-        solution_ref[pl.ds(r, half, stride=2), :] = w1_ref[:, lanes].astype(F32) * scale1 + w3[:, lanes] * scale3
+        w1 = placed[:, 128 * r : 128 * r + 128]
+        w3 = placed[:, 256 + 128 * r : 384 + 128 * r]
+        solution_ref[pl.ds(r, half, stride=2), :] = w1 * scale1 + w3 * scale3
 
 
 def struct(shape, dtype):
@@ -375,65 +422,81 @@
     slot_table = struct((slots, 128), F32)
     lane_table = struct((8, 128), BF16)
     tile = tiles[0, 0]
-    pairs = rhs.reshape(2, span, 128).transpose(1, 0, 2).reshape(2 * span, 128).astype(BF16)
-    slot_v, slot_u, lane_v, lane_u, u0, fetch = call(
+    sent, u0 = call(
+        begin,
+        [VMEM],
+        [struct((chips, 2 * span, 128), BF16), piece],
+        [pltpu.VMEM((2 * span, 128), F32)],
+        rhs,
+    )
+    (lane_v,) = call(own_lanes, [SMEM, SMEM], [lane_table], [], places, counts)
+    n_x, n_z = lax.axis_size("x"), lax.axis_size("z")
+    near = [lax.ppermute(lane_v, "x", [(i, (i + shift) % n_x) for i in range(n_x)]) for shift in range(1, n_x)]
+    slot_v, slot_u, lane_u, fetch = call(
         functools.partial(tables, spans=(span, chips, lax.axis_size("core"))),
-        [SMEM, SMEM, VMEM],
-        [slot_table, slot_table, lane_table, lane_table, piece, struct((2, slots), jnp.int32)],
-        [pltpu.VMEM((2 * span, 128), F32)],
-        places, counts, pairs,
-        out_specs=[VMEM] * 5 + [SMEM],
-    )
-    sent = jnp.broadcast_to(pairs[None], (chips, 2 * span, 128))
+        [SMEM, SMEM],
+        [slot_table, slot_table, lane_table, struct((2, slots), jnp.int32)],
+        [],
+        places, counts,
+        out_specs=[VMEM] * 3 + [SMEM],
+    )
     u_group = exchange_col(sent).reshape(n_col * span, 2, 128)
+    line = [pltpu.VMEM((n_z // 4, 128), F32)]
     sent, own_u = call(
         first_adjoint,
         [SMEM] + [VMEM] * 3,
-        [struct((n_row, rows + 8, 128), BF16), own],
+        [struct((n_z, rows + 8, 128), BF16), own],
         [wide, wide],
         fetch, lane_v, u_group, tile,
     )
-    sent, own_w1, w1, v_map = call(
+    sent, target = call(
+        first_regroup,
+        [VMEM] * 5,
+        [struct((n_x, rows + 8, 128), BF16), struct((8, 128), F32)],
+        line,
+        lane_v, *near, exchange(sent, "z"),
+    )
+    sent, own_w1, v_map = call(
         first_forward,
-        [VMEM] * 4,
-        [struct((chips, rows + 8, 128), BF16), own, piece, struct((n_row // 4, 128), F32)],
+        [VMEM] * 3,
+        [struct((chips, rows + 8, 128), BF16), own, struct((n_row // 4, 128), F32)],
         [wide, wide],
-        slot_v, lane_u, exchange(sent, ROW), tile,
+        lane_u, exchange(sent, "x"), tile,
     )
     sent, own_w2, w2, u_map = call(
         second_adjoint,
         [VMEM] * 4,
-        [struct((lax.axis_size("z"), rows + 8, 128), BF16), own, piece, struct((n_col // 4, 128), F32)],
+        [struct((n_z, rows + 8, 128), BF16), own, piece, struct((n_col // 4, 128), F32)],
         [wide, wide],
         slot_u, lane_v, exchange_col(sent), tile,
     )
     (sent,) = call(
-        regroup,
+        second_regroup,
         [VMEM] * 2,
-        [struct((lax.axis_size("x"), rows, 128), BF16)],
-        [pltpu.VMEM((lax.axis_size("z") // 4, 128), F32)],
-        v_map, exchange(sent, "z"),
-    )
-    sent, lead_w3, lead = call(
+        [struct((n_x, rows, 128), BF16)],
+        line,
+        target, exchange(sent, "z"),
+    )
+    sent, lead_w1, lead_w3, lead = call(
         second_forward,
         [VMEM] * 9,
-        [struct((chips, rows + 8, 128), BF16), own, slot_table],
+        [struct((chips, rows + 8, 128), BF16), own, own, slot_table],
         [wide, wide],
         slot_v, v_map, exchange(sent, "x"), tile, own_w1, w2, u0, own_w2, own_u,
     )
     (sent,) = call(
         functools.partial(gather_sums, span=span),
-        [VMEM] * 6,
-        [struct((n_row * 4, 128), BF16)],
-        [pltpu.VMEM((n_row * 4, 128), F32)],
-        exchange_col(sent), u_map, lane_v, slot_v, lead_w3, lead,
+        [VMEM] * 7,
+        [struct((n_row * 8, 128), BF16)],
+        [pltpu.VMEM((n_row * 8, 128), F32)],
+        exchange_col(sent), u_map, lane_v, slot_v, lead_w1, lead_w3, lead,
     )
     result, phi_bar = call(
         finish,
-        [VMEM] * 2,
+        [VMEM],
         [struct((2 * span, 128), F32), struct((1, 2), F32)],
-        [pltpu.VMEM((n_row * 4, 128), F32)],
-        exchange(sent.reshape(n_row, 4, 128), ROW).reshape(n_row * 4, 128), w1,
+        [pltpu.VMEM((n_row * 8, 128), F32)],
+        exchange(sent.reshape(n_row, 8, 128), ROW).reshape(n_row * 8, 128),
     )
     result = result.reshape(span, 2, 128).transpose(1, 0, 2).reshape(2, span * 128)
     return (result, phi_bar.reshape(2))

time: 122 us -> 127 us (1.041)
  starting transfers between devices: 7.65 us -> 28 us
  blocking collectives: 98.1 us -> 80.7 us
  Pallas kernels: 5.78 us -> 7.66 us
    all_to_all x6, blocking collectives: 81.8 us -> 62.7 us  [exchange(): return lax.all_to_all(sent, axis, split_axis=0, concat_axis=0, tiled=True)]
    ppermute x0 -> x3, starting transfers between devices: none -> 10.5 us  [on_device(): lax.ppermute(lane_v, 'x', [(i, (i + shift) % n_x) for i in range(n_x)])]
    all_to_all x1 -> x2, starting transfers between devices: 7.65 us -> 17.5 us  [exchange(): return lax.all_to_all(sent, axis, split_axis=0, concat_axis=0, tiled=True)]
    pallas_call x8 -> x11, Pallas kernels: 5.78 us -> 7.66 us  [call(): pl.pallas_call(body, out_shape=outs, in_specs=specs, out_specs=[VMEM] * l...]
    all_gather x3, blocking collectives: 16.3 us -> 17.9 us  [exchange_col(): return lax.all_gather(exchange(sent, 'y'), 'core', axis=0, tiled=True)]
    all_to_all x1 -> x2, waiting for transfers between devices: 6.41 us -> 5.86 us  [exchange(): return lax.all_to_all(sent, axis, split_axis=0, concat_axis=0, tiled=True)]
  transfers between devices with their start and end apart: 1 -> 5, of which waited for: 1 -> 2; matrix products, arithmetic and copies ran while one was open for 0% -> 0% of each run, Pallas kernels for 1% -> 2%
where the time goes in v6:
time: 127 us; the launch traced here: 126 us
  blocking collectives  80.7 us (64%)
  starting transfers between devices  28 us (22%)
  Pallas kernels  7.66 us (6%)
  waiting for transfers between devices  7.11 us (6%)
  local copies, waits for them, and re-layouts  1.51 us (1%)
  between operations  1.39 us (1%)
    all_to_all x6, blocking collectives, exchange(): return lax.all_to_all(sent, axis, split_axis=0, concat_axis=0, tiled=True)  62.7 us
    all_gather x3, blocking collectives, exchange_col(): return lax.all_gather(exchange(sent, 'y'), 'core', axis=0, tiled=True)  17.9 us
    all_to_all x2, starting transfers between devices, exchange(): return lax.all_to_all(sent, axis, split_axis=0, concat_axis=0, tiled=True)  17.5 us
    ppermute x3, starting transfers between devices, on_device(): lax.ppermute(lane_v, 'x', [(i, (i + shift) % n_x) for i in range(n_x)])  10.5 us
    pallas_call x11, Pallas kernels, call(): pl.pallas_call(body, out_shape=outs, in_specs=specs, out_specs=[VMEM] * l...  7.66 us
    all_to_all x2, waiting for transfers between devices, exchange(): return lax.all_to_all(sent, axis, split_axis=0, concat_axis=0, tiled=True)  5.86 us
  transfers between devices with their start and end apart: 5, of which 2 were waited for; matrix products, arithmetic and copies ran while one was open for 0% of the time, Pallas kernels for 2%

profile of v6, /device:TPU:1, one launch (start us, length us, event | category | flops | bytes accessed | tf_op | source)
XLA Modules:
  0.0 126.3 jit_solution(17595632674411670313)
XLA Ops:
  0.6 0.0 copy-start.1
  0.6 0.8 copy-done.1
  1.5 0.0 copy-start
  1.5 0.7 shard_map.61
  2.2 7.7 %all-to-all-start = ((bf16[8,128,128]{2,1,0:T(8,128)(2,1)}), bf16[8,128,128]{2,1,0:T(8,128)(2,1)S(1)}, u32[]{:S(2)}, u32[]{:S(2)}) async-start(bf16[8,128,128]{2,1,0:T(8,128)(2,1)} %get-tuple-element.28), calls=%async_computation | async-start | bytes 524288 | tf_op jit(solution)/shard_map/all_to_all | solution.py:414
  10.5 0.0 copy-start.2
  10.5 0.7 copy-done.2
  11.2 0.6 shard_map.60.lane_ref
  11.8 1.6 %shard_map.59 = (f32[32,128]{1,0:T(8,128)S(1)}, f32[32,128]{1,0:T(8,128)S(1)}, bf16[8,128]{1,0:T(8,128)(2,1)S(1)}, s32[2,32]{1,0:T(2,128)S(1)}) custom-call(s32[2,32]{1,0:T(2,128)S(1)} %bitcast.21, s32[1,1]{1,0:T(1,128)S(6)} %copy.8.counts_ref), custom_call_target="tpu_custom_call" | custom-call | tf_op jit(solution)/shard_map/pallas_call | solution.py:404
  13.4 5.9 %all-to-all-done = bf16[8,128,128]{2,1,0:T(8,128)(2,1)S(1)} async-done(((bf16[8,128,128]{2,1,0:T(8,128)(2,1)}), bf16[8,128,128]{2,1,0:T(8,128)(2,1)S(1)}, u32[]{:S(2)}, u32[]{:S(2)}) %all-to-all-start) | async-done | bytes 262176 | tf_op jit(solution)/shard_map/all_to_all | solution.py:414
  19.2 5.4 %all_gather.9 = bf16[16,128,128]{2,1,0:T(8,128)(2,1)S(1)} all-gather(bf16[8,128,128]{2,1,0:T(8,128)(2,1)S(1)} %all-to-all-done), channel_id=1, replica_groups=mesh['z'=8,'x'=4,'y'=8,'core'=2] {'core'}, dimensions={0}, use_global_device_ids=true | all-gather | bytes 786432 | tf_op jit(solution)/shard_map/all_gather | solution.py:417
  24.7 0.0 copy-done
  24.7 1.5 %shard_map.62 = (bf16[8,72,128]{2,1,0:T(8,128)(2,1)}, bf16[64,128]{1,0:T(8,128)(2,1)S(1)}) custom-call(s32[2,32]{1,0:T(2,128)S(1)} %get-tuple-element.27.fetch_ref, bf16[8,128]{1,0:T(8,128)(2,1)S(1)} %shard_map.60.lane_ref, bf16[1024,2,128]{2,1,0:T(2,128)(2,1)S(1)} %bitcast.17, bf16[32,128,128]{2,1,0:T(8,128)(2,1)S(1)} %bitcast.13), custom_call_target="tpu_custom_call" | custom-call | tf_op jit(solution)/shard_map/pallas_call | solution.py:404
  26.2 9.8 %all-to-all-start.1 = ((bf16[8,72,128]{2,1,0:T(8,128)(2,1)}), bf16[8,72,128]{2,1,0:T(8,128)(2,1)S(1)}, u32[]{:S(2)}, u32[]{:S(2)}) async-start(bf16[8,72,128]{2,1,0:T(8,128)(2,1)} %get-tuple-element.29), calls=%async_computation.1 | async-start | bytes 294912 | tf_op jit(solution)/shard_map/all_to_all | solution.py:414
  36.0 3.1 %collective-permute-start = (bf16[8,128]{1,0:T(8,128)(2,1)S(1)}, bf16[8,128]{1,0:T(8,128)(2,1)S(1)}, u32[]{:S(2)}, u32[]{:S(2)}) collective-permute-start(bf16[8,128]{1,0:T(8,128)(2,1)S(1)} %shard_map.60.lane_ref), channel_id=1, source_target_pairs={{0,16},{16,32},{32,48},{48,0},{1,17},{17,33},{33,49},{49,1},{2,18}... | collective-permute-start | bytes 6152 | tf_op jit(solution)/shard_map/ppermute | solution.py:434
  39.1 4.4 %collective-permute-start.1 = (bf16[8,128]{1,0:T(8,128)(2,1)S(1)}, bf16[8,128]{1,0:T(8,128)(2,1)S(1)}, u32[]{:S(2)}, u32[]{:S(2)}) collective-permute-start(bf16[8,128]{1,0:T(8,128)(2,1)S(1)} %shard_map.60.lane_ref), channel_id=1, source_target_pairs={{0,32},{16,48},{32,0},{48,16},{1,33},{17,49},{33,1},{49,17},{2,34}... | collective-permute-start | bytes 6152 | tf_op jit(solution)/shard_map/ppermute | solution.py:434
  43.5 3.1 %collective-permute-start.2 = (bf16[8,128]{1,0:T(8,128)(2,1)S(1)}, bf16[8,128]{1,0:T(8,128)(2,1)S(1)}, u32[]{:S(2)}, u32[]{:S(2)}) collective-permute-start(bf16[8,128]{1,0:T(8,128)(2,1)S(1)} %shard_map.60.lane_ref), channel_id=1, source_target_pairs={{0,48},{16,0},{32,16},{48,32},{1,49},{17,1},{33,17},{49,33},{2,50}... | collective-permute-start | bytes 6152 | tf_op jit(solution)/shard_map/ppermute | solution.py:434
  46.6 0.0 collective-permute-done.near1_ref
  46.6 0.0 collective-permute-done.1.near2_ref
  46.6 1.2 collective-permute-done.2.near3_ref
  47.8 0.0 all-to-all-done.1.got_ref
  47.8 0.2 shard_map.63
  48.1 8.0 %all_to_all.40.got_ref = bf16[4,72,128]{2,1,0:T(8,128)(2,1)S(1)} all-to-all(bf16[4,72,128]{2,1,0:T(8,128)(2,1)S(1)} %get-tuple-element.30), channel_id=1, replica_groups=mesh['z'=8,'x'=4,'y'=8,'core'=2] {'x'}, dimensions={0} | all-to-all | bytes 147456 | tf_op jit(solution)/shard_map/all_to_all | solution.py:414
  56.0 0.4 shard_map.64
  56.4 10.5 %all_to_all.41 = bf16[8,72,128]{2,1,0:T(8,128)(2,1)S(1)} all-to-all(bf16[8,72,128]{2,1,0:T(8,128)(2,1)S(1)} %get-tuple-element.34), channel_id=1, replica_groups=mesh['z'=8,'x'=4,'y'=8,'core'=2] {'y'}, dimensions={0} | all-to-all | bytes 294912 | tf_op jit(solution)/shard_map/all_to_all | solution.py:414
  66.9 6.6 %all_gather.10.got_ref = bf16[16,72,128]{2,1,0:T(8,128)(2,1)S(1)} all-gather(bf16[8,72,128]{2,1,0:T(8,128)(2,1)S(1)} %all_to_all.41), channel_id=1, replica_groups=mesh['z'=8,'x'=4,'y'=8,'core'=2] {'core'}, dimensions={0}, use_global_device_ids=true | all-gather | bytes 442368 | tf_op jit(solution)/shard_map/all_gather | solution.py:417
  73.5 0.5 shard_map.65
  74.0 15.0 %all_to_all.42.got_ref = bf16[8,72,128]{2,1,0:T(8,128)(2,1)S(1)} all-to-all(bf16[8,72,128]{2,1,0:T(8,128)(2,1)S(1)} %get-tuple-element.35), channel_id=1, replica_groups=mesh['z'=8,'x'=4,'y'=8,'core'=2] {'z'}, dimensions={0} | all-to-all | bytes 294912 | tf_op jit(solution)/shard_map/all_to_all | solution.py:414
  89.0 0.2 shard_map.66
  89.2 6.8 %all_to_all.43.got_ref = bf16[4,64,128]{2,1,0:T(8,128)(2,1)S(1)} all-to-all(bf16[4,64,128]{2,1,0:T(8,128)(2,1)S(1)} %shard_map.66), channel_id=1, replica_groups=mesh['z'=8,'x'=4,'y'=8,'core'=2] {'x'}, dimensions={0} | all-to-all | bytes 131072 | tf_op jit(solution)/shard_map/all_to_all | solution.py:414
  96.1 0.6 shard_map.67
  96.6 10.6 %all_to_all.44 = bf16[8,72,128]{2,1,0:T(8,128)(2,1)S(1)} all-to-all(bf16[8,72,128]{2,1,0:T(8,128)(2,1)S(1)} %get-tuple-element.41), channel_id=1, replica_groups=mesh['z'=8,'x'=4,'y'=8,'core'=2] {'y'}, dimensions={0} | all-to-all | bytes 294912 | tf_op jit(solution)/shard_map/all_to_all | solution.py:414
  107.2 5.9 %all_gather.11.got_ref = bf16[16,72,128]{2,1,0:T(8,128)(2,1)S(1)} all-gather(bf16[8,72,128]{2,1,0:T(8,128)(2,1)S(1)} %all_to_all.44), channel_id=1, replica_groups=mesh['z'=8,'x'=4,'y'=8,'core'=2] {'core'}, dimensions={0}, use_global_device_ids=true | all-gather | bytes 442368 | tf_op jit(solution)/shard_map/all_gather | solution.py:417
  113.1 0.5 shard_map.68
  113.6 11.8 %all_to_all.45 = bf16[32,8,128]{2,1,0:T(8,128)(2,1)S(1)} all-to-all(bf16[32,8,128]{2,1,0:T(8,128)(2,1)S(1)} %bitcast.19), channel_id=1, replica_groups=mesh['z'=8,'x'=4,'y'=8,'core'=2] {'z','x'}, dimensions={0} | all-to-all | bytes 131072 | tf_op jit(solution)/shard_map/all_to_all | solution.py:414
  125.4 0.9 shard_map.69
Async XLA Ops:
  0.6 0.8 copy-start.1
  1.5 23.2 %copy-start = (bf16[1,1,32,128,128]{4,3,2,1,0:T(8,128)(2,1)S(1)}, bf16[1,1,32,128,128]{4,3,2,1,0:T(8,128)(2,1)}, u32[]{:S(2)}) copy-start(bf16[1,1,32,128,128]{4,3,2,1,0:T(8,128)(2,1)} %param.4) | copy-start | bytes 3145732
  2.2 17.1 %all-to-all-start = ((bf16[8,128,128]{2,1,0:T(8,128)(2,1)}), bf16[8,128,128]{2,1,0:T(8,128)(2,1)S(1)}, u32[]{:S(2)}, u32[]{:S(2)}) async-start(bf16[8,128,128]{2,1,0:T(8,128)(2,1)} %get-tuple-element.28), calls=%async_computation | async-start | bytes 524288 | tf_op jit(solution)/shard_map/all_to_all | solution.py:414
  10.5 0.7 copy-start.2
  26.2 21.6 %all-to-all-start.1 = ((bf16[8,72,128]{2,1,0:T(8,128)(2,1)}), bf16[8,72,128]{2,1,0:T(8,128)(2,1)S(1)}, u32[]{:S(2)}, u32[]{:S(2)}) async-start(bf16[8,72,128]{2,1,0:T(8,128)(2,1)} %get-tuple-element.29), calls=%async_computation.1 | async-start | bytes 294912 | tf_op jit(solution)/shard_map/all_to_all | solution.py:414
  36.0 10.6 %collective-permute-start = (bf16[8,128]{1,0:T(8,128)(2,1)S(1)}, bf16[8,128]{1,0:T(8,128)(2,1)S(1)}, u32[]{:S(2)}, u32[]{:S(2)}) collective-permute-start(bf16[8,128]{1,0:T(8,128)(2,1)S(1)} %shard_map.60.lane_ref), channel_id=1, source_target_pairs={{0,16},{16,32},{32,48},{48,0},{1,17},{17,33},{33,49},{49,1},{2,18}... | collective-permute-start | bytes 6152 | tf_op jit(solution)/shard_map/ppermute | solution.py:434
  39.1 7.5 %collective-permute-start.1 = (bf16[8,128]{1,0:T(8,128)(2,1)S(1)}, bf16[8,128]{1,0:T(8,128)(2,1)S(1)}, u32[]{:S(2)}, u32[]{:S(2)}) collective-permute-start(bf16[8,128]{1,0:T(8,128)(2,1)S(1)} %shard_map.60.lane_ref), channel_id=1, source_target_pairs={{0,32},{16,48},{32,0},{48,16},{1,33},{17,49},{33,1},{49,17},{2,34}... | collective-permute-start | bytes 6152 | tf_op jit(solution)/shard_map/ppermute | solution.py:434
  43.5 4.3 %collective-permute-start.2 = (bf16[8,128]{1,0:T(8,128)(2,1)S(1)}, bf16[8,128]{1,0:T(8,128)(2,1)S(1)}, u32[]{:S(2)}, u32[]{:S(2)}) collective-permute-start(bf16[8,128]{1,0:T(8,128)(2,1)S(1)} %shard_map.60.lane_ref), channel_id=1, source_target_pairs={{0,48},{16,0},{32,16},{48,32},{1,49},{17,1},{33,17},{49,33},{2,50}... | collective-permute-start | bytes 6152 | tf_op jit(solution)/shard_map/ppermute | solution.py:434

commit v7 on v5

--- a/solution.py
+++ b/solution.py
@@ -15,6 +15,7 @@
 COL = ("y", "core")
 VMEM = pl.BlockSpec(memory_space=pltpu.VMEM)
 SMEM = pl.BlockSpec(memory_space=pltpu.SMEM)
+HBM = pl.BlockSpec(memory_space=pltpu.HBM)
 
 
 def iota(shape, dim):
@@ -38,8 +39,8 @@
     return keys.astype(F32)
 
 
-def with_range(slot_ref, me, span):
-    return jnp.concatenate([slot_ref[...], (me * span + iota((span, 128), 0)).astype(F32)], axis=0)
+def range_keys(me, span):
+    return (me * span + iota((span, 128), 0)).astype(F32)
 
 
 def lane_keys(places_ref, count, axis):
@@ -110,12 +111,23 @@
             sent_ref[peer, rows:, :] = extra
 
 
-def tables(
-    places_ref, counts_ref, piece_ref, slot_v_ref, slot_u_ref, lane_v_ref, lane_u_ref, u0_ref, fetch_ref, rows, spans
-):
-    rows[...] = piece_ref[...].astype(F32)
+def begin(rhs_hbm, sent_hbm, piece_ref, rhs_ref, rows, packed, in_sem, out_sems):
+    copy = pltpu.make_async_copy(rhs_hbm, rhs_ref, in_sem)
+    copy.start()
+    copy.wait()
+    for b in range(rows.shape[0] // 2):
+        rows[2 * b : 2 * b + 2, :] = rhs_ref[:, 128 * b : 128 * b + 128]
+    packed[...] = rows[...].astype(BF16)
+    copies = [pltpu.make_async_copy(packed, sent_hbm.at[i], out_sems.at[i]) for i in range(sent_hbm.shape[0])]
+    for copy in copies:
+        copy.start()
     half = rows.shape[0] // 2
-    u0_ref[...] = jnp.concatenate([rows[pl.ds(r, half, stride=2), :] for r in range(2)], axis=1).astype(BF16)
+    piece_ref[...] = jnp.concatenate([rows[pl.ds(r, half, stride=2), :] for r in range(2)], axis=1).astype(BF16)
+    for copy in copies:
+        copy.wait()
+
+
+def tables(places_ref, counts_ref, slot_v_ref, slot_u_ref, lane_v_ref, lane_u_ref, fetch_ref, spans):
     count = counts_ref[0, 0]
     for axis, slot_ref, lane_ref in ((0, slot_u_ref, lane_u_ref), (1, slot_v_ref, lane_v_ref)):
         slot_ref[...] = slot_keys(places_ref, count, axis)
@@ -136,27 +148,22 @@
     send_all(sent_ref, split_rows(out).astype(BF16), lane_ref[...])
 
 
-def keep(w, w_ref, piece_ref, held):
-    slots = held.shape[0] // 2
+def keep(w, w_ref, held):
     w = w.astype(BF16)
-    own = w[0:slots, :]
-    piece_ref[...] = w[slots:, :]
-    hold(held, own)
-    w_ref[...] = jnp.concatenate([own[:, 0:128], own[:, 128:256]], axis=0)
-
-
-def first_forward(slot_ref, lane_ref, got_ref, tile_ref, sent_ref, w_ref, piece_ref, map_ref, held, out):
+    hold(held, w)
+    w_ref[...] = jnp.concatenate([w[:, 0:128], w[:, 128:256]], axis=0)
+
+
+def first_forward(slot_ref, lane_ref, got_ref, tile_ref, sent_ref, w_ref, map_ref, held, out):
     read_keys(got_ref, map_ref)
-    keys = with_range(slot_ref, row_index(), piece_ref.shape[0])
-    keep(sum_by_key(got_ref, map_ref, keys), w_ref, piece_ref, held)
+    keep(sum_by_key(got_ref, map_ref, slot_ref[...]), w_ref, held)
     products(held, tile_ref, out, False)
     send_all(sent_ref, split_rows(out).astype(BF16), lane_ref[...])
 
 
-def second_adjoint(slot_ref, lane_ref, got_ref, tile_ref, sent_ref, w_ref, piece_ref, map_ref, held, out):
+def second_adjoint(slot_ref, lane_ref, got_ref, tile_ref, sent_ref, w_ref, map_ref, held, out):
     read_keys(got_ref, map_ref)
-    keys = with_range(slot_ref, col_index(), piece_ref.shape[0])
-    keep(sum_by_key(got_ref, map_ref, keys), w_ref, piece_ref, held)
+    keep(sum_by_key(got_ref, map_ref, slot_ref[...]), w_ref, held)
     products(held, tile_ref, out, True)
     send_all(sent_ref, split_rows(out).astype(BF16), lane_ref[...])
 
@@ -210,9 +217,34 @@
     return parts + pltpu.roll(parts, 112, 1) + pltpu.roll(parts, 96, 1)
 
 
+def lay_out(sums):
+    lane = iota((8, 128), 1)
+    block = jnp.zeros((8, 128), F32)
+    for j, value in sums.items():
+        block = jnp.where(lane == j, value, block)
+    return block
+
+
+def aside_v(got_ref, map_ref, slot_ref, piece_ref, lead_ref):
+    piece_ref[...] = sum_by_key(got_ref, map_ref, range_keys(row_index(), piece_ref.shape[0])).astype(BF16)
+    lead_ref[...] = leaders(map_ref, slot_ref, row_index())
+
+
+def aside_u(got_ref, map_ref, w1_ref, u0_ref, early_ref, match_ref):
+    w2 = sum_by_key(got_ref, map_ref, range_keys(col_index(), u0_ref.shape[0])).astype(BF16).astype(F32)
+    w1 = w1_ref[...].astype(F32)
+    u0 = u0_ref[...].astype(F32)
+    early_ref[...] = lay_out({0: sum_piece(w1 * w1), 3: sum_piece(u0 * u0), 4: sum_piece(u0 * w2), 5: sum_piece(w2 * w2)})
+    groups = map_ref.shape[0]
+    for g in range(groups):
+        column = jnp.transpose(jnp.broadcast_to(map_ref[g : g + 1, :], (128, 128)))
+        for h in range(g, groups):
+            match = jnp.where(column == map_ref[h : h + 1, :], 1.0 if h == g else 2.0, 0.0)
+            match_ref[128 * g : 128 * g + 128, 128 * h : 128 * h + 128] = match.astype(BF16)
+
+
 def second_forward(
-    slot_ref, map_ref, got_ref, tile_ref, own_w1_ref, w2_ref, u0_ref, own_w2_ref, own_u_ref,
-    sent_ref, lead_w3_ref, lead_ref, held, out,
+    lead_ref, got_ref, tile_ref, early_ref, own_w1_ref, own_w2_ref, own_u_ref, sent_ref, lead_w3_ref, held, out
 ):
     w3 = got_ref[0].astype(F32)
     for peer in range(1, got_ref.shape[0]):
@@ -223,33 +255,36 @@
         held[pl.ds(r, half, stride=2), :] = w3[half * r : half * r + half, :]
     products(held, tile_ref, out, False)
     sent = split_rows(out).astype(BF16)
-    lead = leaders(map_ref, slot_ref, row_index())
-    lead_ref[...] = lead
-    lead = jnp.concatenate([lead, lead], axis=0)
-    lead_w3 = w3 * lead
+    lead = lead_ref[...]
+    lead_w3 = w3 * jnp.concatenate([lead, lead], axis=0)
     lead_w3_ref[...] = lead_w3.astype(BF16)
-    w1 = own_w1_ref[...].astype(F32)
-    w2 = w2_ref[...].astype(F32)
-    u0 = u0_ref[...].astype(F32)
     c4 = sent.astype(F32)
-    sums = [
-        sum_slots(w1 * w1 * lead),
-        sum_slots(w1 * lead_w3),
-        sum_slots(w3 * lead_w3),
-        sum_piece(u0 * u0),
-        sum_piece(u0 * w2),
-        sum_piece(w2 * w2),
-        sum_slots(c4 * own_w2_ref[...].astype(F32)),
-        sum_slots(c4 * own_u_ref[...].astype(F32)),
-    ]
-    lane = iota((8, 128), 1)
-    block = jnp.zeros((8, 128), F32)
-    for j, value in enumerate(sums):
-        block = jnp.where(lane == j, value, block)
-    send_all(sent_ref, sent, three_parts(block).astype(BF16))
-
-
-def gather_sums(got_ref, map_ref, lane_ref, slot_ref, lead_w3_ref, lead_ref, sent_ref, wide, span):
+    sums = {
+        1: sum_slots(own_w1_ref[...].astype(F32) * lead_w3),
+        2: sum_slots(w3 * lead_w3),
+        6: sum_slots(c4 * own_w2_ref[...].astype(F32)),
+        7: sum_slots(c4 * own_u_ref[...].astype(F32)),
+    }
+    send_all(sent_ref, sent, three_parts(early_ref[...] + lay_out(sums)).astype(BF16))
+
+
+def aside_w3(lane_ref, slot_ref, lead_ref, lead_w3_ref, placed_ref, span):
+    owners = placed_ref.shape[0] // 4
+    slots = slot_ref.shape[0]
+    keys = slot_ref[...]
+    label = (keys - span * jnp.floor(keys * (1.0 / span)) + 1.0) * lead_ref[...]
+    here = iota((slots, 128), 1) == 64 + row_index()
+    values = [lead_w3_ref[0:slots, :], lead_w3_ref[slots:, :], jnp.where(here, label, 0.0).astype(BF16)]
+    values = jnp.concatenate(values, axis=1)
+    values = jnp.concatenate([values, jnp.zeros((128 - slots, 384), BF16)], axis=0)
+    match = (iota((owners, 128), 0) == lane_ref[...].astype(jnp.int32)[0:1, :]) & (iota((owners, 128), 1) < slots)
+    placed = jnp.dot(match.astype(F32).astype(BF16), values, preferred_element_type=F32)
+    for i in range(3):
+        placed_ref[pl.ds(i, owners, stride=4), :] = placed[:, 128 * i : 128 * i + 128]
+    placed_ref[pl.ds(3, owners, stride=4), :] = jnp.zeros((owners, 128), F32)
+
+
+def gather_sums(got_ref, match_ref, placed_ref, sent_ref):
     peers = got_ref.shape[0]
     rows = got_ref.shape[1] - 8
     partial = got_ref[0, rows:, :].astype(F32)
@@ -259,29 +294,16 @@
     values = jnp.concatenate([four_peers(got_ref, g) for g in range(groups)], axis=0)
     square = jnp.zeros((8, 256), F32)
     for g in range(groups):
-        column = jnp.transpose(jnp.broadcast_to(map_ref[g : g + 1, :], (128, 128)))
-        match = [jnp.where(column == map_ref[h : h + 1, :], 1.0 if h == g else 2.0, 0.0) for h in range(g, groups)]
-        total = jnp.dot(jnp.concatenate(match, axis=1).astype(BF16), values[128 * g :, :], preferred_element_type=F32)
-        square = square + jnp.sum((values[128 * g : 128 * g + 128, :].astype(F32) * total).reshape(16, 8, 256), axis=0)
-    lane = iota((8, 128), 1)
-    block = jnp.where(lane == 8, sum_piece(square), whole_sums(partial))
+        here = slice(128 * g, 128 * g + 128)
+        total = jnp.dot(match_ref[here, 128 * g :], values[128 * g :, :], preferred_element_type=F32)
+        square = square + jnp.sum((values[here, :].astype(F32) * total).reshape(16, 8, 256), axis=0)
+    block = jnp.where(iota((8, 128), 1) == 8, sum_piece(square), whole_sums(partial))
     block = block + pltpu.roll(block, 1, 0)
     block = three_parts(block + pltpu.roll(block, 2, 0))
-    owners = sent_ref.shape[0] // 4
-    slots = slot_ref.shape[0]
-    keys = slot_ref[...]
-    label = (keys - span * jnp.floor(keys * (1.0 / span)) + 1.0) * lead_ref[...]
-    here = iota((slots, 128), 1) == 64 + row_index()
-    values = [lead_w3_ref[0:slots, :], lead_w3_ref[slots:, :], jnp.where(here, label, 0.0).astype(BF16)]
-    values = jnp.concatenate(values, axis=1)
-    values = jnp.concatenate([values, jnp.zeros((128 - slots, 384), BF16)], axis=0)
-    match = (iota((owners, 128), 0) == lane_ref[...].astype(jnp.int32)[0:1, :]) & (iota((owners, 128), 1) < slots)
-    placed = jnp.dot(match.astype(F32).astype(BF16), values, preferred_element_type=F32)
-    wide[pl.ds(0, owners, stride=4), :] = placed[:, 0:128]
-    wide[pl.ds(1, owners, stride=4), :] = placed[:, 128:256]
-    wide[pl.ds(2, owners, stride=4), :] = placed[:, 256:384] + block[3:4, :]
-    wide[pl.ds(3, owners, stride=4), :] = jnp.broadcast_to(block[7:8, :], (owners, 128))
-    sent_ref[...] = wide[...].astype(BF16)
+    place = iota((8, 128), 0) % 4
+    block = jnp.where(place == 2, block[3:4, :], jnp.where(place == 3, block[7:8, :], 0.0))
+    placed = placed_ref[...].reshape(placed_ref.shape[0] // 8, 8, 128) + block[None]
+    sent_ref[...] = placed.reshape(placed_ref.shape).astype(BF16)
 
 
 def finish(got_ref, w1_ref, solution_ref, phi_ref, wide):
@@ -375,16 +397,28 @@
     slot_table = struct((slots, 128), F32)
     lane_table = struct((8, 128), BF16)
     tile = tiles[0, 0]
-    pairs = rhs.reshape(2, span, 128).transpose(1, 0, 2).reshape(2 * span, 128).astype(BF16)
-    slot_v, slot_u, lane_v, lane_u, u0, fetch = call(
+    sent, u0 = call(
+        begin,
+        [HBM],
+        [struct((chips, 2 * span, 128), BF16), piece],
+        [
+            pltpu.VMEM(rhs.shape, F32),
+            pltpu.VMEM((2 * span, 128), F32),
+            pltpu.VMEM((2 * span, 128), BF16),
+            pltpu.SemaphoreType.DMA(()),
+            pltpu.SemaphoreType.DMA((chips,)),
+        ],
+        pltpu.with_memory_space_constraint(rhs, pltpu.HBM),
+        out_specs=[HBM, VMEM],
+    )
+    slot_v, slot_u, lane_v, lane_u, fetch = call(
         functools.partial(tables, spans=(span, chips, lax.axis_size("core"))),
-        [SMEM, SMEM, VMEM],
-        [slot_table, slot_table, lane_table, lane_table, piece, struct((2, slots), jnp.int32)],
-        [pltpu.VMEM((2 * span, 128), F32)],
-        places, counts, pairs,
-        out_specs=[VMEM] * 5 + [SMEM],
-    )
-    sent = jnp.broadcast_to(pairs[None], (chips, 2 * span, 128))
+        [SMEM, SMEM],
+        [slot_table, slot_table, lane_table, lane_table, struct((2, slots), jnp.int32)],
+        [],
+        places, counts,
+        out_specs=[VMEM] * 4 + [SMEM],
+    )
     u_group = exchange_col(sent).reshape(n_col * span, 2, 128)
     sent, own_u = call(
         first_adjoint,
@@ -393,19 +427,29 @@
         [wide, wide],
         fetch, lane_v, u_group, tile,
     )
-    sent, own_w1, w1, v_map = call(
+    got = exchange(sent, ROW)
+    sent, own_w1, v_map = call(
         first_forward,
         [VMEM] * 4,
-        [struct((chips, rows + 8, 128), BF16), own, piece, struct((n_row // 4, 128), F32)],
+        [struct((chips, rows + 8, 128), BF16), own, struct((n_row // 4, 128), F32)],
         [wide, wide],
-        slot_v, lane_u, exchange(sent, ROW), tile,
-    )
-    sent, own_w2, w2, u_map = call(
+        slot_v, lane_u, got, tile,
+    )
+    w1, lead = call(aside_v, [VMEM] * 3, [piece, slot_table], [], got, v_map, slot_v)
+    got = exchange_col(sent)
+    sent, own_w2, u_map = call(
         second_adjoint,
         [VMEM] * 4,
-        [struct((lax.axis_size("z"), rows + 8, 128), BF16), own, piece, struct((n_col // 4, 128), F32)],
+        [struct((lax.axis_size("z"), rows + 8, 128), BF16), own, struct((n_col // 4, 128), F32)],
         [wide, wide],
-        slot_u, lane_v, exchange_col(sent), tile,
+        slot_u, lane_v, got, tile,
+    )
+    early, match = call(
+        aside_u,
+        [VMEM] * 4,
+        [struct((8, 128), F32), struct((n_col * slots, n_col * slots), BF16)],
+        [],
+        got, u_map, w1, u0,
     )
     (sent,) = call(
         regroup,
@@ -414,19 +458,26 @@
         [pltpu.VMEM((lax.axis_size("z") // 4, 128), F32)],
         v_map, exchange(sent, "z"),
     )
-    sent, lead_w3, lead = call(
+    sent, lead_w3 = call(
         second_forward,
-        [VMEM] * 9,
-        [struct((chips, rows + 8, 128), BF16), own, slot_table],
+        [VMEM] * 7,
+        [struct((chips, rows + 8, 128), BF16), own],
         [wide, wide],
-        slot_v, v_map, exchange(sent, "x"), tile, own_w1, w2, u0, own_w2, own_u,
+        lead, exchange(sent, "x"), tile, early, own_w1, own_w2, own_u,
+    )
+    (placed,) = call(
+        functools.partial(aside_w3, span=span),
+        [VMEM] * 4,
+        [struct((n_row * 4, 128), F32)],
+        [],
+        lane_v, slot_v, lead, lead_w3,
     )
     (sent,) = call(
-        functools.partial(gather_sums, span=span),
-        [VMEM] * 6,
+        gather_sums,
+        [VMEM] * 3,
         [struct((n_row * 4, 128), BF16)],
-        [pltpu.VMEM((n_row * 4, 128), F32)],
-        exchange_col(sent), u_map, lane_v, slot_v, lead_w3, lead,
+        [],
+        exchange_col(sent), match, placed,
     )
     result, phi_bar = call(
         finish,

time: 122 us -> 125 us (1.025)
  blocking collectives: 98.1 us -> 79.8 us
  waiting for transfers between devices: 6.41 us -> 18.3 us
  starting transfers between devices: 7.65 us -> 14.5 us
  Pallas kernels: 5.78 us -> 9.37 us
    all_to_all x6 -> x4, blocking collectives: 81.8 us -> 63.5 us  [exchange(): return lax.all_to_all(sent, axis, split_axis=0, concat_axis=0, tiled=True)]
    all_to_all x1 -> x3, waiting for transfers between devices: 6.41 us -> 18.3 us  [exchange(): return lax.all_to_all(sent, axis, split_axis=0, concat_axis=0, tiled=True)]
    all_to_all x1 -> x3, starting transfers between devices: 7.65 us -> 14.5 us  [exchange(): return lax.all_to_all(sent, axis, split_axis=0, concat_axis=0, tiled=True)]
    pallas_call x8 -> x12, Pallas kernels: 5.78 us -> 9.37 us  [call(): pl.pallas_call(body, out_shape=outs, in_specs=specs, out_specs=[VMEM] * l...]
  transfers between devices with their start and end apart: 1 -> 3, of which waited for: 1 -> 3; matrix products, arithmetic and copies ran while one was open for 0% -> 0% of each run, Pallas kernels for 1% -> 2%
where the time goes in v7:
time: 125 us; the launch traced here: 124 us
  blocking collectives  79.8 us (64%)
  waiting for transfers between devices  18.3 us (15%)
  starting transfers between devices  14.5 us (12%)
  Pallas kernels  9.37 us (7%)
  between operations  1.35 us (1%)
    all_to_all x4, blocking collectives, exchange(): return lax.all_to_all(sent, axis, split_axis=0, concat_axis=0, tiled=True)  63.5 us
    all_to_all x3, waiting for transfers between devices, exchange(): return lax.all_to_all(sent, axis, split_axis=0, concat_axis=0, tiled=True)  18.3 us
    all_gather x3, blocking collectives, exchange_col(): return lax.all_gather(exchange(sent, 'y'), 'core', axis=0, tiled=True)  16.3 us
    all_to_all x3, starting transfers between devices, exchange(): return lax.all_to_all(sent, axis, split_axis=0, concat_axis=0, tiled=True)  14.5 us
    pallas_call x12, Pallas kernels, call(): pl.pallas_call(body, out_shape=outs, in_specs=specs, out_specs=[VMEM] * l...  9.37 us
  transfers between devices with their start and end apart: 3, of which 3 were waited for; matrix products, arithmetic and copies ran while one was open for 0% of the time, Pallas kernels for 2%

profile of v7, /device:TPU:1, one launch (start us, length us, event | category | flops | bytes accessed | tf_op | source)
XLA Modules:
  0.0 124.0 jit_solution(7371751389556192563)
XLA Ops:
  0.6 0.0 copy-start
  0.6 1.7 %shard_map.60 = (bf16[8,128,128]{2,1,0:T(8,128)(2,1)}, bf16[64,256]{1,0:T(8,128)(2,1)S(1)}) custom-call(f32[2,8192]{1,0:T(2,128)} %rhs_hbm.1), custom_call_target="tpu_custom_call" | custom-call | tf_op jit(solution)/shard_map/pallas_call | solution.py:379
  2.4 7.7 %all-to-all-start = ((bf16[8,128,128]{2,1,0:T(8,128)(2,1)}), bf16[8,128,128]{2,1,0:T(8,128)(2,1)S(1)}, u32[]{:S(2)}, u32[]{:S(2)}) async-start(bf16[8,128,128]{2,1,0:T(8,128)(2,1)} %get-tuple-element.27), calls=%async_computation | async-start | bytes 524288 | tf_op jit(solution)/shard_map/all_to_all | solution.py:389
  10.7 0.0 copy-start.1
  10.7 0.7 copy-done.1
  11.4 1.7 %shard_map.59 = (f32[32,128]{1,0:T(8,128)S(1)}, f32[32,128]{1,0:T(8,128)S(1)}, bf16[8,128]{1,0:T(8,128)(2,1)S(1)}, bf16[8,128]{1,0:T(8,128)(2,1)S(1)}, s32[2,32]{1,0:T(2,128)S(1)}) custom-call(s32[2,32]{1,0:T(2,128)S(1)} %bitcast.20, s32[1,1]{1,0:T(1,128)S(6)} %copy.8.counts_ref), custom_call_target="tpu_custom_call" | custom-call | tf_op jit(solution)/shard_map/pallas_call | solution.py:379
  13.0 6.4 %all-to-all-done = bf16[8,128,128]{2,1,0:T(8,128)(2,1)S(1)} async-done(((bf16[8,128,128]{2,1,0:T(8,128)(2,1)}), bf16[8,128,128]{2,1,0:T(8,128)(2,1)S(1)}, u32[]{:S(2)}, u32[]{:S(2)}) %all-to-all-start) | async-done | bytes 262176 | tf_op jit(solution)/shard_map/all_to_all | solution.py:389
  19.4 5.4 %all_gather.9 = bf16[16,128,128]{2,1,0:T(8,128)(2,1)S(1)} all-gather(bf16[8,128,128]{2,1,0:T(8,128)(2,1)S(1)} %all-to-all-done), channel_id=1, replica_groups=mesh['z'=8,'x'=4,'y'=8,'core'=2] {'core'}, dimensions={0}, use_global_device_ids=true | all-gather | bytes 786432 | tf_op jit(solution)/shard_map/all_gather | solution.py:392
  24.9 0.0 copy-done
  24.9 0.8 shard_map.61
  25.7 30.1 %all_to_all.35.got_ref = bf16[32,72,128]{2,1,0:T(8,128)(2,1)S(1)} all-to-all(bf16[32,72,128]{2,1,0:T(8,128)(2,1)S(1)} %get-tuple-element.28), channel_id=1, replica_groups=mesh['z'=8,'x'=4,'y'=8,'core'=2] {'z','x'}, dimensions={0} | all-to-all | bytes 1179648 | tf_op jit(solution)/shard_map/all_to_all | solution.py:389
  55.8 0.7 shard_map.62
  56.5 10.6 %all_to_all.36 = bf16[8,72,128]{2,1,0:T(8,128)(2,1)S(1)} all-to-all(bf16[8,72,128]{2,1,0:T(8,128)(2,1)S(1)} %get-tuple-element.34), channel_id=1, replica_groups=mesh['z'=8,'x'=4,'y'=8,'core'=2] {'y'}, dimensions={0} | all-to-all | bytes 294912 | tf_op jit(solution)/shard_map/all_to_all | solution.py:389
  67.1 5.1 %all_gather.10.got_ref = bf16[16,72,128]{2,1,0:T(8,128)(2,1)S(1)} all-gather(bf16[8,72,128]{2,1,0:T(8,128)(2,1)S(1)} %all_to_all.36), channel_id=1, replica_groups=mesh['z'=8,'x'=4,'y'=8,'core'=2] {'core'}, dimensions={0}, use_global_device_ids=true | all-gather | bytes 442368 | tf_op jit(solution)/shard_map/all_gather | solution.py:392
  72.1 0.5 shard_map.64
  72.6 11.1 %all_to_all.37.got_ref = bf16[8,72,128]{2,1,0:T(8,128)(2,1)S(1)} all-to-all(bf16[8,72,128]{2,1,0:T(8,128)(2,1)S(1)} %get-tuple-element.35), channel_id=1, replica_groups=mesh['z'=8,'x'=4,'y'=8,'core'=2] {'z'}, dimensions={0} | all-to-all | bytes 294912 | tf_op jit(solution)/shard_map/all_to_all | solution.py:389
  83.7 0.9 shard_map.65
  84.6 3.5 %all-to-all-start.4 = ((bf16[4,64,128]{2,1,0:T(8,128)(2,1)}), bf16[4,64,128]{2,1,0:T(8,128)(2,1)S(1)}, u32[]{:S(2)}, u32[]{:S(2)}) async-start(bf16[4,64,128]{2,1,0:T(8,128)(2,1)} %shard_map.65), calls=%async_computation.4 | async-start | bytes 131072 | tf_op jit(solution)/shard_map/all_to_all | solution.py:389
  88.1 0.2 shard_map.63
  88.3 0.3 shard_map.66
  88.6 3.9 %all-to-all-done.4.got_ref = bf16[4,64,128]{2,1,0:T(8,128)(2,1)S(1)} async-done(((bf16[4,64,128]{2,1,0:T(8,128)(2,1)}), bf16[4,64,128]{2,1,0:T(8,128)(2,1)S(1)}, u32[]{:S(2)}, u32[]{:S(2)}) %all-to-all-start.4) | async-done | bytes 65568 | tf_op jit(solution)/shard_map/all_to_all | solution.py:389
  92.6 1.2 shard_map.67
  93.8 3.4 %all-to-all-start.5 = ((bf16[8,72,128]{2,1,0:T(8,128)(2,1)}), bf16[8,72,128]{2,1,0:T(8,128)(2,1)S(1)}, u32[]{:S(2)}, u32[]{:S(2)}) async-start(bf16[8,72,128]{2,1,0:T(8,128)(2,1)} %get-tuple-element.43), calls=%async_computation.5 | async-start | bytes 294912 | tf_op jit(solution)/shard_map/all_to_all | solution.py:389
  97.2 0.1 shard_map.68.placed_ref
  97.3 7.9 %all-to-all-done.5 = bf16[8,72,128]{2,1,0:T(8,128)(2,1)S(1)} async-done(((bf16[8,72,128]{2,1,0:T(8,128)(2,1)}), bf16[8,72,128]{2,1,0:T(8,128)(2,1)S(1)}, u32[]{:S(2)}, u32[]{:S(2)}) %all-to-all-start.5) | async-done | bytes 147488 | tf_op jit(solution)/shard_map/all_to_all | solution.py:389
  105.2 5.8 %all_gather.11.got_ref = bf16[16,72,128]{2,1,0:T(8,128)(2,1)S(1)} all-gather(bf16[8,72,128]{2,1,0:T(8,128)(2,1)S(1)} %all-to-all-done.5), channel_id=1, replica_groups=mesh['z'=8,'x'=4,'y'=8,'core'=2] {'core'}, dimensions={0}, use_global_device_ids=true | all-gather | bytes 442368 | tf_op jit(solution)/shard_map/all_gather | solution.py:392
  111.0 0.4 shard_map.69
  111.4 11.7 %all_to_all.38 = bf16[32,4,128]{2,1,0:T(4,128)(2,1)S(1)} all-to-all(bf16[32,4,128]{2,1,0:T(4,128)(2,1)S(1)} %bitcast.18), channel_id=1, replica_groups=mesh['z'=8,'x'=4,'y'=8,'core'=2] {'z','x'}, dimensions={0} | all-to-all | bytes 65536 | tf_op jit(solution)/shard_map/all_to_all | solution.py:389
  123.1 0.9 shard_map.70
Async XLA Ops:
  0.6 24.2 %copy-start = (bf16[1,1,32,128,128]{4,3,2,1,0:T(8,128)(2,1)S(1)}, bf16[1,1,32,128,128]{4,3,2,1,0:T(8,128)(2,1)}, u32[]{:S(2)}) copy-start(bf16[1,1,32,128,128]{4,3,2,1,0:T(8,128)(2,1)} %param.4) | copy-start | bytes 3145732
  2.4 17.1 %all-to-all-start = ((bf16[8,128,128]{2,1,0:T(8,128)(2,1)}), bf16[8,128,128]{2,1,0:T(8,128)(2,1)S(1)}, u32[]{:S(2)}, u32[]{:S(2)}) async-start(bf16[8,128,128]{2,1,0:T(8,128)(2,1)} %get-tuple-element.27), calls=%async_computation | async-start | bytes 524288 | tf_op jit(solution)/shard_map/all_to_all | solution.py:389
  10.7 0.7 copy-start.1
  84.6 8.0 %all-to-all-start.4 = ((bf16[4,64,128]{2,1,0:T(8,128)(2,1)}), bf16[4,64,128]{2,1,0:T(8,128)(2,1)S(1)}, u32[]{:S(2)}, u32[]{:S(2)}) async-start(bf16[4,64,128]{2,1,0:T(8,128)(2,1)} %shard_map.65), calls=%async_computation.4 | async-start | bytes 131072 | tf_op jit(solution)/shard_map/all_to_all | solution.py:389
  93.8 11.4 %all-to-all-start.5 = ((bf16[8,72,128]{2,1,0:T(8,128)(2,1)}), bf16[8,72,128]{2,1,0:T(8,128)(2,1)S(1)}, u32[]{:S(2)}, u32[]{:S(2)}) async-start(bf16[8,72,128]{2,1,0:T(8,128)(2,1)} %get-tuple-element.43), calls=%async_computation.5 | async-start | bytes 294912 | tf_op jit(solution)/shard_map/all_to_all | solution.py:389

commit v8 on v5

--- a/solution.py
+++ b/solution.py
@@ -80,15 +80,13 @@
     return total
 
 
-def products(held_ref, tile_ref, out_ref, adjoint):
+def products(held_ref, tile_ref, out_ref):
     pair = iota((8, 128), 0) // 2
     for j in range(tile_ref.shape[0] // 4):
         rows = held_ref[8 * j : 8 * j + 8, :]
         left = jnp.concatenate([jnp.where(pair == i, rows, 0.0) for i in range(4)], axis=1).astype(BF16)
-        blocks = [tile_ref[4 * j + i] for i in range(4)]
-        right = jnp.concatenate(blocks, axis=0 if adjoint else 1)
-        dims = (((1,), (0 if adjoint else 1,)), ((), ()))
-        out_ref[8 * j : 8 * j + 8, :] = lax.dot_general(left, right, dims, preferred_element_type=F32)
+        right = jnp.concatenate([tile_ref[4 * j + i] for i in range(4)], axis=0)
+        out_ref[8 * j : 8 * j + 8, :] = jnp.dot(left, right, preferred_element_type=F32)
 
 
 def split_rows(ref):
@@ -110,12 +108,19 @@
             sent_ref[peer, rows:, :] = extra
 
 
+def begin(rhs_ref, sent_ref, piece_ref, rows):
+    for b in range(rows.shape[0] // 2):
+        rows[2 * b : 2 * b + 2, :] = rhs_ref[:, 128 * b : 128 * b + 128]
+    send_all(sent_ref, rows[...].astype(BF16), None)
+    half = rows.shape[0] // 2
+    piece_ref[...] = jnp.concatenate([rows[pl.ds(r, half, stride=2), :] for r in range(2)], axis=1).astype(BF16)
+
+
 def tables(
-    places_ref, counts_ref, piece_ref, slot_v_ref, slot_u_ref, lane_v_ref, lane_u_ref, u0_ref, fetch_ref, rows, spans
+    places_ref, counts_ref, tile_ref, slot_v_ref, slot_u_ref, lane_v_ref, lane_u_ref, turned_ref, fetch_ref, spans
 ):
-    rows[...] = piece_ref[...].astype(F32)
-    half = rows.shape[0] // 2
-    u0_ref[...] = jnp.concatenate([rows[pl.ds(r, half, stride=2), :] for r in range(2)], axis=1).astype(BF16)
+    for k in range(tile_ref.shape[0]):
+        turned_ref[k] = jnp.transpose(tile_ref[k])
     count = counts_ref[0, 0]
     for axis, slot_ref, lane_ref in ((0, slot_u_ref, lane_u_ref), (1, slot_v_ref, lane_v_ref)):
         slot_ref[...] = slot_keys(places_ref, count, axis)
@@ -132,7 +137,7 @@
     for k in range(fetch_ref.shape[1]):
         held[2 * k : 2 * k + 2, :] = u_ref[fetch_ref[0, k]].astype(F32) * fetch_ref[1, k].astype(F32)
     own_u_ref[...] = split_rows(held).astype(BF16)
-    products(held, tile_ref, out, True)
+    products(held, tile_ref, out)
     send_all(sent_ref, split_rows(out).astype(BF16), lane_ref[...])
 
 
@@ -145,11 +150,11 @@
     w_ref[...] = jnp.concatenate([own[:, 0:128], own[:, 128:256]], axis=0)
 
 
-def first_forward(slot_ref, lane_ref, got_ref, tile_ref, sent_ref, w_ref, piece_ref, map_ref, held, out):
+def first_forward(slot_ref, lane_ref, got_ref, turned_ref, sent_ref, w_ref, piece_ref, map_ref, held, out):
     read_keys(got_ref, map_ref)
     keys = with_range(slot_ref, row_index(), piece_ref.shape[0])
     keep(sum_by_key(got_ref, map_ref, keys), w_ref, piece_ref, held)
-    products(held, tile_ref, out, False)
+    products(held, turned_ref, out)
     send_all(sent_ref, split_rows(out).astype(BF16), lane_ref[...])
 
 
@@ -157,7 +162,7 @@
     read_keys(got_ref, map_ref)
     keys = with_range(slot_ref, col_index(), piece_ref.shape[0])
     keep(sum_by_key(got_ref, map_ref, keys), w_ref, piece_ref, held)
-    products(held, tile_ref, out, True)
+    products(held, tile_ref, out)
     send_all(sent_ref, split_rows(out).astype(BF16), lane_ref[...])
 
 
@@ -211,7 +216,7 @@
 
 
 def second_forward(
-    slot_ref, map_ref, got_ref, tile_ref, own_w1_ref, w2_ref, u0_ref, own_w2_ref, own_u_ref,
+    slot_ref, map_ref, got_ref, turned_ref, own_w1_ref, w2_ref, u0_ref, own_w2_ref, own_u_ref,
     sent_ref, lead_w3_ref, lead_ref, held, out,
 ):
     w3 = got_ref[0].astype(F32)
@@ -221,7 +226,7 @@
     half = w3.shape[0] // 2
     for r in range(2):
         held[pl.ds(r, half, stride=2), :] = w3[half * r : half * r + half, :]
-    products(held, tile_ref, out, False)
+    products(held, turned_ref, out)
     sent = split_rows(out).astype(BF16)
     lead = leaders(map_ref, slot_ref, row_index())
     lead_ref[...] = lead
@@ -375,16 +380,21 @@
     slot_table = struct((slots, 128), F32)
     lane_table = struct((8, 128), BF16)
     tile = tiles[0, 0]
-    pairs = rhs.reshape(2, span, 128).transpose(1, 0, 2).reshape(2 * span, 128).astype(BF16)
-    slot_v, slot_u, lane_v, lane_u, u0, fetch = call(
+    sent, u0 = call(
+        begin,
+        [VMEM],
+        [struct((chips, 2 * span, 128), BF16), piece],
+        [pltpu.VMEM((2 * span, 128), F32)],
+        rhs,
+    )
+    slot_v, slot_u, lane_v, lane_u, turned, fetch = call(
         functools.partial(tables, spans=(span, chips, lax.axis_size("core"))),
         [SMEM, SMEM, VMEM],
-        [slot_table, slot_table, lane_table, lane_table, piece, struct((2, slots), jnp.int32)],
-        [pltpu.VMEM((2 * span, 128), F32)],
-        places, counts, pairs,
+        [slot_table, slot_table, lane_table, lane_table, struct(tile.shape, BF16), struct((2, slots), jnp.int32)],
+        [],
+        places, counts, tile,
         out_specs=[VMEM] * 5 + [SMEM],
     )
-    sent = jnp.broadcast_to(pairs[None], (chips, 2 * span, 128))
     u_group = exchange_col(sent).reshape(n_col * span, 2, 128)
     sent, own_u = call(
         first_adjoint,
@@ -398,7 +408,7 @@
         [VMEM] * 4,
         [struct((chips, rows + 8, 128), BF16), own, piece, struct((n_row // 4, 128), F32)],
         [wide, wide],
-        slot_v, lane_u, exchange(sent, ROW), tile,
+        slot_v, lane_u, exchange(sent, ROW), turned,
     )
     sent, own_w2, w2, u_map = call(
         second_adjoint,
@@ -419,7 +429,7 @@
         [VMEM] * 9,
         [struct((chips, rows + 8, 128), BF16), own, slot_table],
         [wide, wide],
-        slot_v, v_map, exchange(sent, "x"), tile, own_w1, w2, u0, own_w2, own_u,
+        slot_v, v_map, exchange(sent, "x"), turned, own_w1, w2, u0, own_w2, own_u,
     )
     (sent,) = call(
         functools.partial(gather_sums, span=span),

time: 122 us -> 122 us (level)
  waiting for transfers between devices: 6.41 us -> 4.96 us
  local copies, waits for them, and re-layouts: 1.41 us -> 2.73 us
    unnamed x4 -> x8, local copies, waits for them, and re-layouts: 0.68 us -> 2.73 us
    all_to_all x1, waiting for transfers between devices: 6.41 us -> 4.96 us  [exchange(): return lax.all_to_all(sent, axis, split_axis=0, concat_axis=0, tiled=True)]
    pallas_call x8 -> x9, Pallas kernels: 5.78 us -> 6.48 us  [call(): pl.pallas_call(body, out_shape=outs, in_specs=specs, out_specs=[VMEM] * l...]
  transfers between devices with their start and end apart: 1 -> 1, of which waited for: 1 -> 1; matrix products, arithmetic and copies ran while one was open for 0% -> 0% of each run, Pallas kernels for 1% -> 2%
where the time goes in v8:
time: 122 us; the launch traced here: 121 us
  blocking collectives  98.1 us (80%)
  starting transfers between devices  7.65 us (6%)
  Pallas kernels  6.48 us (5%)
  waiting for transfers between devices  4.96 us (4%)
  local copies, waits for them, and re-layouts  2.73 us (2%)
  between operations  1.34 us (1%)
    all_to_all x6, blocking collectives, exchange(): return lax.all_to_all(sent, axis, split_axis=0, concat_axis=0, tiled=True)  81.8 us
    all_gather x3, blocking collectives, exchange_col(): return lax.all_gather(exchange(sent, 'y'), 'core', axis=0, tiled=True)  16.3 us
    all_to_all x1, starting transfers between devices, exchange(): return lax.all_to_all(sent, axis, split_axis=0, concat_axis=0, tiled=True)  7.65 us
    pallas_call x9, Pallas kernels, call(): pl.pallas_call(body, out_shape=outs, in_specs=specs, out_specs=[VMEM] * l...  6.48 us
    all_to_all x1, waiting for transfers between devices, exchange(): return lax.all_to_all(sent, axis, split_axis=0, concat_axis=0, tiled=True)  4.96 us
    unnamed x8, local copies, waits for them, and re-layouts  2.73 us
  transfers between devices with their start and end apart: 1, of which 1 were waited for; matrix products, arithmetic and copies ran while one was open for 0% of the time, Pallas kernels for 2%

profile of v8, /device:TPU:1, one launch (start us, length us, event | category | flops | bytes accessed | tf_op | source)
XLA Modules:
  0.0 121.2 jit_solution(2581340232869568940)
XLA Ops:
  0.6 0.0 copy-start.2
  0.6 0.8 copy-done.2
  1.5 0.7 shard_map.60
  2.2 7.7 %all-to-all-start = ((bf16[8,128,128]{2,1,0:T(8,128)(2,1)}), bf16[8,128,128]{2,1,0:T(8,128)(2,1)S(1)}, u32[]{:S(2)}, u32[]{:S(2)}) async-start(bf16[8,128,128]{2,1,0:T(8,128)(2,1)} %get-tuple-element.29), calls=%async_computation | async-start | bytes 524288 | tf_op jit(solution)/shard_map/all_to_all | solution.py:372
  10.5 0.0 copy-start.3
  10.5 0.7 copy-done.3
  11.2 0.0 copy-start
  11.2 1.2 %copy-done = bf16[1,1,32,128,128]{4,3,2,1,0:T(8,128)(2,1)S(1)} copy-done((bf16[1,1,32,128,128]{4,3,2,1,0:T(8,128)(2,1)S(1)}, bf16[1,1,32,128,128]{4,3,2,1,0:T(8,128)(2,1)}, u32[]{:S(2)}) %copy-start) | copy-done | bytes 1048600
  12.4 0.0 copy-start.1
  12.4 1.9 %shard_map.59 = (f32[32,128]{1,0:T(8,128)S(1)}, f32[32,128]{1,0:T(8,128)S(1)}, bf16[8,128]{1,0:T(8,128)(2,1)S(1)}, bf16[8,128]{1,0:T(8,128)(2,1)S(1)}, bf16[32,1...) custom-call(s32[2,32]{1,0:T(2,128)S(1)} %bitcast.19, s32[1,1]{1,0:T(1,128)S(6)} %copy.8.counts_ref, ...), custom_call_target="tpu_custom_call" | custom-call | tf_op jit(solution)/shard_map/pallas_call | solution.py:362
  14.3 5.0 %all-to-all-done = bf16[8,128,128]{2,1,0:T(8,128)(2,1)S(1)} async-done(((bf16[8,128,128]{2,1,0:T(8,128)(2,1)}), bf16[8,128,128]{2,1,0:T(8,128)(2,1)S(1)}, u32[]{:S(2)}, u32[]{:S(2)}) %all-to-all-start) | async-done | bytes 262176 | tf_op jit(solution)/shard_map/all_to_all | solution.py:372
  19.3 5.4 %all_gather.9 = bf16[16,128,128]{2,1,0:T(8,128)(2,1)S(1)} all-gather(bf16[8,128,128]{2,1,0:T(8,128)(2,1)S(1)} %all-to-all-done), channel_id=1, replica_groups=mesh['z'=8,'x'=4,'y'=8,'core'=2] {'core'}, dimensions={0}, use_global_device_ids=true | all-gather | bytes 786432 | tf_op jit(solution)/shard_map/all_gather | solution.py:375
  24.7 0.0 copy-done.1
  24.7 0.8 shard_map.61
  25.5 30.1 %all_to_all.35.got_ref = bf16[32,72,128]{2,1,0:T(8,128)(2,1)S(1)} all-to-all(bf16[32,72,128]{2,1,0:T(8,128)(2,1)S(1)} %get-tuple-element.30), channel_id=1, replica_groups=mesh['z'=8,'x'=4,'y'=8,'core'=2] {'z','x'}, dimensions={0} | all-to-all | bytes 1179648 | tf_op jit(solution)/shard_map/all_to_all | solution.py:372
  55.6 0.6 shard_map.62
  56.2 10.6 %all_to_all.36 = bf16[8,72,128]{2,1,0:T(8,128)(2,1)S(1)} all-to-all(bf16[8,72,128]{2,1,0:T(8,128)(2,1)S(1)} %get-tuple-element.34), channel_id=1, replica_groups=mesh['z'=8,'x'=4,'y'=8,'core'=2] {'y'}, dimensions={0} | all-to-all | bytes 294912 | tf_op jit(solution)/shard_map/all_to_all | solution.py:372
  66.8 5.0 %all_gather.10.got_ref = bf16[16,72,128]{2,1,0:T(8,128)(2,1)S(1)} all-gather(bf16[8,72,128]{2,1,0:T(8,128)(2,1)S(1)} %all_to_all.36), channel_id=1, replica_groups=mesh['z'=8,'x'=4,'y'=8,'core'=2] {'core'}, dimensions={0}, use_global_device_ids=true | all-gather | bytes 442368 | tf_op jit(solution)/shard_map/all_gather | solution.py:375
  71.8 0.5 shard_map.63
  72.3 11.2 %all_to_all.37.got_ref = bf16[8,72,128]{2,1,0:T(8,128)(2,1)S(1)} all-to-all(bf16[8,72,128]{2,1,0:T(8,128)(2,1)S(1)} %get-tuple-element.35), channel_id=1, replica_groups=mesh['z'=8,'x'=4,'y'=8,'core'=2] {'z'}, dimensions={0} | all-to-all | bytes 294912 | tf_op jit(solution)/shard_map/all_to_all | solution.py:372
  83.5 0.2 shard_map.64
  83.7 7.8 %all_to_all.38.got_ref = bf16[4,64,128]{2,1,0:T(8,128)(2,1)S(1)} all-to-all(bf16[4,64,128]{2,1,0:T(8,128)(2,1)S(1)} %shard_map.64), channel_id=1, replica_groups=mesh['z'=8,'x'=4,'y'=8,'core'=2] {'x'}, dimensions={0} | all-to-all | bytes 131072 | tf_op jit(solution)/shard_map/all_to_all | solution.py:372
  91.5 0.4 shard_map.65
  91.9 10.5 %all_to_all.39 = bf16[8,72,128]{2,1,0:T(8,128)(2,1)S(1)} all-to-all(bf16[8,72,128]{2,1,0:T(8,128)(2,1)S(1)} %get-tuple-element.41), channel_id=1, replica_groups=mesh['z'=8,'x'=4,'y'=8,'core'=2] {'y'}, dimensions={0} | all-to-all | bytes 294912 | tf_op jit(solution)/shard_map/all_to_all | solution.py:372
  102.4 5.8 %all_gather.11.got_ref = bf16[16,72,128]{2,1,0:T(8,128)(2,1)S(1)} all-gather(bf16[8,72,128]{2,1,0:T(8,128)(2,1)S(1)} %all_to_all.39), channel_id=1, replica_groups=mesh['z'=8,'x'=4,'y'=8,'core'=2] {'core'}, dimensions={0}, use_global_device_ids=true | all-gather | bytes 442368 | tf_op jit(solution)/shard_map/all_gather | solution.py:375
  108.2 0.5 shard_map.66
  108.7 11.7 %all_to_all.40 = bf16[32,4,128]{2,1,0:T(4,128)(2,1)S(1)} all-to-all(bf16[32,4,128]{2,1,0:T(4,128)(2,1)S(1)} %bitcast.17), channel_id=1, replica_groups=mesh['z'=8,'x'=4,'y'=8,'core'=2] {'z','x'}, dimensions={0} | all-to-all | bytes 65536 | tf_op jit(solution)/shard_map/all_to_all | solution.py:372
  120.3 0.9 shard_map.67
Async XLA Ops:
  0.6 0.8 copy-start.2
  2.2 17.1 %all-to-all-start = ((bf16[8,128,128]{2,1,0:T(8,128)(2,1)}), bf16[8,128,128]{2,1,0:T(8,128)(2,1)S(1)}, u32[]{:S(2)}, u32[]{:S(2)}) async-start(bf16[8,128,128]{2,1,0:T(8,128)(2,1)} %get-tuple-element.29), calls=%async_computation | async-start | bytes 524288 | tf_op jit(solution)/shard_map/all_to_all | solution.py:372
  10.5 0.7 copy-start.3
  11.2 1.2 %copy-start = (bf16[1,1,32,128,128]{4,3,2,1,0:T(8,128)(2,1)S(1)}, bf16[1,1,32,128,128]{4,3,2,1,0:T(8,128)(2,1)}, u32[]{:S(2)}) copy-start(bf16[1,1,32,128,128]{4,3,2,1,0:T(8,128)(2,1)} %param.4) | copy-start | bytes 3145732
  12.4 12.3 %copy-start.1 = (bf16[1,1,32,128,128]{4,3,2,1,0:T(8,128)(2,1)S(1)}, bf16[1,1,32,128,128]{4,3,2,1,0:T(8,128)(2,1)}, u32[]{:S(2)}) copy-start(bf16[1,1,32,128,128]{4,3,2,1,0:T(8,128)(2,1)} %param.4) | copy-start | bytes 3145732

commit v9 on v8

--- a/solution.py
+++ b/solution.py
@@ -29,12 +29,13 @@
     return lax.axis_index("y") * lax.axis_size("core") + lax.axis_index("core")
 
 
-def slot_keys(places_ref, count, axis):
-    slots = places_ref.shape[1]
+def slot_keys(sorted_ref, axis):
+    slots = sorted_ref.shape[1]
     row = iota((slots, 128), 0)
     keys = jnp.full((slots, 128), -8, jnp.int32)
     for k in range(slots):
-        keys = jnp.where(row == k, jnp.where(k < count, places_ref[axis, k], -8), keys)
+        block = sorted_ref[axis, k]
+        keys = jnp.where(row == k, jnp.where(block < 0, -8, block), keys)
     return keys.astype(F32)
 
 
@@ -42,12 +43,12 @@
     return jnp.concatenate([slot_ref[...], (me * span + iota((span, 128), 0)).astype(F32)], axis=0)
 
 
-def lane_keys(places_ref, count, axis):
-    slots = places_ref.shape[1]
+def lane_keys(sorted_ref, axis):
+    slots = sorted_ref.shape[1]
     slot = iota((8, 128), 1) % slots
     keys = jnp.full((8, 128), -1, jnp.int32)
     for k in range(slots):
-        keys = jnp.where(slot == k, jnp.where(k < count, places_ref[axis, k], -1), keys)
+        keys = jnp.where(slot == k, sorted_ref[axis, k], keys)
     keys = keys.astype(F32)
     high = jnp.floor(keys * (1.0 / 64.0))
     sub = iota((8, 128), 0)
@@ -117,20 +118,32 @@
 
 
 def tables(
-    places_ref, counts_ref, tile_ref, slot_v_ref, slot_u_ref, lane_v_ref, lane_u_ref, turned_ref, fetch_ref, spans
+    places_ref, counts_ref, tile_ref,
+    slot_v_ref, slot_u_ref, lane_v_ref, lane_u_ref, held_ref, turned_ref, fetch_ref, order_ref, sorted_ref, spans,
 ):
-    for k in range(tile_ref.shape[0]):
-        turned_ref[k] = jnp.transpose(tile_ref[k])
     count = counts_ref[0, 0]
-    for axis, slot_ref, lane_ref in ((0, slot_u_ref, lane_u_ref), (1, slot_v_ref, lane_v_ref)):
-        slot_ref[...] = slot_keys(places_ref, count, axis)
-        lane_ref[...] = lane_keys(places_ref, count, axis)
     span, chips, cores = spans
-    for k in range(places_ref.shape[1]):
+    slots = places_ref.shape[1]
+    seen = jnp.int32(0)
+    for k in range(slots):
+        odd = (places_ref[0, k] // span) % 2
+        order_ref[jnp.where(odd == 1, slots // 2 + seen, k - seen)] = k
+        seen = seen + odd
+    for i in range(slots):
+        k = order_ref[i]
+        held_ref[i] = tile_ref[k]
+        turned_ref[i] = jnp.transpose(tile_ref[k])
         block = places_ref[0, k]
         owner = block // span
-        fetch_ref[0, k] = ((owner % cores) * chips + owner // cores) * span + block % span
-        fetch_ref[1, k] = (k < count).astype(jnp.int32)
+        used = k < count
+        sorted_ref[0, i] = jnp.where(used, block, -1)
+        sorted_ref[1, i] = jnp.where(used, places_ref[1, k], -1)
+        fetch_ref[0, i] = ((owner % cores) * chips + owner // cores) * span + block % span
+        fetch_ref[1, i] = used.astype(jnp.int32)
+    slot_u_ref[...] = slot_keys(sorted_ref, 0)
+    slot_v_ref[...] = slot_keys(sorted_ref, 1)
+    lane_u_ref[...] = lane_keys(sorted_ref, 0)
+    lane_v_ref[...] = lane_keys(sorted_ref, 1)
 
 
 def first_adjoint(fetch_ref, lane_ref, u_ref, tile_ref, sent_ref, own_u_ref, held, out):
@@ -251,17 +264,38 @@
     block = jnp.zeros((8, 128), F32)
     for j, value in enumerate(sums):
         block = jnp.where(lane == j, value, block)
-    send_all(sent_ref, sent, three_parts(block).astype(BF16))
+    block = three_parts(block).astype(BF16)
+    chips = sent_ref.shape[0] // 2
+    for core in range(2):
+        for r in range(2):
+            values = sent[half * r + half // 2 * core : half * r + half // 2 * core + half // 2, :]
+            for chip in range(chips):
+                sent_ref[core * chips + chip, half // 2 * r : half // 2 * r + half // 2, :] = values
+        for chip in range(chips):
+            sent_ref[core * chips + chip, half:, :] = block
+
+
+def half_slots(got_ref, g):
+    core = lax.axis_index("core")
+    halves = []
+    for r in range(2):
+        for i in range(4):
+            values = got_ref[4 * g + i, 16 * r : 16 * r + 16, :]
+            zeros = jnp.zeros_like(values)
+            halves += [jnp.where(core == 0, values, zeros), jnp.where(core == 0, zeros, values)]
+    return jnp.concatenate([jnp.concatenate(halves[0:8], axis=0), jnp.concatenate(halves[8:16], axis=0)], axis=1)
 
 
 def gather_sums(got_ref, map_ref, lane_ref, slot_ref, lead_w3_ref, lead_ref, sent_ref, wide, span):
     peers = got_ref.shape[0]
     rows = got_ref.shape[1] - 8
+    core = lax.axis_index("core")
     partial = got_ref[0, rows:, :].astype(F32)
     for peer in range(1, peers):
         partial = partial + got_ref[peer, rows:, :].astype(F32)
+    partial = jnp.where(core == 0, partial, 0.0)
     groups = peers // 4
-    values = jnp.concatenate([four_peers(got_ref, g) for g in range(groups)], axis=0)
+    values = jnp.concatenate([half_slots(got_ref, g) for g in range(groups)], axis=0)
     square = jnp.zeros((8, 256), F32)
     for g in range(groups):
         column = jnp.transpose(jnp.broadcast_to(map_ref[g : g + 1, :], (128, 128)))
@@ -272,7 +306,7 @@
     block = jnp.where(lane == 8, sum_piece(square), whole_sums(partial))
     block = block + pltpu.roll(block, 1, 0)
     block = three_parts(block + pltpu.roll(block, 2, 0))
-    owners = sent_ref.shape[0] // 4
+    owners = sent_ref.shape[0] // 8
     slots = slot_ref.shape[0]
     keys = slot_ref[...]
     label = (keys - span * jnp.floor(keys * (1.0 / span)) + 1.0) * lead_ref[...]
@@ -282,17 +316,19 @@
     values = jnp.concatenate([values, jnp.zeros((128 - slots, 384), BF16)], axis=0)
     match = (iota((owners, 128), 0) == lane_ref[...].astype(jnp.int32)[0:1, :]) & (iota((owners, 128), 1) < slots)
     placed = jnp.dot(match.astype(F32).astype(BF16), values, preferred_element_type=F32)
-    wide[pl.ds(0, owners, stride=4), :] = placed[:, 0:128]
-    wide[pl.ds(1, owners, stride=4), :] = placed[:, 128:256]
-    wide[pl.ds(2, owners, stride=4), :] = placed[:, 256:384] + block[3:4, :]
-    wide[pl.ds(3, owners, stride=4), :] = jnp.broadcast_to(block[7:8, :], (owners, 128))
+    for to in range(2):
+        mine = [jnp.where(core == to, placed[:, 128 * i : 128 * i + 128], 0.0) for i in range(3)]
+        wide[pl.ds(4 * to, owners, stride=8), :] = mine[0]
+        wide[pl.ds(4 * to + 1, owners, stride=8), :] = mine[1]
+        wide[pl.ds(4 * to + 2, owners, stride=8), :] = mine[2] + block[3:4, :]
+        wide[pl.ds(4 * to + 3, owners, stride=8), :] = jnp.broadcast_to(block[7:8, :], (owners, 128))
     sent_ref[...] = wide[...].astype(BF16)
 
 
 def finish(got_ref, w1_ref, solution_ref, phi_ref, wide):
     wide[...] = got_ref[...].astype(F32)
-    peers = got_ref.shape[0] // 4
-    parts = [wide[pl.ds(i, peers, stride=4), :] for i in range(4)]
+    peers = got_ref.shape[0] // 8
+    parts = [wide[pl.ds(i, peers, stride=8), :] + wide[pl.ds(4 + i, peers, stride=8), :] for i in range(4)]
     total = jnp.concatenate([jnp.sum(parts[i], axis=0, keepdims=True) for i in (2, 3)], axis=0)
     half = w1_ref.shape[0]
     labels = pltpu.roll(jnp.broadcast_to(total[0:1, :], (half, 128)), 64, 1)
@@ -387,13 +423,13 @@
         [pltpu.VMEM((2 * span, 128), F32)],
         rhs,
     )
-    slot_v, slot_u, lane_v, lane_u, turned, fetch = call(
+    slot_v, slot_u, lane_v, lane_u, held, turned, fetch = call(
         functools.partial(tables, spans=(span, chips, lax.axis_size("core"))),
         [SMEM, SMEM, VMEM],
-        [slot_table, slot_table, lane_table, lane_table, struct(tile.shape, BF16), struct((2, slots), jnp.int32)],
-        [],
+        [slot_table] * 2 + [lane_table] * 2 + [struct(tile.shape, BF16)] * 2 + [struct((2, slots), jnp.int32)],
+        [pltpu.SMEM((slots,), jnp.int32), pltpu.SMEM((2, slots), jnp.int32)],
         places, counts, tile,
-        out_specs=[VMEM] * 5 + [SMEM],
+        out_specs=[VMEM] * 6 + [SMEM],
     )
     u_group = exchange_col(sent).reshape(n_col * span, 2, 128)
     sent, own_u = call(
@@ -401,7 +437,7 @@
         [SMEM] + [VMEM] * 3,
         [struct((n_row, rows + 8, 128), BF16), own],
         [wide, wide],
-        fetch, lane_v, u_group, tile,
+        fetch, lane_v, u_group, held,
     )
     sent, own_w1, w1, v_map = call(
         first_forward,
@@ -415,7 +451,7 @@
         [VMEM] * 4,
         [struct((lax.axis_size("z"), rows + 8, 128), BF16), own, piece, struct((n_col // 4, 128), F32)],
         [wide, wide],
-        slot_u, lane_v, exchange_col(sent), tile,
+        slot_u, lane_v, exchange_col(sent), held,
     )
     (sent,) = call(
         regroup,
@@ -427,23 +463,23 @@
     sent, lead_w3, lead = call(
         second_forward,
         [VMEM] * 9,
-        [struct((chips, rows + 8, 128), BF16), own, slot_table],
+        [struct((n_col, slots + 8, 128), BF16), own, slot_table],
         [wide, wide],
         slot_v, v_map, exchange(sent, "x"), turned, own_w1, w2, u0, own_w2, own_u,
     )
     (sent,) = call(
         functools.partial(gather_sums, span=span),
         [VMEM] * 6,
-        [struct((n_row * 4, 128), BF16)],
-        [pltpu.VMEM((n_row * 4, 128), F32)],
-        exchange_col(sent), u_map, lane_v, slot_v, lead_w3, lead,
+        [struct((n_row * 8, 128), BF16)],
+        [pltpu.VMEM((n_row * 8, 128), F32)],
+        exchange(sent, ("core", "y")), u_map, lane_v, slot_v, lead_w3, lead,
     )
     result, phi_bar = call(
         finish,
         [VMEM] * 2,
         [struct((2 * span, 128), F32), struct((1, 2), F32)],
-        [pltpu.VMEM((n_row * 4, 128), F32)],
-        exchange(sent.reshape(n_row, 4, 128), ROW).reshape(n_row * 4, 128), w1,
+        [pltpu.VMEM((n_row * 8, 128), F32)],
+        exchange(sent.reshape(n_row * 2, 4, 128), ROW + ("core",)).reshape(n_row * 8, 128), w1,
     )
     result = result.reshape(span, 2, 128).transpose(1, 0, 2).reshape(2, span * 128)
     return (result, phi_bar.reshape(2))

time: 122 us -> 121 us (level)
    all_gather x3 -> x2, blocking collectives: 16.3 us -> 10.5 us  [exchange_col(): return lax.all_gather(exchange(sent, 'y'), 'core', axis=0, tiled=True)]
    all_to_all x6, blocking collectives: 81.8 us -> 87.2 us  [exchange(): return lax.all_to_all(sent, axis, split_axis=0, concat_axis=0, tiled=True)]
    unnamed x8 -> x6, local copies, waits for them, and re-layouts: 2.73 us -> 2.73 us
where the time goes in v9:
time: 121 us
  blocking collectives  97.7 us (81%)
  starting transfers between devices  7.65 us (6%)
  Pallas kernels  6.7 us (6%)
  waiting for transfers between devices  4.75 us (4%)
  local copies, waits for them, and re-layouts  2.73 us (2%)
  between operations  1.34 us (1%)
    all_to_all x6, blocking collectives, exchange(): return lax.all_to_all(sent, axis, split_axis=0, concat_axis=0, tiled=True)  87.2 us
    all_gather x2, blocking collectives, exchange_col(): return lax.all_gather(exchange(sent, 'y'), 'core', axis=0, tiled=True)  10.5 us
    all_to_all x1, starting transfers between devices, exchange(): return lax.all_to_all(sent, axis, split_axis=0, concat_axis=0, tiled=True)  7.65 us
    pallas_call x9, Pallas kernels, call(): pl.pallas_call(body, out_shape=outs, in_specs=specs, out_specs=[VMEM] * l...  6.7 us
    all_to_all x1, waiting for transfers between devices, exchange(): return lax.all_to_all(sent, axis, split_axis=0, concat_axis=0, tiled=True)  4.75 us
    unnamed x6, local copies, waits for them, and re-layouts  2.73 us
  transfers between devices with their start and end apart: 1, of which 1 were waited for; matrix products, arithmetic and copies ran while one was open for 0% of the time, Pallas kernels for 2%

profile of v9, /device:TPU:1, one launch (start us, length us, event | category | flops | bytes accessed | tf_op | source)
XLA Modules:
  0.0 120.9 jit_solution(633570559381128936)
XLA Ops:
  0.6 0.0 copy-start.1
  0.6 0.8 copy-done.1
  1.5 0.7 shard_map.60
  2.2 7.7 %all-to-all-start = ((bf16[8,128,128]{2,1,0:T(8,128)(2,1)}), bf16[8,128,128]{2,1,0:T(8,128)(2,1)S(1)}, u32[]{:S(2)}, u32[]{:S(2)}) async-start(bf16[8,128,128]{2,1,0:T(8,128)(2,1)} %get-tuple-element.30), calls=%async_computation | async-start | bytes 524288 | tf_op jit(solution)/shard_map/all_to_all | solution.py:408
  10.5 0.0 copy-start.2
  10.5 0.7 copy-done.2
  11.2 0.0 copy-start
  11.2 1.2 %copy-done = bf16[1,1,32,128,128]{4,3,2,1,0:T(8,128)(2,1)S(1)} copy-done((bf16[1,1,32,128,128]{4,3,2,1,0:T(8,128)(2,1)S(1)}, bf16[1,1,32,128,128]{4,3,2,1,0:T(8,128)(2,1)}, u32[]{:S(2)}) %copy-start) | copy-done | bytes 1048600
  12.4 2.1 %shard_map.59 = (f32[32,128]{1,0:T(8,128)S(1)}, f32[32,128]{1,0:T(8,128)S(1)}, bf16[8,128]{1,0:T(8,128)(2,1)S(1)}, bf16[8,128]{1,0:T(8,128)(2,1)S(1)}, bf16[32,1...) custom-call(s32[2,32]{1,0:T(2,128)S(1)} %bitcast.17, s32[1,1]{1,0:T(1,128)S(6)} %copy.8.counts_ref, ...), custom_call_target="tpu_custom_call" | custom-call | tf_op jit(solution)/shard_map/pallas_call | solution.py:398
  14.5 4.8 %all-to-all-done = bf16[8,128,128]{2,1,0:T(8,128)(2,1)S(1)} async-done(((bf16[8,128,128]{2,1,0:T(8,128)(2,1)}), bf16[8,128,128]{2,1,0:T(8,128)(2,1)S(1)}, u32[]{:S(2)}, u32[]{:S(2)}) %all-to-all-start) | async-done | bytes 262176 | tf_op jit(solution)/shard_map/all_to_all | solution.py:408
  19.3 5.4 %all_gather.6 = bf16[16,128,128]{2,1,0:T(8,128)(2,1)S(1)} all-gather(bf16[8,128,128]{2,1,0:T(8,128)(2,1)S(1)} %all-to-all-done), channel_id=1, replica_groups=mesh['z'=8,'x'=4,'y'=8,'core'=2] {'core'}, dimensions={0}, use_global_device_ids=true | all-gather | bytes 786432 | tf_op jit(solution)/shard_map/all_gather | solution.py:411
  24.7 0.8 shard_map.61
  25.5 30.1 %all_to_all.35.got_ref = bf16[32,72,128]{2,1,0:T(8,128)(2,1)S(1)} all-to-all(bf16[32,72,128]{2,1,0:T(8,128)(2,1)S(1)} %get-tuple-element.32), channel_id=1, replica_groups=mesh['z'=8,'x'=4,'y'=8,'core'=2] {'z','x'}, dimensions={0} | all-to-all | bytes 1179648 | tf_op jit(solution)/shard_map/all_to_all | solution.py:408
  55.6 0.6 shard_map.62
  56.2 10.6 %all_to_all.36 = bf16[8,72,128]{2,1,0:T(8,128)(2,1)S(1)} all-to-all(bf16[8,72,128]{2,1,0:T(8,128)(2,1)S(1)} %get-tuple-element.36), channel_id=1, replica_groups=mesh['z'=8,'x'=4,'y'=8,'core'=2] {'y'}, dimensions={0} | all-to-all | bytes 294912 | tf_op jit(solution)/shard_map/all_to_all | solution.py:408
  66.8 5.1 %all_gather.7.got_ref = bf16[16,72,128]{2,1,0:T(8,128)(2,1)S(1)} all-gather(bf16[8,72,128]{2,1,0:T(8,128)(2,1)S(1)} %all_to_all.36), channel_id=1, replica_groups=mesh['z'=8,'x'=4,'y'=8,'core'=2] {'core'}, dimensions={0}, use_global_device_ids=true | all-gather | bytes 442368 | tf_op jit(solution)/shard_map/all_gather | solution.py:411
  71.9 0.5 shard_map.63
  72.3 11.1 %all_to_all.37.got_ref = bf16[8,72,128]{2,1,0:T(8,128)(2,1)S(1)} all-to-all(bf16[8,72,128]{2,1,0:T(8,128)(2,1)S(1)} %get-tuple-element.37), channel_id=1, replica_groups=mesh['z'=8,'x'=4,'y'=8,'core'=2] {'z'}, dimensions={0} | all-to-all | bytes 294912 | tf_op jit(solution)/shard_map/all_to_all | solution.py:408
  83.5 0.2 shard_map.64
  83.7 7.8 %all_to_all.38.got_ref = bf16[4,64,128]{2,1,0:T(8,128)(2,1)S(1)} all-to-all(bf16[4,64,128]{2,1,0:T(8,128)(2,1)S(1)} %shard_map.64), channel_id=1, replica_groups=mesh['z'=8,'x'=4,'y'=8,'core'=2] {'x'}, dimensions={0} | all-to-all | bytes 131072 | tf_op jit(solution)/shard_map/all_to_all | solution.py:408
  91.5 0.4 shard_map.65
  91.9 13.3 %all_to_all.39.got_ref = bf16[16,40,128]{2,1,0:T(8,128)(2,1)S(1)} all-to-all(bf16[16,40,128]{2,1,0:T(8,128)(2,1)S(1)} %get-tuple-element.43), channel_id=1, replica_groups=mesh['z'=8,'x'=4,'y'=8,'core'=2] {'core','y'}, dimensions={0} | all-to-all | bytes 327680 | tf_op jit(solution)/shard_map/all_to_all | solution.py:408
  105.2 0.5 shard_map.66
  105.7 14.3 %all_to_all.40 = bf16[64,4,128]{2,1,0:T(4,128)(2,1)S(1)} all-to-all(bf16[64,4,128]{2,1,0:T(4,128)(2,1)S(1)} %bitcast.15), channel_id=1, replica_groups=mesh['z'=8,'x'=4,'y'=8,'core'=2] {'z','x','core'}, dimensions={0} | all-to-all | bytes 131072 | tf_op jit(solution)/shard_map/all_to_all | solution.py:408
  120.0 0.9 shard_map.67
Async XLA Ops:
  0.6 0.8 copy-start.1
  2.2 17.1 %all-to-all-start = ((bf16[8,128,128]{2,1,0:T(8,128)(2,1)}), bf16[8,128,128]{2,1,0:T(8,128)(2,1)S(1)}, u32[]{:S(2)}, u32[]{:S(2)}) async-start(bf16[8,128,128]{2,1,0:T(8,128)(2,1)} %get-tuple-element.30), calls=%async_computation | async-start | bytes 524288 | tf_op jit(solution)/shard_map/all_to_all | solution.py:408
  10.5 0.7 copy-start.2
  11.2 1.2 %copy-start = (bf16[1,1,32,128,128]{4,3,2,1,0:T(8,128)(2,1)S(1)}, bf16[1,1,32,128,128]{4,3,2,1,0:T(8,128)(2,1)}, u32[]{:S(2)}) copy-start(bf16[1,1,32,128,128]{4,3,2,1,0:T(8,128)(2,1)} %param.4) | copy-start | bytes 3145732

commit v10 on v9

--- a/solution.py
+++ b/solution.py
@@ -318,17 +318,17 @@
     placed = jnp.dot(match.astype(F32).astype(BF16), values, preferred_element_type=F32)
     for to in range(2):
         mine = [jnp.where(core == to, placed[:, 128 * i : 128 * i + 128], 0.0) for i in range(3)]
-        wide[pl.ds(4 * to, owners, stride=8), :] = mine[0]
-        wide[pl.ds(4 * to + 1, owners, stride=8), :] = mine[1]
-        wide[pl.ds(4 * to + 2, owners, stride=8), :] = mine[2] + block[3:4, :]
-        wide[pl.ds(4 * to + 3, owners, stride=8), :] = jnp.broadcast_to(block[7:8, :], (owners, 128))
+        wide[pl.ds(4 * owners * to + 0, owners, stride=4), :] = mine[0]
+        wide[pl.ds(4 * owners * to + 1, owners, stride=4), :] = mine[1]
+        wide[pl.ds(4 * owners * to + 2, owners, stride=4), :] = mine[2] + block[3:4, :]
+        wide[pl.ds(4 * owners * to + 3, owners, stride=4), :] = jnp.broadcast_to(block[7:8, :], (owners, 128))
     sent_ref[...] = wide[...].astype(BF16)
 
 
 def finish(got_ref, w1_ref, solution_ref, phi_ref, wide):
     wide[...] = got_ref[...].astype(F32)
     peers = got_ref.shape[0] // 8
-    parts = [wide[pl.ds(i, peers, stride=8), :] + wide[pl.ds(4 + i, peers, stride=8), :] for i in range(4)]
+    parts = [wide[pl.ds(i, peers, stride=4), :] + wide[pl.ds(4 * peers + i, peers, stride=4), :] for i in range(4)]
     total = jnp.concatenate([jnp.sum(parts[i], axis=0, keepdims=True) for i in (2, 3)], axis=0)
     half = w1_ref.shape[0]
     labels = pltpu.roll(jnp.broadcast_to(total[0:1, :], (half, 128)), 64, 1)
@@ -479,7 +479,7 @@
         [VMEM] * 2,
         [struct((2 * span, 128), F32), struct((1, 2), F32)],
         [pltpu.VMEM((n_row * 8, 128), F32)],
-        exchange(sent.reshape(n_row * 2, 4, 128), ROW + ("core",)).reshape(n_row * 8, 128), w1,
+        exchange(sent.reshape(n_row * 2, 4, 128), ("core",) + ROW).reshape(n_row * 8, 128), w1,
     )
     result = result.reshape(span, 2, 128).transpose(1, 0, 2).reshape(2, span * 128)
     return (result, phi_bar.reshape(2))

time: 121 us -> 121 us (level)
  no operation moved by 1% of the time
where the time goes in v10:
time: 121 us
  blocking collectives  97.4 us (80%)
  starting transfers between devices  7.65 us (6%)
  Pallas kernels  6.7 us (6%)
  waiting for transfers between devices  4.75 us (4%)
  local copies, waits for them, and re-layouts  2.73 us (2%)
  between operations  1.34 us (1%)
    all_to_all x6, blocking collectives, exchange(): return lax.all_to_all(sent, axis, split_axis=0, concat_axis=0, tiled=True)  86.9 us
    all_gather x2, blocking collectives, exchange_col(): return lax.all_gather(exchange(sent, 'y'), 'core', axis=0, tiled=True)  10.5 us
    all_to_all x1, starting transfers between devices, exchange(): return lax.all_to_all(sent, axis, split_axis=0, concat_axis=0, tiled=True)  7.65 us
    pallas_call x9, Pallas kernels, call(): pl.pallas_call(body, out_shape=outs, in_specs=specs, out_specs=[VMEM] * l...  6.7 us
    all_to_all x1, waiting for transfers between devices, exchange(): return lax.all_to_all(sent, axis, split_axis=0, concat_axis=0, tiled=True)  4.75 us
    unnamed x6, local copies, waits for them, and re-layouts  2.73 us
  transfers between devices with their start and end apart: 1, of which 1 were waited for; matrix products, arithmetic and copies ran while one was open for 0% of the time, Pallas kernels for 2%

profile of v10, /device:TPU:1, one launch (start us, length us, event | category | flops | bytes accessed | tf_op | source)
XLA Modules:
  0.0 120.6 jit_solution(1348651475820073405)
XLA Ops:
  0.6 0.0 copy-start.1
  0.6 0.8 copy-done.1
  1.5 0.7 shard_map.60
  2.2 7.7 %all-to-all-start = ((bf16[8,128,128]{2,1,0:T(8,128)(2,1)}), bf16[8,128,128]{2,1,0:T(8,128)(2,1)S(1)}, u32[]{:S(2)}, u32[]{:S(2)}) async-start(bf16[8,128,128]{2,1,0:T(8,128)(2,1)} %get-tuple-element.30), calls=%async_computation | async-start | bytes 524288 | tf_op jit(solution)/shard_map/all_to_all | solution.py:408
  10.5 0.0 copy-start.2
  10.5 0.7 copy-done.2
  11.2 0.0 copy-start
  11.2 1.2 %copy-done = bf16[1,1,32,128,128]{4,3,2,1,0:T(8,128)(2,1)S(1)} copy-done((bf16[1,1,32,128,128]{4,3,2,1,0:T(8,128)(2,1)S(1)}, bf16[1,1,32,128,128]{4,3,2,1,0:T(8,128)(2,1)}, u32[]{:S(2)}) %copy-start) | copy-done | bytes 1048600
  12.4 2.1 %shard_map.59 = (f32[32,128]{1,0:T(8,128)S(1)}, f32[32,128]{1,0:T(8,128)S(1)}, bf16[8,128]{1,0:T(8,128)(2,1)S(1)}, bf16[8,128]{1,0:T(8,128)(2,1)S(1)}, bf16[32,1...) custom-call(s32[2,32]{1,0:T(2,128)S(1)} %bitcast.17, s32[1,1]{1,0:T(1,128)S(6)} %copy.8.counts_ref, ...), custom_call_target="tpu_custom_call" | custom-call | tf_op jit(solution)/shard_map/pallas_call | solution.py:398
  14.5 4.8 %all-to-all-done = bf16[8,128,128]{2,1,0:T(8,128)(2,1)S(1)} async-done(((bf16[8,128,128]{2,1,0:T(8,128)(2,1)}), bf16[8,128,128]{2,1,0:T(8,128)(2,1)S(1)}, u32[]{:S(2)}, u32[]{:S(2)}) %all-to-all-start) | async-done | bytes 262176 | tf_op jit(solution)/shard_map/all_to_all | solution.py:408
  19.3 5.4 %all_gather.6 = bf16[16,128,128]{2,1,0:T(8,128)(2,1)S(1)} all-gather(bf16[8,128,128]{2,1,0:T(8,128)(2,1)S(1)} %all-to-all-done), channel_id=1, replica_groups=mesh['z'=8,'x'=4,'y'=8,'core'=2] {'core'}, dimensions={0}, use_global_device_ids=true | all-gather | bytes 786432 | tf_op jit(solution)/shard_map/all_gather | solution.py:411
  24.7 0.8 shard_map.61
  25.5 30.1 %all_to_all.35.got_ref = bf16[32,72,128]{2,1,0:T(8,128)(2,1)S(1)} all-to-all(bf16[32,72,128]{2,1,0:T(8,128)(2,1)S(1)} %get-tuple-element.32), channel_id=1, replica_groups=mesh['z'=8,'x'=4,'y'=8,'core'=2] {'z','x'}, dimensions={0} | all-to-all | bytes 1179648 | tf_op jit(solution)/shard_map/all_to_all | solution.py:408
  55.6 0.6 shard_map.62
  56.2 10.6 %all_to_all.36 = bf16[8,72,128]{2,1,0:T(8,128)(2,1)S(1)} all-to-all(bf16[8,72,128]{2,1,0:T(8,128)(2,1)S(1)} %get-tuple-element.36), channel_id=1, replica_groups=mesh['z'=8,'x'=4,'y'=8,'core'=2] {'y'}, dimensions={0} | all-to-all | bytes 294912 | tf_op jit(solution)/shard_map/all_to_all | solution.py:408
  66.8 5.1 %all_gather.7.got_ref = bf16[16,72,128]{2,1,0:T(8,128)(2,1)S(1)} all-gather(bf16[8,72,128]{2,1,0:T(8,128)(2,1)S(1)} %all_to_all.36), channel_id=1, replica_groups=mesh['z'=8,'x'=4,'y'=8,'core'=2] {'core'}, dimensions={0}, use_global_device_ids=true | all-gather | bytes 442368 | tf_op jit(solution)/shard_map/all_gather | solution.py:411
  71.9 0.5 shard_map.63
  72.3 11.1 %all_to_all.37.got_ref = bf16[8,72,128]{2,1,0:T(8,128)(2,1)S(1)} all-to-all(bf16[8,72,128]{2,1,0:T(8,128)(2,1)S(1)} %get-tuple-element.37), channel_id=1, replica_groups=mesh['z'=8,'x'=4,'y'=8,'core'=2] {'z'}, dimensions={0} | all-to-all | bytes 294912 | tf_op jit(solution)/shard_map/all_to_all | solution.py:408
  83.5 0.2 shard_map.64
  83.7 7.8 %all_to_all.38.got_ref = bf16[4,64,128]{2,1,0:T(8,128)(2,1)S(1)} all-to-all(bf16[4,64,128]{2,1,0:T(8,128)(2,1)S(1)} %shard_map.64), channel_id=1, replica_groups=mesh['z'=8,'x'=4,'y'=8,'core'=2] {'x'}, dimensions={0} | all-to-all | bytes 131072 | tf_op jit(solution)/shard_map/all_to_all | solution.py:408
  91.5 0.4 shard_map.65
  91.9 13.3 %all_to_all.39.got_ref = bf16[16,40,128]{2,1,0:T(8,128)(2,1)S(1)} all-to-all(bf16[16,40,128]{2,1,0:T(8,128)(2,1)S(1)} %get-tuple-element.43), channel_id=1, replica_groups=mesh['z'=8,'x'=4,'y'=8,'core'=2] {'core','y'}, dimensions={0} | all-to-all | bytes 327680 | tf_op jit(solution)/shard_map/all_to_all | solution.py:408
  105.2 0.5 shard_map.66
  105.7 14.0 %all_to_all.40 = bf16[64,4,128]{2,1,0:T(4,128)(2,1)S(1)} all-to-all(bf16[64,4,128]{2,1,0:T(4,128)(2,1)S(1)} %bitcast.15), channel_id=1, replica_groups=mesh['z'=8,'x'=4,'y'=8,'core'=2] {'core','z','x'}, dimensions={0} | all-to-all | bytes 131072 | tf_op jit(solution)/shard_map/all_to_all | solution.py:408
  119.7 0.9 shard_map.67
Async XLA Ops:
  0.6 0.8 copy-start.1
  2.2 17.1 %all-to-all-start = ((bf16[8,128,128]{2,1,0:T(8,128)(2,1)}), bf16[8,128,128]{2,1,0:T(8,128)(2,1)S(1)}, u32[]{:S(2)}, u32[]{:S(2)}) async-start(bf16[8,128,128]{2,1,0:T(8,128)(2,1)} %get-tuple-element.30), calls=%async_computation | async-start | bytes 524288 | tf_op jit(solution)/shard_map/all_to_all | solution.py:408
  10.5 0.7 copy-start.2
  11.2 1.2 %copy-start = (bf16[1,1,32,128,128]{4,3,2,1,0:T(8,128)(2,1)S(1)}, bf16[1,1,32,128,128]{4,3,2,1,0:T(8,128)(2,1)}, u32[]{:S(2)}) copy-start(bf16[1,1,32,128,128]{4,3,2,1,0:T(8,128)(2,1)} %param.4) | copy-start | bytes 3145732

commit v11 on v10

--- a/solution.py
+++ b/solution.py
@@ -171,16 +171,23 @@
     send_all(sent_ref, split_rows(out).astype(BF16), lane_ref[...])
 
 
-def second_adjoint(slot_ref, lane_ref, got_ref, tile_ref, sent_ref, w_ref, piece_ref, map_ref, held, out):
+def second_adjoint(slot_ref, got_ref, tile_ref, sent_ref, w_ref, piece_ref, map_ref, held, out):
     read_keys(got_ref, map_ref)
     keys = with_range(slot_ref, col_index(), piece_ref.shape[0])
     keep(sum_by_key(got_ref, map_ref, keys), w_ref, piece_ref, held)
     products(held, tile_ref, out)
-    send_all(sent_ref, split_rows(out).astype(BF16), lane_ref[...])
+    send_all(sent_ref, split_rows(out).astype(BF16), None)
 
 
 def regroup(map_ref, got_ref, sent_ref, line_ref):
-    read_keys(got_ref, line_ref)
+    me = lax.axis_index("x")
+    quarter = iota((8, 128), 1) // 32
+    for g in range(line_ref.shape[0]):
+        keys = jnp.zeros((8, 128), F32)
+        for i in range(4):
+            row = jnp.broadcast_to(map_ref[4 * g + i : 4 * g + i + 1, :], (8, 128))
+            keys = jnp.where(quarter == i, pltpu.roll(row, (i - me + 4) % 4 * 32, 1), keys)
+        line_ref[g : g + 1, :] = keys[0:1, :]
     target = map_ref[pl.ds(lax.axis_index("z"), 1), :]
     column = jnp.transpose(jnp.broadcast_to(target, (128, 128)))
     total = sum_by_key(got_ref, line_ref, column).astype(BF16)
@@ -448,10 +455,10 @@
     )
     sent, own_w2, w2, u_map = call(
         second_adjoint,
-        [VMEM] * 4,
-        [struct((lax.axis_size("z"), rows + 8, 128), BF16), own, piece, struct((n_col // 4, 128), F32)],
+        [VMEM] * 3,
+        [struct((lax.axis_size("z"), rows, 128), BF16), own, piece, struct((n_col // 4, 128), F32)],
         [wide, wide],
-        slot_u, lane_v, exchange_col(sent), held,
+        slot_u, exchange_col(sent), held,
     )
     (sent,) = call(
         regroup,

time: 121 us -> 121 us (level)
  no operation moved by 1% of the time
where the time goes in v11:
time: 121 us; the launch traced here: 120 us
  blocking collectives  97.1 us (80%)
  starting transfers between devices  7.65 us (6%)
  Pallas kernels  6.72 us (6%)
  waiting for transfers between devices  4.75 us (4%)
  local copies, waits for them, and re-layouts  2.73 us (2%)
  between operations  1.34 us (1%)
    all_to_all x6, blocking collectives, exchange(): return lax.all_to_all(sent, axis, split_axis=0, concat_axis=0, tiled=True)  86.6 us
    all_gather x2, blocking collectives, exchange_col(): return lax.all_gather(exchange(sent, 'y'), 'core', axis=0, tiled=True)  10.5 us
    all_to_all x1, starting transfers between devices, exchange(): return lax.all_to_all(sent, axis, split_axis=0, concat_axis=0, tiled=True)  7.65 us
    pallas_call x9, Pallas kernels, call(): pl.pallas_call(body, out_shape=outs, in_specs=specs, out_specs=[VMEM] * l...  6.72 us
    all_to_all x1, waiting for transfers between devices, exchange(): return lax.all_to_all(sent, axis, split_axis=0, concat_axis=0, tiled=True)  4.75 us
    unnamed x6, local copies, waits for them, and re-layouts  2.73 us
  transfers between devices with their start and end apart: 1, of which 1 were waited for; matrix products, arithmetic and copies ran while one was open for 0% of the time, Pallas kernels for 2%

profile of v11, /device:TPU:1, one launch (start us, length us, event | category | flops | bytes accessed | tf_op | source)
XLA Modules:
  0.0 120.3 jit_solution(14256884274173774645)
XLA Ops:
  0.6 0.0 copy-start.1
  0.6 0.8 copy-done.1
  1.5 0.7 shard_map.60
  2.2 7.7 %all-to-all-start = ((bf16[8,128,128]{2,1,0:T(8,128)(2,1)}), bf16[8,128,128]{2,1,0:T(8,128)(2,1)S(1)}, u32[]{:S(2)}, u32[]{:S(2)}) async-start(bf16[8,128,128]{2,1,0:T(8,128)(2,1)} %get-tuple-element.30), calls=%async_computation | async-start | bytes 524288 | tf_op jit(solution)/shard_map/all_to_all | solution.py:415
  10.5 0.0 copy-start.2
  10.5 0.7 copy-done.2
  11.2 0.0 copy-start
  11.2 1.2 %copy-done = bf16[1,1,32,128,128]{4,3,2,1,0:T(8,128)(2,1)S(1)} copy-done((bf16[1,1,32,128,128]{4,3,2,1,0:T(8,128)(2,1)S(1)}, bf16[1,1,32,128,128]{4,3,2,1,0:T(8,128)(2,1)}, u32[]{:S(2)}) %copy-start) | copy-done | bytes 1048600
  12.4 2.1 %shard_map.59 = (f32[32,128]{1,0:T(8,128)S(1)}, f32[32,128]{1,0:T(8,128)S(1)}, bf16[8,128]{1,0:T(8,128)(2,1)S(1)}, bf16[8,128]{1,0:T(8,128)(2,1)S(1)}, bf16[32,1...) custom-call(s32[2,32]{1,0:T(2,128)S(1)} %bitcast.17, s32[1,1]{1,0:T(1,128)S(6)} %copy.8.counts_ref, ...), custom_call_target="tpu_custom_call" | custom-call | tf_op jit(solution)/shard_map/pallas_call | solution.py:405
  14.5 4.8 %all-to-all-done = bf16[8,128,128]{2,1,0:T(8,128)(2,1)S(1)} async-done(((bf16[8,128,128]{2,1,0:T(8,128)(2,1)}), bf16[8,128,128]{2,1,0:T(8,128)(2,1)S(1)}, u32[]{:S(2)}, u32[]{:S(2)}) %all-to-all-start) | async-done | bytes 262176 | tf_op jit(solution)/shard_map/all_to_all | solution.py:415
  19.3 5.4 %all_gather.6 = bf16[16,128,128]{2,1,0:T(8,128)(2,1)S(1)} all-gather(bf16[8,128,128]{2,1,0:T(8,128)(2,1)S(1)} %all-to-all-done), channel_id=1, replica_groups=mesh['z'=8,'x'=4,'y'=8,'core'=2] {'core'}, dimensions={0}, use_global_device_ids=true | all-gather | bytes 786432 | tf_op jit(solution)/shard_map/all_gather | solution.py:418
  24.7 0.8 shard_map.61
  25.5 30.1 %all_to_all.35.got_ref = bf16[32,72,128]{2,1,0:T(8,128)(2,1)S(1)} all-to-all(bf16[32,72,128]{2,1,0:T(8,128)(2,1)S(1)} %get-tuple-element.32), channel_id=1, replica_groups=mesh['z'=8,'x'=4,'y'=8,'core'=2] {'z','x'}, dimensions={0} | all-to-all | bytes 1179648 | tf_op jit(solution)/shard_map/all_to_all | solution.py:415
  55.6 0.6 shard_map.62
  56.2 10.6 %all_to_all.36 = bf16[8,72,128]{2,1,0:T(8,128)(2,1)S(1)} all-to-all(bf16[8,72,128]{2,1,0:T(8,128)(2,1)S(1)} %get-tuple-element.36), channel_id=1, replica_groups=mesh['z'=8,'x'=4,'y'=8,'core'=2] {'y'}, dimensions={0} | all-to-all | bytes 294912 | tf_op jit(solution)/shard_map/all_to_all | solution.py:415
  66.8 5.1 %all_gather.7.got_ref = bf16[16,72,128]{2,1,0:T(8,128)(2,1)S(1)} all-gather(bf16[8,72,128]{2,1,0:T(8,128)(2,1)S(1)} %all_to_all.36), channel_id=1, replica_groups=mesh['z'=8,'x'=4,'y'=8,'core'=2] {'core'}, dimensions={0}, use_global_device_ids=true | all-gather | bytes 442368 | tf_op jit(solution)/shard_map/all_gather | solution.py:418
  71.9 0.5 shard_map.63
  72.3 10.7 %all_to_all.37.got_ref = bf16[8,64,128]{2,1,0:T(8,128)(2,1)S(1)} all-to-all(bf16[8,64,128]{2,1,0:T(8,128)(2,1)S(1)} %get-tuple-element.37), channel_id=1, replica_groups=mesh['z'=8,'x'=4,'y'=8,'core'=2] {'z'}, dimensions={0} | all-to-all | bytes 262144 | tf_op jit(solution)/shard_map/all_to_all | solution.py:415
  83.1 0.3 shard_map.64
  83.3 7.8 %all_to_all.38.got_ref = bf16[4,64,128]{2,1,0:T(8,128)(2,1)S(1)} all-to-all(bf16[4,64,128]{2,1,0:T(8,128)(2,1)S(1)} %shard_map.64), channel_id=1, replica_groups=mesh['z'=8,'x'=4,'y'=8,'core'=2] {'x'}, dimensions={0} | all-to-all | bytes 131072 | tf_op jit(solution)/shard_map/all_to_all | solution.py:415
  91.2 0.4 shard_map.65
  91.6 13.3 %all_to_all.39.got_ref = bf16[16,40,128]{2,1,0:T(8,128)(2,1)S(1)} all-to-all(bf16[16,40,128]{2,1,0:T(8,128)(2,1)S(1)} %get-tuple-element.43), channel_id=1, replica_groups=mesh['z'=8,'x'=4,'y'=8,'core'=2] {'core','y'}, dimensions={0} | all-to-all | bytes 327680 | tf_op jit(solution)/shard_map/all_to_all | solution.py:415
  104.9 0.5 shard_map.66
  105.4 14.0 %all_to_all.40 = bf16[64,4,128]{2,1,0:T(4,128)(2,1)S(1)} all-to-all(bf16[64,4,128]{2,1,0:T(4,128)(2,1)S(1)} %bitcast.15), channel_id=1, replica_groups=mesh['z'=8,'x'=4,'y'=8,'core'=2] {'core','z','x'}, dimensions={0} | all-to-all | bytes 131072 | tf_op jit(solution)/shard_map/all_to_all | solution.py:415
  119.4 0.9 shard_map.67
Async XLA Ops:
  0.6 0.8 copy-start.1
  2.2 17.1 %all-to-all-start = ((bf16[8,128,128]{2,1,0:T(8,128)(2,1)}), bf16[8,128,128]{2,1,0:T(8,128)(2,1)S(1)}, u32[]{:S(2)}, u32[]{:S(2)}) async-start(bf16[8,128,128]{2,1,0:T(8,128)(2,1)} %get-tuple-element.30), calls=%async_computation | async-start | bytes 524288 | tf_op jit(solution)/shard_map/all_to_all | solution.py:415
  10.5 0.7 copy-start.2
  11.2 1.2 %copy-start = (bf16[1,1,32,128,128]{4,3,2,1,0:T(8,128)(2,1)S(1)}, bf16[1,1,32,128,128]{4,3,2,1,0:T(8,128)(2,1)}, u32[]{:S(2)}) copy-start(bf16[1,1,32,128,128]{4,3,2,1,0:T(8,128)(2,1)} %param.4) | copy-start | bytes 3145732

commit v12 on v11

--- a/solution.py
+++ b/solution.py
@@ -131,15 +131,14 @@
         seen = seen + odd
     for i in range(slots):
         k = order_ref[i]
-        held_ref[i] = tile_ref[k]
         turned_ref[i] = jnp.transpose(tile_ref[k])
         block = places_ref[0, k]
         owner = block // span
         used = k < count
+        held_ref[i] = jnp.where(used, tile_ref[k], jnp.zeros_like(tile_ref[k]))
         sorted_ref[0, i] = jnp.where(used, block, -1)
         sorted_ref[1, i] = jnp.where(used, places_ref[1, k], -1)
-        fetch_ref[0, i] = ((owner % cores) * chips + owner // cores) * span + block % span
-        fetch_ref[1, i] = used.astype(jnp.int32)
+        fetch_ref[i] = ((owner % cores) * chips + owner // cores) * span + block % span
     slot_u_ref[...] = slot_keys(sorted_ref, 0)
     slot_v_ref[...] = slot_keys(sorted_ref, 1)
     lane_u_ref[...] = lane_keys(sorted_ref, 0)
@@ -147,8 +146,8 @@
 
 
 def first_adjoint(fetch_ref, lane_ref, u_ref, tile_ref, sent_ref, own_u_ref, held, out):
-    for k in range(fetch_ref.shape[1]):
-        held[2 * k : 2 * k + 2, :] = u_ref[fetch_ref[0, k]].astype(F32) * fetch_ref[1, k].astype(F32)
+    for k in range(fetch_ref.shape[0]):
+        held[2 * k : 2 * k + 2, :] = u_ref[fetch_ref[k]].astype(F32)
     own_u_ref[...] = split_rows(held).astype(BF16)
     products(held, tile_ref, out)
     send_all(sent_ref, split_rows(out).astype(BF16), lane_ref[...])
@@ -433,7 +432,7 @@
     slot_v, slot_u, lane_v, lane_u, held, turned, fetch = call(
         functools.partial(tables, spans=(span, chips, lax.axis_size("core"))),
         [SMEM, SMEM, VMEM],
-        [slot_table] * 2 + [lane_table] * 2 + [struct(tile.shape, BF16)] * 2 + [struct((2, slots), jnp.int32)],
+        [slot_table] * 2 + [lane_table] * 2 + [struct(tile.shape, BF16)] * 2 + [struct((slots,), jnp.int32)],
         [pltpu.SMEM((slots,), jnp.int32), pltpu.SMEM((2, slots), jnp.int32)],
         places, counts, tile,
         out_specs=[VMEM] * 6 + [SMEM],

time: 121 us -> 121 us (level)
  no operation moved by 1% of the time
where the time goes in v12:
time: 121 us; the launch traced here: 120 us
  blocking collectives  97.1 us (80%)
  starting transfers between devices  7.65 us (6%)
  Pallas kernels  6.78 us (6%)
  waiting for transfers between devices  4.69 us (4%)
  local copies, waits for them, and re-layouts  2.73 us (2%)
  between operations  1.34 us (1%)
    all_to_all x6, blocking collectives, exchange(): return lax.all_to_all(sent, axis, split_axis=0, concat_axis=0, tiled=True)  86.6 us
    all_gather x2, blocking collectives, exchange_col(): return lax.all_gather(exchange(sent, 'y'), 'core', axis=0, tiled=True)  10.5 us
    all_to_all x1, starting transfers between devices, exchange(): return lax.all_to_all(sent, axis, split_axis=0, concat_axis=0, tiled=True)  7.65 us
    pallas_call x9, Pallas kernels, call(): pl.pallas_call(body, out_shape=outs, in_specs=specs, out_specs=[VMEM] * l...  6.78 us
    all_to_all x1, waiting for transfers between devices, exchange(): return lax.all_to_all(sent, axis, split_axis=0, concat_axis=0, tiled=True)  4.69 us
    unnamed x6, local copies, waits for them, and re-layouts  2.73 us
  transfers between devices with their start and end apart: 1, of which 1 were waited for; matrix products, arithmetic and copies ran while one was open for 0% of the time, Pallas kernels for 2%

profile of v12, /device:TPU:1, one launch (start us, length us, event | category | flops | bytes accessed | tf_op | source)
XLA Modules:
  0.0 120.2 jit_solution(15568198475350280819)
XLA Ops:
  0.6 0.0 copy-start.1
  0.6 0.8 copy-done.1
  1.5 0.7 shard_map.60
  2.2 7.7 %all-to-all-start = ((bf16[8,128,128]{2,1,0:T(8,128)(2,1)}), bf16[8,128,128]{2,1,0:T(8,128)(2,1)S(1)}, u32[]{:S(2)}, u32[]{:S(2)}) async-start(bf16[8,128,128]{2,1,0:T(8,128)(2,1)} %get-tuple-element.30), calls=%async_computation | async-start | bytes 524288 | tf_op jit(solution)/shard_map/all_to_all | solution.py:414
  10.5 0.0 copy-start.2
  10.5 0.7 copy-done.2
  11.2 0.0 copy-start
  11.2 1.2 %copy-done = bf16[1,1,32,128,128]{4,3,2,1,0:T(8,128)(2,1)S(1)} copy-done((bf16[1,1,32,128,128]{4,3,2,1,0:T(8,128)(2,1)S(1)}, bf16[1,1,32,128,128]{4,3,2,1,0:T(8,128)(2,1)}, u32[]{:S(2)}) %copy-start) | copy-done | bytes 1048600
  12.4 2.2 %shard_map.59 = (f32[32,128]{1,0:T(8,128)S(1)}, f32[32,128]{1,0:T(8,128)S(1)}, bf16[8,128]{1,0:T(8,128)(2,1)S(1)}, bf16[8,128]{1,0:T(8,128)(2,1)S(1)}, bf16[32,1...) custom-call(s32[2,32]{1,0:T(2,128)S(1)} %bitcast.17, s32[1,1]{1,0:T(1,128)S(6)} %copy.8.counts_ref, ...), custom_call_target="tpu_custom_call" | custom-call | tf_op jit(solution)/shard_map/pallas_call | solution.py:404
  14.6 4.7 %all-to-all-done = bf16[8,128,128]{2,1,0:T(8,128)(2,1)S(1)} async-done(((bf16[8,128,128]{2,1,0:T(8,128)(2,1)}), bf16[8,128,128]{2,1,0:T(8,128)(2,1)S(1)}, u32[]{:S(2)}, u32[]{:S(2)}) %all-to-all-start) | async-done | bytes 262176 | tf_op jit(solution)/shard_map/all_to_all | solution.py:414
  19.3 5.4 %all_gather.6 = bf16[16,128,128]{2,1,0:T(8,128)(2,1)S(1)} all-gather(bf16[8,128,128]{2,1,0:T(8,128)(2,1)S(1)} %all-to-all-done), channel_id=1, replica_groups=mesh['z'=8,'x'=4,'y'=8,'core'=2] {'core'}, dimensions={0}, use_global_device_ids=true | all-gather | bytes 786432 | tf_op jit(solution)/shard_map/all_gather | solution.py:417
  24.7 0.8 shard_map.61
  25.5 30.1 %all_to_all.35.got_ref = bf16[32,72,128]{2,1,0:T(8,128)(2,1)S(1)} all-to-all(bf16[32,72,128]{2,1,0:T(8,128)(2,1)S(1)} %get-tuple-element.32), channel_id=1, replica_groups=mesh['z'=8,'x'=4,'y'=8,'core'=2] {'z','x'}, dimensions={0} | all-to-all | bytes 1179648 | tf_op jit(solution)/shard_map/all_to_all | solution.py:414
  55.6 0.6 shard_map.62
  56.2 10.6 %all_to_all.36 = bf16[8,72,128]{2,1,0:T(8,128)(2,1)S(1)} all-to-all(bf16[8,72,128]{2,1,0:T(8,128)(2,1)S(1)} %get-tuple-element.36), channel_id=1, replica_groups=mesh['z'=8,'x'=4,'y'=8,'core'=2] {'y'}, dimensions={0} | all-to-all | bytes 294912 | tf_op jit(solution)/shard_map/all_to_all | solution.py:414
  66.8 5.0 %all_gather.7.got_ref = bf16[16,72,128]{2,1,0:T(8,128)(2,1)S(1)} all-gather(bf16[8,72,128]{2,1,0:T(8,128)(2,1)S(1)} %all_to_all.36), channel_id=1, replica_groups=mesh['z'=8,'x'=4,'y'=8,'core'=2] {'core'}, dimensions={0}, use_global_device_ids=true | all-gather | bytes 442368 | tf_op jit(solution)/shard_map/all_gather | solution.py:417
  71.8 0.5 shard_map.63
  72.3 10.7 %all_to_all.37.got_ref = bf16[8,64,128]{2,1,0:T(8,128)(2,1)S(1)} all-to-all(bf16[8,64,128]{2,1,0:T(8,128)(2,1)S(1)} %get-tuple-element.37), channel_id=1, replica_groups=mesh['z'=8,'x'=4,'y'=8,'core'=2] {'z'}, dimensions={0} | all-to-all | bytes 262144 | tf_op jit(solution)/shard_map/all_to_all | solution.py:414
  83.0 0.3 shard_map.64
  83.3 7.8 %all_to_all.38.got_ref = bf16[4,64,128]{2,1,0:T(8,128)(2,1)S(1)} all-to-all(bf16[4,64,128]{2,1,0:T(8,128)(2,1)S(1)} %shard_map.64), channel_id=1, replica_groups=mesh['z'=8,'x'=4,'y'=8,'core'=2] {'x'}, dimensions={0} | all-to-all | bytes 131072 | tf_op jit(solution)/shard_map/all_to_all | solution.py:414
  91.1 0.4 shard_map.65
  91.6 13.3 %all_to_all.39.got_ref = bf16[16,40,128]{2,1,0:T(8,128)(2,1)S(1)} all-to-all(bf16[16,40,128]{2,1,0:T(8,128)(2,1)S(1)} %get-tuple-element.43), channel_id=1, replica_groups=mesh['z'=8,'x'=4,'y'=8,'core'=2] {'core','y'}, dimensions={0} | all-to-all | bytes 327680 | tf_op jit(solution)/shard_map/all_to_all | solution.py:414
  104.9 0.5 shard_map.66
  105.4 14.0 %all_to_all.40 = bf16[64,4,128]{2,1,0:T(4,128)(2,1)S(1)} all-to-all(bf16[64,4,128]{2,1,0:T(4,128)(2,1)S(1)} %bitcast.15), channel_id=1, replica_groups=mesh['z'=8,'x'=4,'y'=8,'core'=2] {'core','z','x'}, dimensions={0} | all-to-all | bytes 131072 | tf_op jit(solution)/shard_map/all_to_all | solution.py:414
  119.4 0.9 shard_map.67
Async XLA Ops:
  0.6 0.8 copy-start.1
  2.2 17.1 %all-to-all-start = ((bf16[8,128,128]{2,1,0:T(8,128)(2,1)}), bf16[8,128,128]{2,1,0:T(8,128)(2,1)S(1)}, u32[]{:S(2)}, u32[]{:S(2)}) async-start(bf16[8,128,128]{2,1,0:T(8,128)(2,1)} %get-tuple-element.30), calls=%async_computation | async-start | bytes 524288 | tf_op jit(solution)/shard_map/all_to_all | solution.py:414
  10.5 0.7 copy-start.2
  11.2 1.2 %copy-start = (bf16[1,1,32,128,128]{4,3,2,1,0:T(8,128)(2,1)S(1)}, bf16[1,1,32,128,128]{4,3,2,1,0:T(8,128)(2,1)}, u32[]{:S(2)}) copy-start(bf16[1,1,32,128,128]{4,3,2,1,0:T(8,128)(2,1)} %param.4) | copy-start | bytes 3145732
